TPU v7x, 256 devices: a whole 4x4x8 slice. The times are simulated.
256 devices in a mesh: seq: 32 (over z, y_lo, core), mp: 8 (over y_hi, x).
Axes of the slice: x: 4, y: 4 (y_hi: 2, y_lo: 2; y = y_hi * 2 + y_lo), z: 8, core: 2. Of those that a mesh axis runs over, the one named last changes fastest.
Arguments:
- tokens: bfloat16 [32768, 4096], P('seq', 'mp'), may hold values from -6 to 6
- segment_ids: int32 [32768], P('seq'), may hold values from 0 to 3, never falling along the last dimension, each value on 1 to 16384 neighbouring positions
- w_x: bfloat16 [4096, 4096], P(None, 'mp'), may hold values from -0.09375 to 0.09375
- w_z: bfloat16 [4096, 4096], P(None, 'mp'), may hold values from -0.09375 to 0.09375
- w_bc: bfloat16 [4096, 256], replicated, may hold values from -0.09375 to 0.09375
- w_dt: bfloat16 [4096, 32], P(None, 'mp'), may hold values from -0.09375 to 0.09375
- dt_bias: float32 [32], P('mp'), may hold values from -1 to 1
- rates: float32 [32], P('mp'), may hold values from 1.5258789e-05 to 0.05
- conv_x: float32 [3, 4096], P(None, 'mp'), may hold values from -3 to 3
- conv_bc: float32 [3, 256], replicated, may hold values from -3 to 3
- norm_gain: float32 [4096], P('mp'), may hold values from 0.5 to 1.5
Outputs:
- encoded: bfloat16 [32768, 4096], P('seq', 'mp')
Inputs may be any that keep to these rules, and one draw needn't show every extreme that they name: `segment_ids`: document numbers never fall along the slab and start at 0; each document holds 1 to 16384 tokens, and one holds exactly 16384.
All inputs are finite; a program needn't handle non-finite values.
Results may differ from a plain program's by a relative error of at most 0.009.
Values may be sent and summed in bfloat16 or wider, within the bound.
No kernel may reach another device: no remote copies, remote signals or barrier semaphores. Data moves between devices by JAX's collectives and lax.ppermute only.
A program may use at most 128 MiB of HBM per device.

v0:
```python
import jax
import jax.numpy as jnp
from jax import lax
from jax.sharding import PartitionSpec as P


def padded(cells, sides, width):
    for axis, dim in sides:
        count = lax.axis_size(axis)
        ends = count - 1
        head = lax.slice_in_dim(cells, 0, width, axis=dim)
        tail = lax.slice_in_dim(cells, cells.shape[dim] - width, cells.shape[dim], axis=dim)
        cells = jnp.concatenate(
            [
                lax.ppermute(tail, axis, [(i, (i + 1) % count) for i in range(ends)]),
                cells,
                lax.ppermute(head, axis, [((i + 1) % count, i) for i in range(ends)]),
            ],
            axis=dim,
        )
    return cells


def entering_2(part, axis, combine, identity, reverse):
    count = lax.axis_size(axis)
    place = lax.axis_index(axis)
    ahead = count - 1 - place if reverse else place
    gathered = jax.tree.map(lambda a: lax.all_gather(a, axis), part)
    state = jax.tree.map(lambda a, e: jnp.zeros_like(a) + jnp.asarray(e, a.dtype), part, identity)

    def one(step, state):
        source = count - 1 - step if reverse else step
        return combine(
            state, jax.tree.map(lambda a: lax.dynamic_index_in_dim(a, source, 0, False), gathered)
        )

    return lax.fori_loop(0, ahead, one, state)


def add_rows(piece, weight):
    return jnp.dot(piece, weight, preferred_element_type=jnp.float32)


def combine(earlier, later):
    return (earlier[0] * later[0], later[0][:, None, None] * earlier[1] + later[1])


def local_sweep(inputs, b_vecs, c_vecs, steps, seg_vals, seg_before, rates, strict):
    tok_rows = inputs.shape[0]
    heads_dev = steps.shape[1]
    head_dim = inputs.shape[1] // heads_dev
    state_dim = b_vecs.shape[1]
    block_len = min(tok_rows // 2, 256)
    block_count = tok_rows // block_len
    x_blocks = inputs.reshape(block_count, block_len, heads_dev, head_dim)
    b_blocks = b_vecs.reshape(block_count, block_len, state_dim)
    c_blocks = c_vecs.reshape(block_count, block_len, state_dim)
    dt_blocks = steps.reshape(block_count, block_len, heads_dev)
    seg_blocks = seg_vals.reshape(block_count, block_len)
    cumul = jnp.cumsum(-dt_blocks * rates, axis=1)
    seg_prev = jnp.concatenate([seg_before[None], seg_blocks[:-1, -1]])
    positions = jnp.arange(block_len)
    if strict:
        lower_tri = positions[None, :] < positions[:, None]
    else:
        lower_tri = positions[None, :] <= positions[:, None]
    keep_mask = (lower_tri[None] & (seg_blocks[:, :, None] == seg_blocks[:, None, :]))[..., None]
    gap_sum = cumul[:, :, None, :] - cumul[:, None, :, :]
    decay = jnp.where(keep_mask, jnp.exp(jnp.where(keep_mask, gap_sum, 0.0)), 0.0)
    scores = jnp.einsum("bin,bjn->bij", c_blocks, b_blocks, preferred_element_type=jnp.float32)
    weights = (scores[..., None] * decay * dt_blocks[:, None, :, :]).astype(jnp.bfloat16)
    inside = jnp.einsum("bijh,bjhp->bihp", weights, x_blocks, preferred_element_type=jnp.float32)
    final_cum = cumul[:, -1, :]
    tail_decay = jnp.where(
        (seg_blocks == seg_blocks[:, -1:])[..., None], jnp.exp(final_cum[:, None, :] - cumul), 0.0
    )
    scaled = (x_blocks * (tail_decay * dt_blocks)[..., None]).astype(jnp.bfloat16)
    fresh = jnp.einsum("bjhp,bjn->bhpn", scaled, b_blocks, preferred_element_type=jnp.float32)
    block_decay = jnp.exp(final_cum) * (seg_blocks[:, -1] == seg_prev)[:, None].astype(jnp.float32)
    opening = jnp.where((seg_blocks == seg_prev[:, None])[..., None], jnp.exp(cumul), 0.0)
    return (inside, block_decay, fresh, opening, c_blocks)


def summarize(parts):
    block_decay = parts[1]
    fresh = parts[2]
    total_decay = jnp.ones(block_decay.shape[1:], jnp.float32)
    state_now = jnp.zeros(fresh.shape[1:], jnp.float32)
    for which in range(fresh.shape[0]):
        total_decay = total_decay * block_decay[which]
        state_now = block_decay[which][:, None, None] * state_now + fresh[which]
    return (total_decay, state_now)


def read_states(parts, entering):
    inside, block_decay, fresh, opening, c_blocks = parts
    state_now = entering
    outputs = []
    for which in range(fresh.shape[0]):
        carried = jnp.einsum(
            "in,hpn->ihp",
            c_blocks[which],
            state_now.astype(jnp.bfloat16),
            preferred_element_type=jnp.float32,
        )
        outputs.append(carried * opening[which][..., None])
        state_now = block_decay[which][:, None, None] * state_now + fresh[which]
    return inside + jnp.stack(outputs)


def shards(tokens, segment_ids, w_x, w_z, w_bc, w_dt, dt_bias, rates, conv_x, conv_bc, norm_gain):
    tok_rows = tokens.shape[0]
    inner_dev = w_x.shape[1]
    heads_dev = w_dt.shape[1]
    head_dim = inner_dev // heads_dev
    state_dim = w_bc.shape[1] // 2
    mp_count = lax.axis_size("mp")
    piece = lax.all_gather(tokens, "mp", axis=1, tiled=True)
    sum_x = add_rows(piece, w_x)
    sum_z = add_rows(piece, w_z)
    sum_dt = add_rows(piece, w_dt)
    sum_bc = add_rows(piece, w_bc)
    proj_x = sum_x.astype(jnp.bfloat16)
    gate = sum_z.astype(jnp.bfloat16)
    proj_bc = sum_bc.astype(jnp.bfloat16)
    steps = jax.nn.softplus(sum_dt + dt_bias)
    values = jnp.concatenate([proj_x, proj_bc], axis=1)
    edge_rows = jnp.concatenate([values[:1], values[-1:]], axis=0).astype(jnp.float32)
    seg_vals = segment_ids.astype(jnp.float32)
    seg_edges = jnp.concatenate([seg_vals[:1], seg_vals[-1:]])[:, None]
    beside, beside_seg = (padded(edge_rows, (("seq", 0),), 1), padded(seg_edges, (("seq", 0),), 1))
    left_seg = beside_seg[0, 0]
    right_seg = beside_seg[3, 0]
    extended = jnp.concatenate([beside[:1], values.astype(jnp.float32), beside[3:]], axis=0)
    seg_extended = jnp.concatenate([beside_seg[:1, 0], seg_vals, beside_seg[3:, 0]])
    kernel = jnp.concatenate([conv_x, conv_bc], axis=1)
    before = extended[:-2] * (seg_extended[:-2] == seg_vals)[:, None].astype(jnp.float32)
    after = extended[2:] * (seg_extended[2:] == seg_vals)[:, None].astype(jnp.float32)
    filtered = jax.nn.silu(kernel[0] * before + kernel[1] * extended[1:-1] + kernel[2] * after)
    inputs = filtered[:, :inner_dev].astype(jnp.bfloat16)
    vectors = filtered[:, inner_dev:].astype(jnp.bfloat16)
    b_vecs = vectors[:, :state_dim]
    c_vecs = vectors[:, state_dim:]
    forward_parts = local_sweep(inputs, b_vecs, c_vecs, steps, seg_vals, left_seg, rates, False)
    backward_parts = local_sweep(
        inputs[::-1],
        b_vecs[::-1],
        c_vecs[::-1],
        steps[::-1],
        seg_vals[::-1],
        right_seg,
        rates,
        True,
    )
    decay_fwd, state_fwd = summarize(forward_parts)
    decay_bwd, state_bwd = summarize(backward_parts)
    identity = (
        jnp.ones((heads_dev,), jnp.float32),
        jnp.zeros((heads_dev, head_dim, state_dim), jnp.float32),
    )
    _, enter_fwd = entering_2((decay_fwd, state_fwd), "seq", combine, identity, False)
    _, enter_bwd = entering_2((decay_bwd, state_bwd), "seq", combine, identity, True)
    out_fwd = read_states(forward_parts, enter_fwd).reshape(tok_rows, inner_dev)
    out_bwd = read_states(backward_parts, enter_bwd).reshape(tok_rows, inner_dev)[::-1]
    mixed_y = out_fwd + out_bwd
    gated = mixed_y * jax.nn.silu(gate.astype(jnp.float32))
    squares = lax.psum(jnp.sum(gated * gated, axis=1), "mp")
    scale = lax.rsqrt(squares / (inner_dev * mp_count) + 1e-05)
    return (gated * scale[:, None] * norm_gain).astype(jnp.bfloat16)


def solution(mesh):
    placed = (
        P("seq", "mp"),
        P("seq"),
        P(None, "mp"),
        P(None, "mp"),
        P(),
        P(None, "mp"),
        P("mp"),
        P("mp"),
        P(None, "mp"),
        P(),
        P("mp"),
    )
    return jax.shard_map(
        shards, mesh=mesh, in_specs=placed, out_specs=P("seq", "mp"), check_vma=False
    )
```

profile of v0, /device:TPU:232, one launch (start us, length us, event | category | flops | bytes accessed | tf_op | source)
XLA Modules:
  0.0 438.1 jit_solution(16433270011740385845)
XLA Ops:
  8.6 1.9 collective-permute-start.3
  10.6 3.0 collective-permute-start.1
  17.0 1.4 fusion.77
  18.4 116.6 %all-gather.6.cloned.1.call-done = bf16[1024,4096]{1,0:T(8,128)(2,1)} async-done(((bf16[1024,512]{1,0:T(8,128)(2,1)}), bf16[1024,4096]{1,0:T(8,128)(2,1)}) %all-gather.6.cloned.1.call-update) | async-done | bytes 8388624 | tf_op jit(solution)/shard_map/all_gather | solution.py:118
  135.0 5.7 %compare_select_fusion = f32[1024,4]{0,1:T(4,128)S(1)} fusion(bf16[1024,4096]{1,0:T(8,128)(2,1)} %all-gather.6.cloned.1.call-done, bf16[4096,4]{0,1:T(4,128)(2,1)} %param.20, f32[4]{0:T(128)} %param.21), kind=kOutput, calls=%fused_computation.115 | convolution fusion | flops 33583104 | bytes 8437776 | tf_op jit(solution)/shard_map/dot_general | solution.py:41
  141.5 4.8 %reduce-window.16 = f32[4,4,2,128]{3,2,1,0:T(2,128)S(1)} reduce-window(f32[4,4,2,128]{3,2,1,0:T(2,128)S(1)} %reshape.243, f32[]{:T(128)} %constant.70.clone.1), window={size=1x1x1x128 pad=0_0x0_0x0_0x127_0}, to_apply=%region_4.5 | reduce-window | flops 520192 | bytes 32772 | tf_op jit(solution)/shard_map/reduce-window.2
  147.6 9.2 %convolution_convert_fusion.1 = bf16[1024,512]{0,1:T(8,128)(2,1)S(1)} fusion(bf16[1024,4096]{1,0:T(8,128)(2,1)} %all-gather.6.cloned.1.call-done, bf16[4096,512]{1,0:T(8,128)(2,1)} %param.17), kind=kOutput, calls=%fused_computation.48 | convolution fusion | flops 4295491584 | bytes 13631488 | tf_op jit(solution)/shard_map/dot_general | solution.py:41
  156.8 2.4 convolution_convert_fusion.2
  160.7 1.9 collective-permute-start
  162.8 3.8 collective-permute-start.2
  166.8 1.4 fusion.24
  168.2 1.6 collective-permute-done
  169.8 4.1 collective-permute-done.2
  173.9 3.0 multiply_convert_fusion.2
  180.6 3.3 rev.18
  184.8 1.6 fusion.34
  189.1 4.8 %reduce-window.14 = f32[4,4,2,128]{3,2,1,0:T(2,128)S(1)} reduce-window(f32[4,4,2,128]{3,2,1,0:T(2,128)S(1)} %reshape.236, f32[]{:T(128)} %constant.70.clone.1), window={size=1x1x1x128 pad=0_0x0_0x0_0x127_0}, to_apply=%region_0.1 | reduce-window | flops 520192 | bytes 32772 | tf_op jit(solution)/shard_map/reduce-window
  196.2 1.6 reshape.232
  197.8 1.7 fusion.33
  202.4 30.6 %all-gather.1 = f32[32,1,4]{2,1,0:T(1,128)} all-gather(f32[1,1,4]{2,1,0:T(1,128)S(1)} %get-tuple-element.268), channel_id=1, replica_groups=mesh['seq'=32,'mp'=8] {'seq'}, dimensions={0}, use_global_device_ids=true | all-gather | bytes 528 | tf_op jit(solution)/shard_map/all_gather | solution.py:28
  233.0 34.5 %all-gather = f32[32,1,4]{2,1,0:T(1,128)} all-gather(f32[1,1,4]{2,1,0:T(1,128)S(1)} %get-tuple-element.273), channel_id=1, replica_groups=mesh['seq'=32,'mp'=8] {'seq'}, dimensions={0}, use_global_device_ids=true | all-gather | bytes 528 | tf_op jit(solution)/shard_map/all_gather | solution.py:28
  276.2 1.8 while.27
  282.4 1.7 maximum_add_fusion.1
  285.4 1.8 copy.464
  287.2 17.6 %rev.23 = f32[1024,512]{0,1:T(8,128)} reverse(f32[1024,512]{0,1:T(8,128)} %bitcast.195), dimensions={0} | reverse | bytes 4194304 | tf_op jit(solution)/shard_map/rev | solution.py:164
  304.8 28.1 %all-gather.8.cloned.1.call-done = f32[32,4,128,128]{3,2,1,0:T(8,128)} async-done(((f32[1,4,128,128]{3,2,1,0:T(8,128)}), f32[32,4,128,128]{3,2,1,0:T(8,128)}) %all-gather.8.cloned.1.call-update) | async-done | bytes 8388624 | tf_op jit(solution)/shard_map/all_gather | solution.py:28
  333.0 53.3 %while.26 = (s32[]{:T(128)}, f32[4,128,128]{2,1,0:T(8,128)S(1)}, s32[]{:T(128)}, f32[32,4]{1,0:T(8,128)}, f32[32,4,128,128]{3,2,1,0:T(8,128)}, /*index=5*/s32[]{:T(128)}, s32[]{:T(128)}, s32[]{:T(128)}) while((s32[]{:T(128)}, f32[4,128,128]{2,1,0:T(8,128)S(1)}, s32[]{:T(128)}, f32[32,4]{1,0:T(8,128)}, f32[32,4,128,128]{3,2,1,0:T(8,128)}, ...), condition=%wide.region_3.4_spmd, body=%wide.region_2.3_spmd.sunk | while | flops 131077 | bytes 786607 | solution.py:37
  391.2 1.6 maximum_add_fusion
  394.2 1.9 copy.463
  396.1 8.9 %multiply_reduce_fusion = (f32[1024]{0:T(1024)S(1)}, f32[1024,512]{0,1:T(8,128)}) fusion(bf16[1024,4096]{1,0:T(8,128)(2,1)S(1)} %bitcast.193, bf16[4096,512]{1,0:T(8,128)(2,1)} %param.18, f32[1024,512]{0,1:T(8,128)} %bitcast.199, f32[1024,512]{0,1:T(8,128)S(1)} %copy-done.7), kind=kOutput, calls=%fused_computation.29 | convolution fusion | flops 4300209152 | bytes 18878464 | tf_op jit(solution)/shard_map/dot_general | solution.py:41
  405.0 23.5 %psum.7 = f32[1024]{0:T(1024)S(1)} all-reduce(f32[1024]{0:T(1024)S(1)} %get-tuple-element.278), channel_id=1, replica_groups=mesh['seq'=32,'mp'=8] {'mp'}, use_global_device_ids=true, to_apply=%region_9.10 | all-reduce | flops 1024 | bytes 8192 | tf_op jit(solution)/shard_map/psum | solution.py:167
  428.4 1.8 multiply_convert_fusion.5
  (239 shorter events, 97.3 us)
Async XLA Ops:
  6.5 150.3 %copy-start = (bf16[4096,256]{1,0:T(8,128)(2,1)S(1)}, bf16[4096,256]{1,0:T(8,128)(2,1)}, u32[]{:S(2)}) copy-start(bf16[4096,256]{1,0:T(8,128)(2,1)} %param.19) | copy-start | bytes 6291460
  6.5 128.4 %all-gather.6.cloned.1.call-start = ((), (), s32[]{:S(2)}) async-start(), calls=%async_computation | async-start | bytes 9437184 | tf_op jit(solution)/shard_map/all_gather | solution.py:118
  7.3 268.9 %all-gather.10.cloned.1.call-start = ((), (), s32[]{:S(2)}) async-start(), calls=%async_computation.2 | async-start | bytes 8650752 | tf_op jit(solution)/shard_map/all_gather | solution.py:28
  8.6 6.6 %collective-permute-start.3 = (f32[1,1]{1,0:T(1,128)}, f32[1,1]{1,0:T(1,128)}, u32[]{:S(2)}, u32[]{:S(2)}) collective-permute-start(f32[1,1]{1,0:T(1,128)} %bitcast.6), channel_id=1, source_target_pairs={{8,0},{16,8},{24,16},{32,24},{40,32},{48,40},{56,48},{64,56},{72,6... | collective-permute-start | bytes 20 | tf_op jit(solution)/shard_map/ppermute | solution.py:17
  10.6 6.4 %collective-permute-start.1 = (f32[1,1]{1,0:T(1,128)}, f32[1,1]{1,0:T(1,128)}, u32[]{:S(2)}, u32[]{:S(2)}) collective-permute-start(f32[1,1]{1,0:T(1,128)} %bitcast.4), channel_id=1, source_target_pairs={{0,8},{8,16},{16,24},{24,32},{32,40},{40,48},{48,56},{56,64},{64,7... | collective-permute-start | bytes 20 | tf_op jit(solution)/shard_map/ppermute | solution.py:15
  18.4 123.0 %copy-start.35 = (f32[4]{0:T(128)S(1)}, f32[4]{0:T(128)}, u32[]{:S(2)}) copy-start(f32[4]{0:T(128)} %param.22) | copy-start | bytes 52
  141.4 25.3 %copy-start.15 = (f32[1024,4]{0,1:T(4,128)}, f32[1024,4]{0,1:T(4,128)S(1)}, u32[]{:S(2)}) copy-start(f32[1024,4]{0,1:T(4,128)S(1)} %rev.22) | copy-start | bytes 49156
  146.8 19.9 %copy-start.17 = (f32[4,4,256]{2,1,0:T(4,128)}, f32[4,4,256]{2,1,0:T(4,128)S(1)}, u32[]{:S(2)}) copy-start(f32[4,4,256]{2,1,0:T(4,128)S(1)} %reduce_window_sum.28) | copy-start | bytes 49156
  147.6 38.8 %copy-start.26 = (f32[4]{0:T(128)}, f32[4]{0:T(128)S(1)}, u32[]{:S(2)}) copy-start(f32[4]{0:T(128)S(1)} %get-tuple-element.270) | copy-start | bytes 52
  147.6 38.8 %copy-start.29 = (f32[4]{0:T(128)}, f32[4]{0:T(128)S(1)}, u32[]{:S(2)}) copy-start(f32[4]{0:T(128)S(1)} %get-tuple-element.269) | copy-start | bytes 52
  147.6 9.3 %copy-start.2 = (bf16[1024,4096]{1,0:T(8,128)(2,1)S(1)}, bf16[1024,4096]{1,0:T(8,128)(2,1)}, u32[]{:S(2)}) copy-start(bf16[1024,4096]{1,0:T(8,128)(2,1)} %all-gather.6.cloned.1.call-done) | copy-start | bytes 25165828
  160.7 9.1 %collective-permute-start = (f32[1,768]{0,1:T(8,128)S(1)}, f32[1,768]{0,1:T(8,128)S(1)}, u32[]{:S(2)}, u32[]{:S(2)}) collective-permute-start(f32[1,768]{0,1:T(8,128)S(1)} %copy.382), channel_id=1, source_target_pairs={{0,8},{8,16},{16,24},{24,32},{32,40},{40,48},{48,56},{56,64},{64,7... | collective-permute-start | bytes 9224 | tf_op jit(solution)/shard_map/ppermute | solution.py:15
  162.8 11.1 %collective-permute-start.2 = (f32[1,768]{0,1:T(8,128)S(1)}, f32[1,768]{0,1:T(8,128)S(1)}, u32[]{:S(2)}, u32[]{:S(2)}) collective-permute-start(f32[1,768]{0,1:T(8,128)S(1)} %copy.383), channel_id=1, source_target_pairs={{8,0},{16,8},{24,16},{32,24},{40,32},{48,40},{56,48},{64,56},{72,6... | collective-permute-start | bytes 9224 | tf_op jit(solution)/shard_map/ppermute | solution.py:17
  184.8 11.5 %copy-start.11 = (bf16[4,256,4,128]{1,0,3,2:T(4,128)(2,1)}, bf16[4,256,4,128]{1,0,3,2:T(4,128)(2,1)S(1)}, u32[]{:S(2)}) copy-start(bf16[4,256,4,128]{1,0,3,2:T(4,128)(2,1)S(1)} %reshape.239) | copy-start | bytes 3145732
  187.3 145.6 %all-gather.8.cloned.1.call-start = ((), (), s32[]{:S(2)}) async-start(), calls=%async_computation.1 | async-start | bytes 8650752 | tf_op jit(solution)/shard_map/all_gather | solution.py:28
  194.5 6.0 %copy-start.19 = (f32[4,4,256]{2,1,0:T(4,128)}, f32[4,4,256]{2,1,0:T(4,128)S(1)}, u32[]{:S(2)}) copy-start(f32[4,4,256]{2,1,0:T(4,128)S(1)} %reduce_window_sum.26) | copy-start | bytes 49156
  195.3 5.1 %copy-start.27 = (f32[4]{0:T(128)}, f32[4]{0:T(128)S(1)}, u32[]{:S(2)}) copy-start(f32[4]{0:T(128)S(1)} %get-tuple-element.275) | copy-start | bytes 52
  195.3 5.1 %copy-start.31 = (f32[4]{0:T(128)}, f32[4]{0:T(128)S(1)}, u32[]{:S(2)}) copy-start(f32[4]{0:T(128)S(1)} %get-tuple-element.274) | copy-start | bytes 52
  197.8 70.9 %copy-start.6 = (bf16[1024,128]{0,1:T(8,128)(2,1)S(1)}, bf16[1024,128]{0,1:T(8,128)(2,1)}, u32[]{:S(2)}) copy-start(bf16[1024,128]{0,1:T(8,128)(2,1)} %get-tuple-element.236) | copy-start | bytes 786436
  199.6 74.1 %copy-start.5 = (bf16[1024,128]{0,1:T(8,128)(2,1)S(1)}, bf16[1024,128]{0,1:T(8,128)(2,1)}, u32[]{:S(2)}) copy-start(bf16[1024,128]{0,1:T(8,128)(2,1)} %copy-done.4) | copy-start | bytes 786436
  304.8 81.5 %copy-start.24 = (f32[256,4]{0,1:T(4,128)S(1)}, f32[256,4]{0,1:T(4,128)}, u32[]{:S(2)}) copy-start(f32[256,4]{0,1:T(4,128)} %get-tuple-element.246) | copy-start | bytes 12292
  304.8 82.6 %copy-start.28 = (f32[4]{0:T(128)S(1)}, f32[4]{0:T(128)}, u32[]{:S(2)}) copy-start(f32[4]{0:T(128)} %copy-done.27) | copy-start | bytes 52
  304.8 82.7 %copy-start.33 = (f32[4]{0:T(128)S(1)}, f32[4]{0:T(128)}, u32[]{:S(2)}) copy-start(f32[4]{0:T(128)} %get-tuple-element.271) | copy-start | bytes 52
  332.9 54.7 %copy-start.23 = (f32[256,4]{0,1:T(4,128)S(1)}, f32[256,4]{0,1:T(4,128)}, u32[]{:S(2)}) copy-start(f32[256,4]{0,1:T(4,128)} %get-tuple-element.249) | copy-start | bytes 12292
  332.9 55.8 %copy-start.22 = (f32[256,4]{0,1:T(4,128)S(1)}, f32[256,4]{0,1:T(4,128)}, u32[]{:S(2)}) copy-start(f32[256,4]{0,1:T(4,128)} %get-tuple-element.248) | copy-start | bytes 12292
  332.9 57.0 %copy-start.21 = (f32[256,4]{0,1:T(4,128)S(1)}, f32[256,4]{0,1:T(4,128)}, u32[]{:S(2)}) copy-start(f32[256,4]{0,1:T(4,128)} %get-tuple-element.247) | copy-start | bytes 12292
  333.0 57.0 %copy-start.32 = (f32[4]{0:T(128)S(1)}, f32[4]{0:T(128)}, u32[]{:S(2)}) copy-start(f32[4]{0:T(128)} %copy-done.31) | copy-start | bytes 52
  386.3 4.9 %copy-start.10 = (bf16[4,256,4,128]{1,0,3,2:T(4,128)(2,1)S(1)}, bf16[4,256,4,128]{1,0,3,2:T(4,128)(2,1)}, u32[]{:S(2)}) copy-start(bf16[4,256,4,128]{1,0,3,2:T(4,128)(2,1)} %reshape.232) | copy-start | bytes 3145732
  388.7 7.3 %slice-start = ((s8[8388608]{0:T(1024)(128)(4,1)}), s8[4194304]{0:T(1024)(128)(4,1)S(1)}, s32[]{:S(2)}) async-start(s8[8388608]{0:T(1024)(128)(4,1)} %bitcast.192), calls=%async_computation.3 | async-start | bytes 8388608
  391.2 4.9 %slice-start.1 = ((s8[8388608]{0:T(1024)(128)(4,1)}), s8[4194304]{0:T(1024)(128)(4,1)S(1)}, s32[]{:S(2)}) async-start(s8[8388608]{0:T(1024)(128)(4,1)} %bitcast.192), calls=%async_computation.4 | async-start | bytes 8388608
  396.1 32.3 %copy-start.34 = (f32[512]{0:T(512)S(1)}, f32[512]{0:T(512)}, u32[]{:S(2)}) copy-start(f32[512]{0:T(512)} %param.25) | copy-start | bytes 6148
  396.1 35.5 %copy-start.1 = (bf16[4096,256]{1,0:T(8,128)(2,1)S(1)}, bf16[4096,256]{1,0:T(8,128)(2,1)}, u32[]{:S(2)}) copy-start(bf16[4096,256]{1,0:T(8,128)(2,1)} %param.19) | copy-start | bytes 6291460
  (13 other events, 44.2 us)
Sparse Core Ops, SparseCore 0:
  9.8 125.0 all-gather.5
  187.4 71.2 all-gather.9
  260.6 72.3 all-gather.7
where the time goes:
time: 442 us; the launch traced here: 438 us
  waiting for transfers between devices  151 us (34%)
  blocking collectives  88.5 us (20%)
  local copies, waits for them, and re-layouts  69 us (16%)
  other arithmetic  60.4 us (14%)
  matrix products  43.4 us (10%)
  between operations  13.9 us (3%)
  starting transfers between devices  10.7 us (2%)
    all_gather x1, waiting for transfers between devices, shards(): piece = lax.all_gather(tokens, 'mp', axis=1, tiled=True)  117 us
    all_gather x2, blocking collectives, entering_2(): gathered = jax.tree.map(lambda a: lax.all_gather(a, axis), part)  65.1 us
    add x31, other arithmetic, combine(): later[0][:, None, None] * earlier[1] + later[1]  32.6 us
    all_gather x2, waiting for transfers between devices, entering_2(): gathered = jax.tree.map(lambda a: lax.all_gather(a, axis), part)  28.1 us
    dot_general x4, matrix products, add_rows(): return jnp.dot(piece, weight, preferred_element_type=jnp.float32)  26.2 us
    psum x1, blocking collectives, shards(): squares = lax.psum(jnp.sum(gated * gated, axis=1), 'mp')  23.5 us
    mul x31, local copies, waits for them, and re-layouts, combine(): later[0][:, None, None] * earlier[1] + later[1]  21.3 us
    rev x1, local copies, waits for them, and re-layouts, shards(): read_states(backward_parts, enter_bwd).reshape(tok_rows, inner_dev)[::-1]  17.6 us
  transfers between devices with their start and end apart: 7, of which 4 were waited for; matrix products, arithmetic and copies ran while one was open for 14% of the time, Pallas kernels for 0%

commit v1 on v0

v1 whole, which is shorter than its diff:
```python
import functools

import jax
import jax.numpy as jnp
from jax import lax
from jax.experimental import pallas as pl
from jax.experimental.pallas import tpu as pltpu
from jax.sharding import PartitionSpec as P

BF16 = jnp.bfloat16
F32 = jnp.float32
BLOCK = 256
LANES = 128
HALO = 16
ANY = pl.BlockSpec(memory_space=pl.ANY)
LIMIT = 48 << 20


def silu(v):
    half = 0.5 * v
    return half + half * jnp.tanh(half)


def dot(a, b):
    return jnp.dot(a, b, preferred_element_type=F32)


def params():
    return pltpu.CompilerParams(vmem_limit_bytes=LIMIT)


def fetch_plan(count, split, rows):
    plan = []
    for slot in range(count):
        if slot in split:
            plan += [(slot, 0, rows // 2), (slot, rows // 2, rows // 2)]
        else:
            plan.append((slot, 0, rows))
    return plan


def load_pieces(step, plan, refs, buf, sems, extra=()):
    copies = [
        pltpu.make_async_copy(ref, buf.at[slot, pl.ds(at, rows)], sems.at[i])
        for i, (ref, (slot, at, rows)) in enumerate(zip(refs, plan))
    ]
    more = [(slot, pltpu.make_async_copy(src, dst, sems.at[len(refs) + i])) for i, (slot, src, dst) in enumerate(extra)]

    @pl.when(step == 0)
    def _():
        for c in copies:
            c.start()
        for _, c in more:
            c.start()

    for slot in range(1 + max(p[0] for p in plan)):

        @pl.when(step == slot)
        def _(slot=slot):
            for c, p in zip(copies, plan):
                if p[0] == slot:
                    c.wait()
            for s, c in more:
                if s == slot:
                    c.wait()


def project_kernel(plan, rows, halo, idx, *refs):
    n = len(plan)
    pieces = refs[:n]
    refs = refs[n:]
    extra = ()
    if halo:
        edge, refs = refs[0], refs[1:]
    wx, wb, wd, bias, xo, bo, do, buf, ax, ab, ad, sems = refs
    step = pl.program_id(0)
    if halo:
        extra = [(k, edge.at[idx[k]], buf.at[k, pl.ds(rows, HALO)]) for k in range(8)]
    load_pieces(step, plan, pieces, buf, sems, extra)

    lhs = buf[step]
    px, pb, pd = dot(lhs, wx[...]), dot(lhs, wb[...]), dot(lhs, wd[...])

    @pl.when(step == 0)
    def _():
        ax[...] = px
        ab[...] = pb
        ad[...] = pd

    @pl.when(step > 0)
    def _():
        ax[...] += px
        ab[...] += pb
        ad[...] += pd

    @pl.when(step == pl.num_programs(0) - 1)
    def _():
        xo[...] = ax[...].astype(BF16)
        bo[...] = ab[...].astype(BF16)
        v = ad[...] + bias[...]
        do[...] = jnp.maximum(v, 0.0) + jnp.log1p(jnp.exp(-jnp.abs(v)))


def project(idx, plan, pieces, edge, wx, wb, wd, bias):
    rows = pieces[0].shape[0]
    depth = pieces[0].shape[1]
    halo = edge is not None
    total = rows + (HALO if halo else 0)
    nx, nb = wx.shape[1], wb.shape[1]
    count = 8
    args = list(pieces) + ([edge] if halo else [])
    return pl.pallas_call(
        functools.partial(project_kernel, plan, rows, halo),
        grid_spec=pltpu.PrefetchScalarGridSpec(
            num_scalar_prefetch=1,
            grid=(count,),
            in_specs=[ANY] * len(args)
            + [
                pl.BlockSpec((depth, nx), lambda k, i: (i[k], 0)),
                pl.BlockSpec((depth, nb), lambda k, i: (i[k], 0)),
                pl.BlockSpec((depth, LANES), lambda k, i: (i[k], 0)),
                pl.BlockSpec((1, LANES), lambda k, i: (0, 0)),
            ],
            out_specs=[
                pl.BlockSpec((total, nx), lambda k, i: (0, 0)),
                pl.BlockSpec((total, nb), lambda k, i: (0, 0)),
                pl.BlockSpec((total, LANES), lambda k, i: (0, 0)),
            ],
            scratch_shapes=[
                pltpu.VMEM((count, total, depth), BF16),
                pltpu.VMEM((total, nx), F32),
                pltpu.VMEM((total, nb), F32),
                pltpu.VMEM((total, LANES), F32),
                pltpu.SemaphoreType.DMA((len(plan) + (8 if halo else 0),)),
            ],
        ),
        out_shape=[
            jax.ShapeDtypeStruct((total, nx), BF16),
            jax.ShapeDtypeStruct((total, nb), BF16),
            jax.ShapeDtypeStruct((total, LANES), F32),
        ],
        compiler_params=params(),
        cost_estimate=pl.CostEstimate(
            flops=2 * total * depth * count * (nx + nb + LANES),
            bytes_accessed=2 * depth * count * (total + nx + nb),
            transcendentals=0,
        ),
        name="project",
    )(idx, *args, wx, wb, wd, bias)


def gate_kernel(plan, rows, idx, *refs):
    n = len(plan)
    pieces = refs[:n]
    wz, out, buf, acc, sems = refs[n:]
    step = pl.program_id(0)
    load_pieces(step, plan, pieces, buf, sems)
    part = dot(buf[step], wz[...])

    @pl.when(step == 0)
    def _():
        acc[...] = part

    @pl.when(step > 0)
    def _():
        acc[...] += part

    @pl.when(step == pl.num_programs(0) - 1)
    def _():
        out[...] = silu(acc[...].astype(BF16).astype(F32))


def gate_project(idx, plan, pieces, wz, rows):
    depth = pieces[0].shape[1]
    nz = wz.shape[1]
    count = 8
    return pl.pallas_call(
        functools.partial(gate_kernel, plan, rows),
        grid_spec=pltpu.PrefetchScalarGridSpec(
            num_scalar_prefetch=1,
            grid=(count,),
            in_specs=[ANY] * len(pieces) + [pl.BlockSpec((depth, nz), lambda k, i: (i[k], 0))],
            out_specs=pl.BlockSpec((rows, nz), lambda k, i: (0, 0)),
            scratch_shapes=[
                pltpu.VMEM((count, rows, depth), BF16),
                pltpu.VMEM((rows, nz), F32),
                pltpu.SemaphoreType.DMA((len(plan),)),
            ],
        ),
        out_shape=jax.ShapeDtypeStruct((rows, nz), F32),
        compiler_params=params(),
        cost_estimate=pl.CostEstimate(
            flops=2 * rows * depth * count * nz, bytes_accessed=2 * depth * count * (rows + nz), transcendentals=0
        ),
        name="gate",
    )(idx, *pieces, wz)


def triangle():
    at = lax.broadcasted_iota(jnp.int32, (BLOCK, BLOCK), 0)
    before = lax.broadcasted_iota(jnp.int32, (BLOCK, BLOCK), 1)
    return before <= at


def running(dt, rates):
    a = -dt * rates
    cf = jnp.dot(triangle().astype(F32), a, precision=lax.Precision.HIGHEST, preferred_element_type=F32)
    return a, cf, cf - a


def spread(row, heads):
    return jnp.concatenate([jnp.broadcast_to(row[:, h : h + 1], (row.shape[0], LANES)) for h in range(heads)], axis=1)


def weigh(values, weights, heads):
    return jnp.concatenate(
        [values[:, h * LANES : (h + 1) * LANES] * weights[:, h : h + 1] for h in range(heads)], axis=1
    )


def state_kernel(heads, xa, xb, ba, bb, da, db, kx, kb, cols, links, rates, xs, bcs, dts, pay, loc, dec, xf, bf):
    half = xb.shape[0]
    blocks = 2 * half // BLOCK
    for dst, lo, hi in ((xf, xa, xb), (bf, ba, bb)):
        dst[8 : 8 + half] = lo[:half].astype(F32)
        dst[8 + half : 8 + 2 * half] = hi[...].astype(F32)
        edge = lo[half : half + HALO].astype(F32)
        dst[7:8] = edge[0:1]
        dst[8 + 2 * half : 9 + 2 * half] = edge[1:2]
    dts[:half] = da[:half]
    dts[half:] = db[...]
    rate = rates[...]
    sums = []
    for b in range(blocks):
        at = b * BLOCK
        col = cols[at : at + BLOCK]
        same_prev, same_next = col[:, 0:1], col[:, 1:2]

        def conv(src, taps):
            base = 8 + at
            before = src[base - 1 : base - 1 + BLOCK] * same_prev
            after = src[base + 1 : base + 1 + BLOCK] * same_next
            return silu(taps[0:1] * before + taps[1:2] * src[base : base + BLOCK] + taps[2:3] * after)

        x_blk = conv(xf, kx).astype(BF16)
        bc_blk = conv(bf, kb).astype(BF16)
        xs[at : at + BLOCK] = x_blk
        bcs[at : at + BLOCK] = bc_blk
        x_f = x_blk.astype(F32)
        b_t = bc_blk[:, :LANES].astype(F32).T.astype(BF16)
        dt = dts[at : at + BLOCK]
        a, cf, ce = running(dt, rate)
        last = cf[BLOCK - 1 : BLOCK]
        wf = jnp.exp(last - cf) * col[:, 2:3] * dt
        wb = jnp.exp(ce) * col[:, 3:4] * dt
        loc[0, b] = dot(b_t, weigh(x_f, wf, heads).astype(BF16))
        loc[1, b] = dot(b_t, weigh(x_f, wb, heads).astype(BF16))
        sums.append(jnp.exp(last))
    zero = jnp.zeros((loc.shape[2], loc.shape[3]), F32)
    link = links[...]
    for way in range(2):
        total = jnp.ones((1, LANES), F32)
        state = zero
        for i in range(blocks):
            b = i if way == 0 else blocks - 1 - i
            fresh = loc[way, b]
            loc[way, b] = state
            dec[way, b : b + 1] = spread(total, heads)
            step = sums[b] * link[way : way + 1, b : b + 1]
            state = spread(step, heads) * state + fresh
            total = total * step
        rows = state.shape[0]
        pay[way * rows : (way + 1) * rows, : state.shape[1]] = state.astype(BF16)
        high = total.astype(BF16).astype(F32)
        low = total - high
        eight = jnp.concatenate(
            [jnp.broadcast_to(p[:, h : h + 1], (1, LANES)) for p in (high, low) for h in range(heads)], axis=0
        ).astype(BF16)
        pair = jnp.concatenate([eight, eight], axis=0)
        for j in range(rows // 16):
            pay[way * rows + 16 * j : way * rows + 16 * j + 16, state.shape[1] :] = pair


def states(heads, xa, xb, ba, bb, da, db, kx, kb, cols, links, rates):
    rows = 2 * xb.shape[0]
    nx, nb = xb.shape[1], bb.shape[1]
    blocks = rows // BLOCK
    return pl.pallas_call(
        functools.partial(state_kernel, heads),
        out_shape=[
            jax.ShapeDtypeStruct((rows, nx), BF16),
            jax.ShapeDtypeStruct((rows, nb), BF16),
            jax.ShapeDtypeStruct((rows, LANES), F32),
            jax.ShapeDtypeStruct((2 * LANES, nx + LANES), BF16),
            jax.ShapeDtypeStruct((2, blocks, LANES, nx), F32),
            jax.ShapeDtypeStruct((2, blocks, nx), F32),
        ],
        scratch_shapes=[pltpu.VMEM((rows + 16, nx), F32), pltpu.VMEM((rows + 16, nb), F32)],
        compiler_params=params(),
        name="states",
    )(xa, xb, ba, bb, da, db, kx, kb, cols, links, rates)


def scan_kernel(heads, flag, src, out):
    count = src.shape[0]
    width = out.shape[2]
    ahead = flag[0] == 1

    def one(i, state):
        q = jnp.where(ahead, i, count - 1 - i)
        out[q] = state.astype(BF16)
        got = src[q].astype(F32)
        d = jnp.concatenate(
            [got[h : h + 1, width:] + got[heads + h : heads + h + 1, width:] for h in range(heads)], axis=1
        )
        return d * state + got[:, :width]

    lax.fori_loop(0, count, one, jnp.zeros((out.shape[1], width), F32), unroll=4)


def scan(heads, flag, src, width):
    return pl.pallas_call(
        functools.partial(scan_kernel, heads),
        in_specs=[pl.BlockSpec(memory_space=pltpu.SMEM), pl.BlockSpec(memory_space=pltpu.VMEM)],
        out_shape=jax.ShapeDtypeStruct((src.shape[0], src.shape[1], width), BF16),
        compiler_params=params(),
        name="scan",
    )(flag, src)


def inside_kernel(heads, xs, bcs, dts, cols, rowseg, rates, out):
    dt = dts[...]
    a, cf, ce = running(dt, rates[...])
    cf_r, ce_r, dt_r = cf.T, ce.T, dt.T
    bc = bcs[...]
    b_t = bc[:, :LANES].astype(F32).T.astype(BF16)
    scores = dot(bc[:, LANES:], b_t)
    same = cols[...][:, 6:7] == rowseg[0]
    scores = jnp.where(same, scores, 0.0)
    lower = triangle()
    x = xs[...]
    for h in range(heads):
        gap = jnp.where(lower, cf[:, h : h + 1] - cf_r[h : h + 1], ce_r[h : h + 1] - ce[:, h : h + 1])
        w = (scores * jnp.exp(gap) * dt_r[h : h + 1]).astype(BF16)
        out[:, h * LANES : (h + 1) * LANES] = dot(w, x[:, h * LANES : (h + 1) * LANES])


def inside(heads, xs, bcs, dts, cols, rowseg, rates):
    rows, nx = xs.shape
    nb = bcs.shape[1]
    row = lambda width: pl.BlockSpec((BLOCK, width), lambda b: (b, 0))
    return pl.pallas_call(
        functools.partial(inside_kernel, heads),
        grid=(rows // BLOCK,),
        in_specs=[
            row(nx),
            row(nb),
            row(LANES),
            row(cols.shape[1]),
            pl.BlockSpec((1, 1, BLOCK), lambda b: (b, 0, 0)),
            pl.BlockSpec((1, LANES), lambda b: (0, 0)),
        ],
        out_specs=row(nx),
        out_shape=jax.ShapeDtypeStruct((rows, nx), F32),
        compiler_params=params(),
        cost_estimate=pl.CostEstimate(
            flops=2 * rows * BLOCK * (nx + LANES), bytes_accessed=rows * nx * 6, transcendentals=rows * BLOCK * heads
        ),
        name="inside",
    )(xs, bcs, dts, cols, rowseg, rates)


def finish_kernel(heads, enter, loc, dec, y_in, sg, bcs, dts, cols, rates, out, ss):
    b = pl.program_id(0)
    dt = dts[...]
    a, cf, ce = running(dt, rates[...])
    last = cf[BLOCK - 1 : BLOCK]
    col = cols[...]
    open_f = jnp.exp(cf) * col[:, 4:5]
    open_b = jnp.exp(last - ce) * col[:, 5:6]
    c = bcs[...][:, LANES:]
    y = y_in[...]
    for way, opening in ((0, open_f), (1, open_b)):
        held = dec[way, b][None] * enter[way * LANES : (way + 1) * LANES].astype(F32) + loc[way, 0]
        y = y + weigh(dot(c, held.astype(BF16)), opening, heads)
    gated = y * sg[...]
    out[...] = gated
    sq = gated * gated
    part = sq[:, :LANES]
    for h in range(1, heads):
        part = part + sq[:, h * LANES : (h + 1) * LANES]
    ss[0] = jnp.sum(part.T, axis=0, keepdims=True)


def finish(heads, enter, loc, dec, y_in, sg, bcs, dts, cols, rates):
    rows, nx = y_in.shape
    nb = bcs.shape[1]
    blocks = rows // BLOCK
    row = lambda width: pl.BlockSpec((BLOCK, width), lambda b: (b, 0))
    return pl.pallas_call(
        functools.partial(finish_kernel, heads),
        grid=(blocks,),
        in_specs=[
            pl.BlockSpec(enter.shape, lambda b: (0, 0)),
            pl.BlockSpec((2, 1, LANES, nx), lambda b: (0, b, 0, 0)),
            pl.BlockSpec(dec.shape, lambda b: (0, 0, 0)),
            row(nx),
            row(nx),
            row(nb),
            row(LANES),
            row(cols.shape[1]),
            pl.BlockSpec((1, LANES), lambda b: (0, 0)),
        ],
        out_specs=[row(nx), pl.BlockSpec((1, 1, BLOCK), lambda b: (b, 0, 0))],
        out_shape=[jax.ShapeDtypeStruct((rows, nx), F32), jax.ShapeDtypeStruct((blocks, 1, BLOCK), F32)],
        compiler_params=params(),
        name="finish",
    )(enter, loc, dec, y_in, sg, bcs, dts, cols, rates)


def scale_kernel(columns, gated, gain, *refs):
    parts, out = refs[:-1], refs[-1]
    total = parts[0][0]
    for p in parts[1:]:
        total = total + p[0]
    scale = lax.rsqrt(total / columns + 1e-05)
    col = jnp.broadcast_to(scale, (LANES, BLOCK)).T[:, 0:1]
    out[...] = (gated[...] * col * gain[...]).astype(BF16)


def scale(columns, gated, gain, parts):
    rows, nx = gated.shape
    row = pl.BlockSpec((BLOCK, nx), lambda b: (b, 0))
    part = pl.BlockSpec((1, 1, BLOCK), lambda b: (b, 0, 0))
    return pl.pallas_call(
        functools.partial(scale_kernel, columns),
        grid=(rows // BLOCK,),
        in_specs=[row, pl.BlockSpec((1, nx), lambda b: (0, 0))] + [part] * len(parts),
        out_specs=row,
        out_shape=jax.ShapeDtypeStruct((rows, nx), BF16),
        compiler_params=params(),
        name="scale",
    )(gated, gain, *parts)


def shards(tokens, segment_ids, w_x, w_z, w_bc, w_dt, dt_bias, rates, conv_x, conv_bc, norm_gain):
    rows, depth = tokens.shape
    heads = w_dt.shape[1]
    nx = w_x.shape[1]
    blocks = rows // BLOCK
    mp, seq = lax.axis_size("mp"), lax.axis_size("seq")
    ring = mp // 2
    me = lax.axis_index("mp")
    row_at, col_at = me // ring, me % ring
    turn = lambda s: [(r * ring + c, r * ring + (c + s) % ring) for r in range(2) for c in range(ring)]
    send = lambda v, pairs: lax.ppermute(v, "mp", pairs)
    right, left = turn(1), turn(-1)
    across = [(i, (i + ring) % mp) for i in range(mp)]
    half = rows // 2
    quarter = half // 2

    first = []
    for i in range(2):
        own = tokens[i * half : (i + 1) * half]
        first.append((own, send(own, right), send(own, left), send(own, across)))
    pieces = []
    for own, r1, l1, p in first:
        o1, o2 = send(r1[:quarter], right), send(l1[quarter:], left)
        pr, pll = send(p, right), send(p, left)
        po1, po2 = send(o1, across), send(o2, across)
        pieces.append([own, r1, l1, p, o1, o2, pr, pll, po1, po2])
    plan = fetch_plan(8, (4, 7), half)
    idx = jnp.stack(
        [r * ring + (col_at + s) % ring for r, s in (
            (row_at, 0), (row_at, -1), (row_at, 1), (1 - row_at, 0),
            (row_at, 2), (1 - row_at, -1), (1 - row_at, 1), (1 - row_at, 2))]
    ).astype(jnp.int32)

    seg = segment_ids.astype(F32) + 1.0
    tail = jnp.concatenate([tokens[rows - 1 :], jnp.broadcast_to(seg[rows - 1 :, None], (1, LANES)).astype(BF16)], axis=1)
    head = jnp.concatenate([tokens[:1], jnp.broadcast_to(seg[:1, None], (1, LANES)).astype(BF16)], axis=1)
    before = lax.ppermute(tail, "seq", [(i, i + 1) for i in range(seq - 1)])
    after = lax.ppermute(head, "seq", [(i + 1, i) for i in range(seq - 1)])
    left_seg = before[0, depth].astype(F32)
    right_seg = after[0, depth].astype(F32)
    edge = jnp.concatenate([before[:, :depth], after[:, :depth], jnp.zeros((HALO - 2, depth), BF16)], axis=0)
    edge = lax.all_to_all(jnp.broadcast_to(edge[None], (mp, HALO, depth)), "mp", 0, 0)

    prev = jnp.concatenate([left_seg[None], seg[:-1]])
    nxt = jnp.concatenate([seg[1:], right_seg[None]])
    by = seg.reshape(blocks, BLOCK)
    ends, starts = by[:, -1], by[:, 0]
    prev_end = jnp.concatenate([left_seg[None], ends[:-1]])
    next_start = jnp.concatenate([starts[1:], right_seg[None]])
    wide = lambda v: jnp.broadcast_to(v[:, None], (blocks, BLOCK)).reshape(rows)
    cols = jnp.stack(
        [
            (seg == prev).astype(F32),
            (seg == nxt).astype(F32),
            (seg == wide(ends)).astype(F32),
            (seg == wide(starts)).astype(F32),
            (seg == wide(prev_end)).astype(F32),
            (seg == wide(next_start)).astype(F32),
            seg,
            seg,
        ],
        axis=1,
    )
    links = jnp.stack([(ends == prev_end).astype(F32), (starts == next_start).astype(F32)])
    rowseg = by[:, None, :]
    rate = jnp.pad(rates, (0, LANES - heads))[None]
    bias = jnp.pad(dt_bias, (0, LANES - heads))[None]
    w_d = jnp.pad(w_dt, ((0, 0), (0, LANES - heads)))

    xa, ba, da = project(idx, plan, pieces[0], edge, w_x, w_bc, w_d, bias)
    xb, bb, db = project(idx, plan, pieces[1], None, w_x, w_bc, w_d, bias)
    xs, bcs, dts, pay, loc, dec = states(heads, xa, xb, ba, bb, da, db, conv_x, conv_bc, cols, links, rate)

    width = nx
    got = lax.all_to_all(pay.reshape(seq, 2 * LANES // seq, width + LANES), "seq", 0, 0)
    flag = (lax.axis_index("seq") < seq // 2).astype(jnp.int32)[None]
    entered = scan(heads, flag, got, width)
    enter = lax.all_to_all(entered, "seq", 0, 0).reshape(2 * LANES, width)

    y_in = inside(heads, xs, bcs, dts, cols, rowseg, rate)
    sg = jnp.concatenate([gate_project(idx, plan, p, w_z, half) for p in pieces], axis=0)

    gated, ss = finish(heads, enter, loc, dec, y_in, sg, bcs, dts, cols, rate)
    ss = ss + send(ss, across)
    parts = [ss] + [send(ss, turn(s)) for s in range(1, ring)]
    return scale(nx * mp, gated, norm_gain[None], parts)


def solution(mesh):
    placed = (
        P("seq", "mp"),
        P("seq"),
        P(None, "mp"),
        P(None, "mp"),
        P(),
        P(None, "mp"),
        P("mp"),
        P("mp"),
        P(None, "mp"),
        P(),
        P("mp"),
    )
    return jax.shard_map(
        shards, mesh=mesh, in_specs=placed, out_specs=P("seq", "mp"), check_vma=False
    )
```

time: 442 us -> 191 us (0.43)
  the two profiles are of different devices: /device:TPU:232 before, /device:TPU:8 now
where the time goes in v1:
time: 191 us; the launch traced here: 190 us
  Pallas kernels  57.4 us (30%)
  starting transfers between devices  56.8 us (30%)
  local copies, waits for them, and re-layouts  36.3 us (19%)
  waiting for transfers between devices  31.6 us (17%)
  other arithmetic  5.66 us (3%)
    ppermute x22, starting transfers between devices, shards(): send = lambda v, pairs: lax.ppermute(v, 'mp', pairs)  34.2 us
    ppermute x22, waiting for transfers between devices, shards(): send = lambda v, pairs: lax.ppermute(v, 'mp', pairs)  25.2 us
    pallas_call x2, Pallas kernels, project(): pl.pallas_call(functools.partial(project_kernel, plan, rows, halo), grid_...  21.1 us
    unnamed x92, local copies, waits for them, and re-layouts  20.7 us
    pallas_call x2, Pallas kernels, gate_project(): pl.pallas_call(functools.partial(gate_kernel, plan, rows), grid_spec=pltp...  16.5 us
    all_to_all x1, starting transfers between devices, shards(): lax.all_to_all(pay.reshape(seq, 2 * LANES // seq, width + LANES), 'seq',...  10.3 us
    pallas_call x1, Pallas kernels, states(): pl.pallas_call(functools.partial(state_kernel, heads), out_shape=[jax.Sha...  7.11 us
    all_to_all x1, waiting for transfers between devices, shards(): lax.all_to_all(pay.reshape(seq, 2 * LANES // seq, width + LANES), 'seq',...  6.44 us
  transfers between devices with their start and end apart: 27, of which 8 were waited for; matrix products, arithmetic and copies ran while one was open for 13% of the time, Pallas kernels for 16%

profile of v1, /device:TPU:8, one launch (start us, length us, event | category | flops | bytes accessed | tf_op | source)
XLA Modules:
  0.0 189.6 jit_solution(1295188841389719728)
XLA Ops:
  1.3 2.4 %collective-permute-start.13 = (bf16[512,512]{1,0:T(8,128)(2,1)S(1)}, bf16[512,512]{1,0:T(8,128)(2,1)}, u32[]{:S(2)}, u32[]{:S(2)}) collective-permute-start(bf16[512,512]{1,0:T(8,128)(2,1)S(1)} %get-tuple-element.37.refs_0_), channel_id=1, source_target_pairs={{0,4},{1,5},{2,6},{3,7},{4,0},{5,1},{6,2},{7,3},{8,12},{9,13},{10,... | collective-permute-start | bytes 1572872 | tf_op jit(solution)/shard_map/ppermute | solution.py:456
  3.7 2.8 %collective-permute-start.12 = (bf16[512,512]{1,0:T(8,128)(2,1)S(1)}, bf16[512,512]{1,0:T(8,128)(2,1)S(1)}, u32[]{:S(2)}, u32[]{:S(2)}) collective-permute-start(bf16[512,512]{1,0:T(8,128)(2,1)S(1)} %get-tuple-element.37.refs_0_), channel_id=1, source_target_pairs={{0,3},{1,0},{2,1},{3,2},{4,7},{5,4},{6,5},{7,6},{8,11},{9,8},{10,9... | collective-permute-start | bytes 1572872 | tf_op jit(solution)/shard_map/ppermute | solution.py:456
  8.4 2.1 %collective-permute-start.10 = (bf16[1,640]{1,0:T(2,128)(2,1)S(1)}, bf16[1,640]{1,0:T(2,128)(2,1)S(1)}, u32[]{:S(2)}, u32[]{:S(2)}) collective-permute-start(bf16[1,640]{1,0:T(2,128)(2,1)S(1)} %concatenate.47), channel_id=1, source_target_pairs={{8,0},{16,8},{24,16},{32,24},{40,32},{48,40},{56,48},{64,56},{72,6... | collective-permute-start | bytes 3848 | tf_op jit(solution)/shard_map/ppermute | solution.py:483
  11.2 2.2 %collective-permute-start.9 = (bf16[1,640]{1,0:T(2,128)(2,1)S(1)}, bf16[1,640]{1,0:T(2,128)(2,1)S(1)}, u32[]{:S(2)}, u32[]{:S(2)}) collective-permute-start(bf16[1,640]{1,0:T(2,128)(2,1)S(1)} %concatenate.46), channel_id=1, source_target_pairs={{0,8},{8,16},{16,24},{24,32},{32,40},{40,48},{48,56},{56,64},{64,7... | collective-permute-start | bytes 3848 | tf_op jit(solution)/shard_map/ppermute | solution.py:482
  18.3 2.4 %pad.13.refs_13_.refs_12_ = bf16[4096,128]{1,0:T(8,128)(2,1)} pad(bf16[4096,4]{1,0:T(8,128)(2,1)} %copy.31, bf16[]{:T(256)} %constant.70.clone.1), padding=0_0x0_124 | pad | bytes 1081346 | tf_op jit(solution)/shard_map/jit(_pad)/pad | solution.py:513
  23.4 3.3 %collective-permute-start.1 = (bf16[512,512]{1,0:T(8,128)(2,1)S(1)}, bf16[512,512]{1,0:T(8,128)(2,1)S(1)}, u32[]{:S(2)}, u32[]{:S(2)}) collective-permute-start(bf16[512,512]{1,0:T(8,128)(2,1)S(1)} %get-tuple-element.38.refs_0_), channel_id=1, source_target_pairs={{0,3},{1,0},{2,1},{3,2},{4,7},{5,4},{6,5},{7,6},{8,11},{9,8},{10,9... | collective-permute-start | bytes 1572872 | tf_op jit(solution)/shard_map/ppermute | solution.py:456
  28.9 3.2 %collective-permute-start.15 = (bf16[256,512]{1,0:T(8,128)(2,1)}, bf16[256,512]{1,0:T(8,128)(2,1)S(1)}, u32[]{:S(2)}, u32[]{:S(2)}) collective-permute-start(bf16[256,512]{1,0:T(8,128)(2,1)} %slice.97), channel_id=1, source_target_pairs={{0,3},{1,0},{2,1},{3,2},{4,7},{5,4},{6,5},{7,6},{8,11},{9,8},{10,9... | collective-permute-start | bytes 786440 | tf_op jit(solution)/shard_map/ppermute | solution.py:456
  33.0 5.9 %collective-permute-done.1.refs_2_ = bf16[512,512]{1,0:T(8,128)(2,1)S(1)} collective-permute-done((bf16[512,512]{1,0:T(8,128)(2,1)S(1)}, bf16[512,512]{1,0:T(8,128)(2,1)S(1)}, u32[]{:S(2)}, u32[]{:S(2)}) %collective-permute-start.1) | collective-permute-done | bytes 524320 | tf_op jit(solution)/shard_map/ppermute | solution.py:456
  39.7 4.2 %collective-permute-done.refs_1_ = bf16[512,512]{1,0:T(8,128)(2,1)S(1)} collective-permute-done((bf16[512,512]{1,0:T(8,128)(2,1)S(1)}, bf16[512,512]{1,0:T(8,128)(2,1)S(1)}, u32[]{:S(2)}, u32[]{:S(2)}) %collective-permute-start) | collective-permute-done | bytes 524320 | tf_op jit(solution)/shard_map/ppermute | solution.py:456
  44.8 1.8 collective-permute-start.3
  48.5 3.8 %all-to-all-start = ((bf16[8,16,512]{2,1,0:T(8,128)(2,1)}), bf16[8,16,512]{2,1,0:T(8,128)(2,1)S(1)}, u32[]{:S(2)}, u32[]{:S(2)}) async-start(bf16[8,16,512]{2,1,0:T(8,128)(2,1)} %broadcast_in_dim.33), calls=%async_computation | async-start | bytes 262144 | tf_op jit(solution)/shard_map/all_to_all | solution.py:487
  52.3 2.0 %collective-permute-start.16 = (bf16[512,512]{1,0:T(8,128)(2,1)}, bf16[512,512]{1,0:T(8,128)(2,1)}, u32[]{:S(2)}, u32[]{:S(2)}) collective-permute-start(bf16[512,512]{1,0:T(8,128)(2,1)} %collective-permute-done.13.refs_3_), channel_id=1, source_target_pairs={{0,1},{1,2},{2,3},{3,0},{4,5},{5,6},{6,7},{7,4},{8,9},{9,10},{10,1... | collective-permute-start | bytes 1572872 | tf_op jit(solution)/shard_map/ppermute | solution.py:456
  57.1 4.9 %collective-permute-done.4.refs_5_ = bf16[256,512]{1,0:T(8,128)(2,1)} collective-permute-done((bf16[256,512]{1,0:T(8,128)(2,1)}, bf16[256,512]{1,0:T(8,128)(2,1)}, u32[]{:S(2)}, u32[]{:S(2)}) %collective-permute-start.4) | collective-permute-done | bytes 262176 | tf_op jit(solution)/shard_map/ppermute | solution.py:456
  63.9 2.5 %collective-permute-start.18 = (bf16[256,512]{1,0:T(8,128)(2,1)}, bf16[256,512]{1,0:T(8,128)(2,1)}, u32[]{:S(2)}, u32[]{:S(2)}) collective-permute-start(bf16[256,512]{1,0:T(8,128)(2,1)} %collective-permute-done.14.refs_4_), channel_id=1, source_target_pairs={{0,4},{1,5},{2,6},{3,7},{4,0},{5,1},{6,2},{7,3},{8,12},{9,13},{10,... | collective-permute-start | bytes 786440 | tf_op jit(solution)/shard_map/ppermute | solution.py:456
  71.3 1.6 collective-permute-start.8
  73.0 1.9 collective-permute-start.7
  74.9 3.5 %collective-permute-done.18.refs_8_ = bf16[256,512]{1,0:T(8,128)(2,1)} collective-permute-done((bf16[256,512]{1,0:T(8,128)(2,1)}, bf16[256,512]{1,0:T(8,128)(2,1)}, u32[]{:S(2)}, u32[]{:S(2)}) %collective-permute-start.18) | collective-permute-done | bytes 262176 | tf_op jit(solution)/shard_map/ppermute | solution.py:456
  80.1 10.4 %project.3 = (bf16[512,512]{1,0:T(8,128)(2,1)S(1)}, bf16[512,256]{1,0:T(8,128)(2,1)S(1)}, f32[512,128]{1,0:T(8,128)S(1)}) custom-call(s32[8]{0:T(128)S(1)} %stack.85.idx, bf16[512,512]{1,0:T(8,128)(2,1)S(1)} %get-tuple-element.37.refs_0_, bf16[512,512]{1,0:T(8,128)(2,1)S(1)} %collective-permute-done.11.refs_1_, ...), custom_call_target="tpu_custom_call" | custom-call | flops 3758096384 | bytes 10485760 | tf_op jit(solution)/shard_map/project/pallas_call | solution.py:112
  95.1 10.7 %project.2 = (bf16[528,512]{1,0:T(8,128)(2,1)S(1)}, bf16[528,256]{1,0:T(8,128)(2,1)S(1)}, f32[528,128]{1,0:T(8,128)S(1)}) custom-call(s32[8]{0:T(128)S(1)} %stack.85.idx, bf16[512,512]{1,0:T(8,128)(2,1)S(1)} %get-tuple-element.38.refs_0_, bf16[512,512]{1,0:T(8,128)(2,1)S(1)} %copy-done.11, bf16[512,512]{1,0:T(8,128)(2,1)S(1)} %collective-permute-done.1.refs_2_, ...), custom_call_target="tpu_custom_call" | custom-call | flops 3875536896 | bytes 10616832 | tf_op jit(solution)/shard_map/project/pallas_call | solution.py:112
  107.9 7.1 %states.1 = (bf16[1024,512]{1,0:T(8,128)(2,1)S(1)}, bf16[1024,256]{1,0:T(8,128)(2,1)S(1)}, f32[1024,128]{1,0:T(8,128)S(1)}, bf16[256,640]{1,0:T(8,128)(2,1)}, f3...) custom-call(bf16[528,512]{1,0:T(8,128)(2,1)S(1)} %get-tuple-element.19.xa, bf16[512,512]{1,0:T(8,128)(2,1)S(1)} %copy-done.19, ...), custom_call_target="tpu_custom_call" | custom-call | tf_op jit(solution)/shard_map/states/pallas_call | solution.py:288
  116.0 10.3 %all-to-all-start.1 = ((bf16[32,8,640]{2,1,0:T(8,128)(2,1)}), bf16[32,8,640]{2,1,0:T(8,128)(2,1)S(1)}, u32[]{:S(2)}, u32[]{:S(2)}) async-start(bf16[32,8,640]{2,1,0:T(8,128)(2,1)} %bitcast.22), calls=%async_computation.1 | async-start | bytes 655360 | tf_op jit(solution)/shard_map/all_to_all | solution.py:520
  127.6 4.4 %inside.1.y_in = f32[1024,512]{1,0:T(8,128)S(1)} custom-call(bf16[1024,512]{1,0:T(8,128)(2,1)S(1)} %copy-done.14, bf16[1024,256]{1,0:T(8,128)(2,1)S(1)} %get-tuple-element.29.bcs, f32[1024,128]{1,0:T(8,128)S(1)} %get-tuple-element.30.dts, f32[1024,8]{1,0:T(8,128)S(1)} %copy.32.cols, f32[4,1,256]{2,1,0:T(1,128)S(1)} %bitcast.49, f32[1,128]{1,0:T(1,128)S(1)} %copy-done.28), custom_call_target="tpu_custom_call" | custom-call | flops 335544320 | bytes 3145728 | tf_op jit(solution)/shard_map/inside/pallas_call | solution.py:352
  133.4 6.4 %all-to-all-done.1.src = bf16[32,8,640]{2,1,0:T(8,128)(2,1)S(1)} async-done(((bf16[32,8,640]{2,1,0:T(8,128)(2,1)}), bf16[32,8,640]{2,1,0:T(8,128)(2,1)S(1)}, u32[]{:S(2)}, u32[]{:S(2)}) %all-to-all-start.1) | async-done | bytes 327712 | tf_op jit(solution)/shard_map/all_to_all | solution.py:520
  140.7 4.1 %all-to-all-start.2 = ((bf16[32,8,512]{2,1,0:T(8,128)(2,1)}), bf16[32,8,512]{2,1,0:T(8,128)(2,1)S(1)}, u32[]{:S(2)}, u32[]{:S(2)}) async-start(bf16[32,8,512]{2,1,0:T(8,128)(2,1)} %scan.1), calls=%async_computation.2 | async-start | bytes 524288 | tf_op jit(solution)/shard_map/all_to_all | solution.py:523
  146.9 8.3 %gate.2 = f32[512,512]{1,0:T(8,128)S(1)} custom-call(s32[8]{0:T(128)S(1)} %stack.85.idx, bf16[512,512]{1,0:T(8,128)(2,1)S(1)} %get-tuple-element.38.refs_0_, bf16[512,512]{1,0:T(8,128)(2,1)S(1)} %copy-done.12, bf16[512,512]{1,0:T(8,128)(2,1)S(1)} %copy-done.9, bf16[512,512]{1,0:T(8,128)(2,1)} %collective-permute-done.2.refs_3_, ...), custom_call_target="tpu_custom_call" | custom-call | flops 2147483648 | bytes 8388608 | tf_op jit(solution)/shard_map/gate/pallas_call | solution.py:177
  155.3 8.1 %gate.3 = f32[512,512]{1,0:T(8,128)S(1)} custom-call(s32[8]{0:T(128)S(1)} %stack.85.idx, bf16[512,512]{1,0:T(8,128)(2,1)S(1)} %get-tuple-element.37.refs_0_, bf16[512,512]{1,0:T(8,128)(2,1)S(1)} %copy-done.7, bf16[512,512]{1,0:T(8,128)(2,1)S(1)} %copy-done.5, bf16[512,512]{1,0:T(8,128)(2,1)} %collective-permute-done.13.refs_3_, ...), custom_call_target="tpu_custom_call" | custom-call | flops 2147483648 | bytes 8388608 | tf_op jit(solution)/shard_map/gate/pallas_call | solution.py:177
  166.8 5.4 %finish.1 = (f32[1024,512]{1,0:T(8,128)S(1)}, f32[4,1,256]{2,1,0:T(1,128)S(1)}) custom-call(bf16[256,512]{1,0:T(8,128)(2,1)S(1)} %bitcast.46, f32[2,4,128,512]{3,2,1,0:T(8,128)S(1)} %copy-done.1, f32[2,4,512]{2,1,0:T(4,128)S(1)} %get-tuple-element.27.dec, f32[1024,512]{1,0:T(8,128)} %copy-done, f32[1024,512]{1,0:T(8,128)} %pad_maximum_fusion.sg, ...), custom_call_target="tpu_custom_call" | custom-call | tf_op jit(solution)/shard_map/finish/pallas_call | solution.py:400
  172.2 2.1 %collective-permute-start.20 = (f32[4,1,256]{2,1,0:T(1,128)S(1)}, f32[4,1,256]{2,1,0:T(1,128)S(1)}, u32[]{:S(2)}, u32[]{:S(2)}) collective-permute-start(f32[4,1,256]{2,1,0:T(1,128)S(1)} %get-tuple-element.32), channel_id=1, source_target_pairs={{0,4},{1,5},{2,6},{3,7},{4,0},{5,1},{6,2},{7,3},{8,12},{9,13},{10,... | collective-permute-start | bytes 12296 | tf_op jit(solution)/shard_map/ppermute | solution.py:456
  174.3 3.1 %collective-permute-done.20 = f32[4,1,256]{2,1,0:T(1,128)S(1)} collective-permute-done((f32[4,1,256]{2,1,0:T(1,128)S(1)}, f32[4,1,256]{2,1,0:T(1,128)S(1)}, u32[]{:S(2)}, u32[]{:S(2)}) %collective-permute-start.20) | collective-permute-done | bytes 4128 | tf_op jit(solution)/shard_map/ppermute | solution.py:456
  177.4 3.8 %collective-permute-start.23 = (f32[4,1,256]{2,1,0:T(1,128)S(1)}, f32[4,1,256]{2,1,0:T(1,128)S(1)}, u32[]{:S(2)}, u32[]{:S(2)}) collective-permute-start(f32[4,1,256]{2,1,0:T(1,128)S(1)} %add.94.refs_0_), channel_id=1, source_target_pairs={{0,3},{1,0},{2,1},{3,2},{4,7},{5,4},{6,5},{7,6},{8,11},{9,8},{10,9... | collective-permute-start | bytes 12296 | tf_op jit(solution)/shard_map/ppermute | solution.py:456
  184.1 2.2 %collective-permute-done.22.refs_2_ = f32[4,1,256]{2,1,0:T(1,128)S(1)} collective-permute-done((f32[4,1,256]{2,1,0:T(1,128)S(1)}, f32[4,1,256]{2,1,0:T(1,128)S(1)}, u32[]{:S(2)}, u32[]{:S(2)}) %collective-permute-start.22) | collective-permute-done | bytes 4128 | tf_op jit(solution)/shard_map/ppermute | solution.py:456
  187.6 2.0 %scale.1 = bf16[1024,512]{1,0:T(8,128)(2,1)} custom-call(f32[1024,512]{1,0:T(8,128)S(1)} %get-tuple-element.31.gated, f32[1,512]{1,0:T(1,128)S(1)} %bitcast.50, f32[4,1,256]{2,1,0:T(1,128)S(1)} %add.94.refs_0_, f32[4,1,256]{2,1,0:T(1,128)S(1)} %collective-permute-done.21.refs_1_, f32[4,1,256]{2,1,0:T(1,128)S(1)} %collective-permute-done.22.refs_2_, ...), custom_call_target="tpu_custom_call" | custom-call | tf_op jit(solution)/shard_map/scale/pallas_call | solution.py:435
  (157 shorter events, 48.5 us)
Async XLA Ops:
  1.3 27.6 %collective-permute-start.13 = (bf16[512,512]{1,0:T(8,128)(2,1)S(1)}, bf16[512,512]{1,0:T(8,128)(2,1)}, u32[]{:S(2)}, u32[]{:S(2)}) collective-permute-start(bf16[512,512]{1,0:T(8,128)(2,1)S(1)} %get-tuple-element.37.refs_0_), channel_id=1, source_target_pairs={{0,4},{1,5},{2,6},{3,7},{4,0},{5,1},{6,2},{7,3},{8,12},{9,13},{10,... | collective-permute-start | bytes 1572872 | tf_op jit(solution)/shard_map/ppermute | solution.py:456
  3.7 24.2 %collective-permute-start.12 = (bf16[512,512]{1,0:T(8,128)(2,1)S(1)}, bf16[512,512]{1,0:T(8,128)(2,1)S(1)}, u32[]{:S(2)}, u32[]{:S(2)}) collective-permute-start(bf16[512,512]{1,0:T(8,128)(2,1)S(1)} %get-tuple-element.37.refs_0_), channel_id=1, source_target_pairs={{0,3},{1,0},{2,1},{3,2},{4,7},{5,4},{6,5},{7,6},{8,11},{9,8},{10,9... | collective-permute-start | bytes 1572872 | tf_op jit(solution)/shard_map/ppermute | solution.py:456
  6.5 25.6 %collective-permute-start.11 = (bf16[512,512]{1,0:T(8,128)(2,1)S(1)}, bf16[512,512]{1,0:T(8,128)(2,1)S(1)}, u32[]{:S(2)}, u32[]{:S(2)}) collective-permute-start(bf16[512,512]{1,0:T(8,128)(2,1)S(1)} %get-tuple-element.37.refs_0_), channel_id=1, source_target_pairs={{0,1},{1,2},{2,3},{3,0},{4,5},{5,6},{6,7},{7,4},{8,9},{9,10},{10,1... | collective-permute-start | bytes 1572872 | tf_op jit(solution)/shard_map/ppermute | solution.py:456
  8.4 12.5 %collective-permute-start.10 = (bf16[1,640]{1,0:T(2,128)(2,1)S(1)}, bf16[1,640]{1,0:T(2,128)(2,1)S(1)}, u32[]{:S(2)}, u32[]{:S(2)}) collective-permute-start(bf16[1,640]{1,0:T(2,128)(2,1)S(1)} %concatenate.47), channel_id=1, source_target_pairs={{8,0},{16,8},{24,16},{32,24},{40,32},{48,40},{56,48},{64,56},{72,6... | collective-permute-start | bytes 3848 | tf_op jit(solution)/shard_map/ppermute | solution.py:483
  11.2 12.2 %collective-permute-start.9 = (bf16[1,640]{1,0:T(2,128)(2,1)S(1)}, bf16[1,640]{1,0:T(2,128)(2,1)S(1)}, u32[]{:S(2)}, u32[]{:S(2)}) collective-permute-start(bf16[1,640]{1,0:T(2,128)(2,1)S(1)} %concatenate.46), channel_id=1, source_target_pairs={{0,8},{8,16},{16,24},{24,32},{32,40},{40,48},{48,56},{56,64},{64,7... | collective-permute-start | bytes 3848 | tf_op jit(solution)/shard_map/ppermute | solution.py:482
  20.9 23.8 %collective-permute-start.2 = (bf16[512,512]{1,0:T(8,128)(2,1)S(1)}, bf16[512,512]{1,0:T(8,128)(2,1)}, u32[]{:S(2)}, u32[]{:S(2)}) collective-permute-start(bf16[512,512]{1,0:T(8,128)(2,1)S(1)} %get-tuple-element.38.refs_0_), channel_id=1, source_target_pairs={{0,4},{1,5},{2,6},{3,7},{4,0},{5,1},{6,2},{7,3},{8,12},{9,13},{10,... | collective-permute-start | bytes 1572872 | tf_op jit(solution)/shard_map/ppermute | solution.py:456
  23.4 15.5 %collective-permute-start.1 = (bf16[512,512]{1,0:T(8,128)(2,1)S(1)}, bf16[512,512]{1,0:T(8,128)(2,1)S(1)}, u32[]{:S(2)}, u32[]{:S(2)}) collective-permute-start(bf16[512,512]{1,0:T(8,128)(2,1)S(1)} %get-tuple-element.38.refs_0_), channel_id=1, source_target_pairs={{0,3},{1,0},{2,1},{3,2},{4,7},{5,4},{6,5},{7,6},{8,11},{9,8},{10,9... | collective-permute-start | bytes 1572872 | tf_op jit(solution)/shard_map/ppermute | solution.py:456
  27.9 62.5 %copy-start.4 = (bf16[512,512]{1,0:T(8,128)(2,1)}, bf16[512,512]{1,0:T(8,128)(2,1)S(1)}, u32[]{:S(2)}) copy-start(bf16[512,512]{1,0:T(8,128)(2,1)S(1)} %collective-permute-done.12.refs_2_) | copy-start | bytes 1572868
  27.9 15.9 %collective-permute-start = (bf16[512,512]{1,0:T(8,128)(2,1)S(1)}, bf16[512,512]{1,0:T(8,128)(2,1)S(1)}, u32[]{:S(2)}, u32[]{:S(2)}) collective-permute-start(bf16[512,512]{1,0:T(8,128)(2,1)S(1)} %get-tuple-element.38.refs_0_), channel_id=1, source_target_pairs={{0,1},{1,2},{2,3},{3,0},{4,5},{5,6},{6,7},{7,4},{8,9},{9,10},{10,1... | collective-permute-start | bytes 1572872 | tf_op jit(solution)/shard_map/ppermute | solution.py:456
  28.9 23.4 %collective-permute-start.15 = (bf16[256,512]{1,0:T(8,128)(2,1)}, bf16[256,512]{1,0:T(8,128)(2,1)S(1)}, u32[]{:S(2)}, u32[]{:S(2)}) collective-permute-start(bf16[256,512]{1,0:T(8,128)(2,1)} %slice.97), channel_id=1, source_target_pairs={{0,3},{1,0},{2,1},{3,2},{4,7},{5,4},{6,5},{7,6},{8,11},{9,8},{10,9... | collective-permute-start | bytes 786440 | tf_op jit(solution)/shard_map/ppermute | solution.py:456
  32.1 58.3 %copy-start.6 = (bf16[512,512]{1,0:T(8,128)(2,1)}, bf16[512,512]{1,0:T(8,128)(2,1)S(1)}, u32[]{:S(2)}) copy-start(bf16[512,512]{1,0:T(8,128)(2,1)S(1)} %collective-permute-done.11.refs_1_) | copy-start | bytes 1572868
  32.1 30.9 %collective-permute-start.17 = (bf16[512,512]{1,0:T(8,128)(2,1)}, bf16[512,512]{1,0:T(8,128)(2,1)S(1)}, u32[]{:S(2)}, u32[]{:S(2)}) collective-permute-start(bf16[512,512]{1,0:T(8,128)(2,1)} %collective-permute-done.13.refs_3_), channel_id=1, source_target_pairs={{0,3},{1,0},{2,1},{3,2},{4,7},{5,4},{6,5},{7,6},{8,11},{9,8},{10,9... | collective-permute-start | bytes 1572872 | tf_op jit(solution)/shard_map/ppermute | solution.py:456
  38.9 54.5 %copy-start.8 = (bf16[512,512]{1,0:T(8,128)(2,1)}, bf16[512,512]{1,0:T(8,128)(2,1)S(1)}, u32[]{:S(2)}) copy-start(bf16[512,512]{1,0:T(8,128)(2,1)S(1)} %collective-permute-done.1.refs_2_) | copy-start | bytes 1572868
  38.9 16.8 %collective-permute-start.14 = (bf16[256,512]{1,0:T(8,128)(2,1)}, bf16[256,512]{1,0:T(8,128)(2,1)}, u32[]{:S(2)}, u32[]{:S(2)}) collective-permute-start(bf16[256,512]{1,0:T(8,128)(2,1)} %slice.96), channel_id=1, source_target_pairs={{0,1},{1,2},{2,3},{3,0},{4,5},{5,6},{6,7},{7,4},{8,9},{9,10},{10,1... | collective-permute-start | bytes 786440 | tf_op jit(solution)/shard_map/ppermute | solution.py:456
  43.9 18.2 %collective-permute-start.4 = (bf16[256,512]{1,0:T(8,128)(2,1)}, bf16[256,512]{1,0:T(8,128)(2,1)}, u32[]{:S(2)}, u32[]{:S(2)}) collective-permute-start(bf16[256,512]{1,0:T(8,128)(2,1)} %slice.93), channel_id=1, source_target_pairs={{0,3},{1,0},{2,1},{3,2},{4,7},{5,4},{6,5},{7,6},{8,11},{9,8},{10,9... | collective-permute-start | bytes 786440 | tf_op jit(solution)/shard_map/ppermute | solution.py:456
  44.8 17.3 %collective-permute-start.3 = (bf16[256,512]{1,0:T(8,128)(2,1)}, bf16[256,512]{1,0:T(8,128)(2,1)}, u32[]{:S(2)}, u32[]{:S(2)}) collective-permute-start(bf16[256,512]{1,0:T(8,128)(2,1)} %slice.92), channel_id=1, source_target_pairs={{0,1},{1,2},{2,3},{3,0},{4,5},{5,6},{6,7},{7,4},{8,9},{9,10},{10,1... | collective-permute-start | bytes 786440 | tf_op jit(solution)/shard_map/ppermute | solution.py:456
  48.5 44.9 %all-to-all-start = ((bf16[8,16,512]{2,1,0:T(8,128)(2,1)}), bf16[8,16,512]{2,1,0:T(8,128)(2,1)S(1)}, u32[]{:S(2)}, u32[]{:S(2)}) async-start(bf16[8,16,512]{2,1,0:T(8,128)(2,1)} %broadcast_in_dim.33), calls=%async_computation | async-start | bytes 262144 | tf_op jit(solution)/shard_map/all_to_all | solution.py:487
  52.3 19.0 %collective-permute-start.16 = (bf16[512,512]{1,0:T(8,128)(2,1)}, bf16[512,512]{1,0:T(8,128)(2,1)}, u32[]{:S(2)}, u32[]{:S(2)}) collective-permute-start(bf16[512,512]{1,0:T(8,128)(2,1)} %collective-permute-done.13.refs_3_), channel_id=1, source_target_pairs={{0,1},{1,2},{2,3},{3,0},{4,5},{5,6},{6,7},{7,4},{8,9},{9,10},{10,1... | collective-permute-start | bytes 1572872 | tf_op jit(solution)/shard_map/ppermute | solution.py:456
  55.7 37.7 %collective-permute-start.6 = (bf16[512,512]{1,0:T(8,128)(2,1)}, bf16[512,512]{1,0:T(8,128)(2,1)}, u32[]{:S(2)}, u32[]{:S(2)}) collective-permute-start(bf16[512,512]{1,0:T(8,128)(2,1)} %collective-permute-done.2.refs_3_), channel_id=1, source_target_pairs={{0,3},{1,0},{2,1},{3,2},{4,7},{5,4},{6,5},{7,6},{8,11},{9,8},{10,9... | collective-permute-start | bytes 1572872 | tf_op jit(solution)/shard_map/ppermute | solution.py:456
  62.0 31.4 %collective-permute-start.5 = (bf16[512,512]{1,0:T(8,128)(2,1)}, bf16[512,512]{1,0:T(8,128)(2,1)}, u32[]{:S(2)}, u32[]{:S(2)}) collective-permute-start(bf16[512,512]{1,0:T(8,128)(2,1)} %collective-permute-done.2.refs_3_), channel_id=1, source_target_pairs={{0,1},{1,2},{2,3},{3,0},{4,5},{5,6},{6,7},{7,4},{8,9},{9,10},{10,1... | collective-permute-start | bytes 1572872 | tf_op jit(solution)/shard_map/ppermute | solution.py:456
  62.0 10.9 %collective-permute-start.19 = (bf16[256,512]{1,0:T(8,128)(2,1)S(1)}, bf16[256,512]{1,0:T(8,128)(2,1)}, u32[]{:S(2)}, u32[]{:S(2)}) collective-permute-start(bf16[256,512]{1,0:T(8,128)(2,1)S(1)} %collective-permute-done.15.refs_5_), channel_id=1, source_target_pairs={{0,4},{1,5},{2,6},{3,7},{4,0},{5,1},{6,2},{7,3},{8,12},{9,13},{10,... | collective-permute-start | bytes 786440 | tf_op jit(solution)/shard_map/ppermute | solution.py:456
  63.9 14.5 %collective-permute-start.18 = (bf16[256,512]{1,0:T(8,128)(2,1)}, bf16[256,512]{1,0:T(8,128)(2,1)}, u32[]{:S(2)}, u32[]{:S(2)}) collective-permute-start(bf16[256,512]{1,0:T(8,128)(2,1)} %collective-permute-done.14.refs_4_), channel_id=1, source_target_pairs={{0,4},{1,5},{2,6},{3,7},{4,0},{5,1},{6,2},{7,3},{8,12},{9,13},{10,... | collective-permute-start | bytes 786440 | tf_op jit(solution)/shard_map/ppermute | solution.py:456
  71.3 22.1 %collective-permute-start.8 = (bf16[256,512]{1,0:T(8,128)(2,1)}, bf16[256,512]{1,0:T(8,128)(2,1)}, u32[]{:S(2)}, u32[]{:S(2)}) collective-permute-start(bf16[256,512]{1,0:T(8,128)(2,1)} %collective-permute-done.4.refs_5_), channel_id=1, source_target_pairs={{0,4},{1,5},{2,6},{3,7},{4,0},{5,1},{6,2},{7,3},{8,12},{9,13},{10,... | collective-permute-start | bytes 786440 | tf_op jit(solution)/shard_map/ppermute | solution.py:456
  73.0 20.4 %collective-permute-start.7 = (bf16[256,512]{1,0:T(8,128)(2,1)}, bf16[256,512]{1,0:T(8,128)(2,1)}, u32[]{:S(2)}, u32[]{:S(2)}) collective-permute-start(bf16[256,512]{1,0:T(8,128)(2,1)} %collective-permute-done.3.refs_4_), channel_id=1, source_target_pairs={{0,4},{1,5},{2,6},{3,7},{4,0},{5,1},{6,2},{7,3},{8,12},{9,13},{10,... | collective-permute-start | bytes 786440 | tf_op jit(solution)/shard_map/ppermute | solution.py:456
  80.1 25.8 %copy-start.26 = (f32[3,512]{1,0:T(4,128)S(1)}, f32[3,512]{1,0:T(4,128)}, u32[]{:S(2)}) copy-start(f32[3,512]{1,0:T(4,128)} %kx.1) | copy-start | bytes 18436
  116.0 23.8 %all-to-all-start.1 = ((bf16[32,8,640]{2,1,0:T(8,128)(2,1)}), bf16[32,8,640]{2,1,0:T(8,128)(2,1)S(1)}, u32[]{:S(2)}, u32[]{:S(2)}) async-start(bf16[32,8,640]{2,1,0:T(8,128)(2,1)} %bitcast.22), calls=%async_computation.1 | async-start | bytes 655360 | tf_op jit(solution)/shard_map/all_to_all | solution.py:520
  140.7 24.3 %all-to-all-start.2 = ((bf16[32,8,512]{2,1,0:T(8,128)(2,1)}), bf16[32,8,512]{2,1,0:T(8,128)(2,1)S(1)}, u32[]{:S(2)}, u32[]{:S(2)}) async-start(bf16[32,8,512]{2,1,0:T(8,128)(2,1)} %scan.1), calls=%async_computation.2 | async-start | bytes 524288 | tf_op jit(solution)/shard_map/all_to_all | solution.py:523
  166.8 20.8 %copy-start.31 = (f32[512]{0:T(512)S(1)}, f32[512]{0:T(512)}, u32[]{:S(2)}) copy-start(f32[512]{0:T(512)} %param.21) | copy-start | bytes 6148
  172.2 5.2 %collective-permute-start.20 = (f32[4,1,256]{2,1,0:T(1,128)S(1)}, f32[4,1,256]{2,1,0:T(1,128)S(1)}, u32[]{:S(2)}, u32[]{:S(2)}) collective-permute-start(f32[4,1,256]{2,1,0:T(1,128)S(1)} %get-tuple-element.32), channel_id=1, source_target_pairs={{0,4},{1,5},{2,6},{3,7},{4,0},{5,1},{6,2},{7,3},{8,12},{9,13},{10,... | collective-permute-start | bytes 12296 | tf_op jit(solution)/shard_map/ppermute | solution.py:456
  177.4 6.7 %collective-permute-start.23 = (f32[4,1,256]{2,1,0:T(1,128)S(1)}, f32[4,1,256]{2,1,0:T(1,128)S(1)}, u32[]{:S(2)}, u32[]{:S(2)}) collective-permute-start(f32[4,1,256]{2,1,0:T(1,128)S(1)} %add.94.refs_0_), channel_id=1, source_target_pairs={{0,3},{1,0},{2,1},{3,2},{4,7},{5,4},{6,5},{7,6},{8,11},{9,8},{10,9... | collective-permute-start | bytes 12296 | tf_op jit(solution)/shard_map/ppermute | solution.py:456
  181.2 5.1 %collective-permute-start.22 = (f32[4,1,256]{2,1,0:T(1,128)S(1)}, f32[4,1,256]{2,1,0:T(1,128)S(1)}, u32[]{:S(2)}, u32[]{:S(2)}) collective-permute-start(f32[4,1,256]{2,1,0:T(1,128)S(1)} %add.94.refs_0_), channel_id=1, source_target_pairs={{0,2},{1,3},{2,0},{3,1},{4,6},{5,7},{6,4},{7,5},{8,10},{9,11},{10,... | collective-permute-start | bytes 12296 | tf_op jit(solution)/shard_map/ppermute | solution.py:456
  182.8 4.8 %collective-permute-start.21 = (f32[4,1,256]{2,1,0:T(1,128)S(1)}, f32[4,1,256]{2,1,0:T(1,128)S(1)}, u32[]{:S(2)}, u32[]{:S(2)}) collective-permute-start(f32[4,1,256]{2,1,0:T(1,128)S(1)} %add.94.refs_0_), channel_id=1, source_target_pairs={{0,1},{1,2},{2,3},{3,0},{4,5},{5,6},{6,7},{7,4},{8,9},{9,10},{10,1... | collective-permute-start | bytes 12296 | tf_op jit(solution)/shard_map/ppermute | solution.py:456
  (37 other events, 239.0 us)

commit v2 on v1

v2 whole, which is shorter than its diff:
```python
import functools

import jax
import jax.numpy as jnp
from jax import lax
from jax.experimental import pallas as pl
from jax.experimental.pallas import tpu as pltpu
from jax.sharding import PartitionSpec as P

BF16 = jnp.bfloat16
F32 = jnp.float32
BLOCK = 256
LANES = 128
SUB = 8
ANY = pl.BlockSpec(memory_space=pl.ANY)
VMEM = pl.BlockSpec(memory_space=pltpu.VMEM)
SMEM = pl.BlockSpec(memory_space=pltpu.SMEM)


def silu(v):
    half = 0.5 * v
    return half + half * jnp.tanh(half)


def dot(a, b):
    return jnp.dot(a, b, preferred_element_type=F32)


def params(mib):
    return pltpu.CompilerParams(vmem_limit_bytes=mib << 20)


def far(*arrays):
    return [pltpu.with_memory_space_constraint(a, pltpu.HBM) for a in arrays]


def fetch(pairs, sems):
    copies = [pltpu.make_async_copy(src, dst, sems.at[i]) for i, (src, dst) in enumerate(pairs)]
    for c in copies:
        c.start()
    return copies


def rows_of(ref, idx, k, depth):
    return ref.at[pl.ds(pl.multiple_of(idx[k] * depth, depth), depth)]


def nt_dot(a, b):
    return lax.dot_general(a, b, (((1,), (1,)), ((), ())), preferred_element_type=F32)


def place(plan, pieces, buf):
    return [(slot, ref, buf.at[slot, pl.ds(at, rows)]) for ref, (slot, at, rows) in zip(pieces, plan)]


def plan_of(pieces, keep=None):
    whole = max(p.shape[0] for p in pieces)
    full = keep or whole
    plan, slot, at = [], 0, 0
    for p in pieces:
        rows = min(p.shape[0], full - at)
        plan.append((slot, at, rows))
        at += p.shape[0]
        if at == whole:
            slot, at = slot + 1, 0
    return tuple(plan), slot


def multiply(slots, plan, idx, pieces, weights, wd, buf, views, sems, sums):
    depth = buf.shape[2]
    order_of = [[] for _ in slots]
    pairs = []
    for i, k in enumerate(slots):
        for w, v in zip(weights, views):
            order_of[i].append(len(pairs))
            pairs.append((rows_of(w, idx, k, depth), v.at[i]))
        for ref, (slot, at, rows) in zip(pieces, plan):
            if slot == i:
                order_of[i].append(len(pairs))
                pairs.append((ref.at[pl.ds(0, rows)], buf.at[i, pl.ds(at, rows)]))
    copies = fetch(pairs, sems)
    for i, k in enumerate(slots):
        for c in order_of[i]:
            copies[c].wait()
        lhs = buf[i]
        parts = [dot(lhs, v[i]) for v in views]
        if wd is not None:
            parts.append(nt_dot(wd[:, pl.ds(pl.multiple_of(idx[k] * depth, depth), depth)], lhs))
        sums = [p if s is None else s + p for s, p in zip(sums, parts)]
    return sums


def step_sizes(v, bias):
    v = v[:SUB] + bias[:SUB]
    return jnp.maximum(v, 0.0) + jnp.log1p(jnp.exp(-jnp.abs(v)))


def project_kernel(slots, plan, last, idx, *refs):
    n = len(plan)
    pieces, refs = refs[:n], refs[n:]
    wx, wb, wd, bias = refs[:4]
    outs, (buf, vx, vb, sems) = refs[4:7], refs[7:]
    sums = multiply(slots, plan, idx, pieces, (wx, wb), wd, buf, (vx, vb), sems, [None] * 3)
    if last:
        outs[0][...] = sums[0].astype(BF16)
        outs[1][...] = sums[1].astype(BF16)
        outs[2][...] = step_sizes(sums[2], bias[...][:, 0:1])
    else:
        for o, s in zip(outs, sums):
            o[...] = s


def scratch_of(n, rows, depth, widths, copies):
    return (
        [pltpu.VMEM((n, rows, depth), BF16)]
        + [pltpu.VMEM((n, depth, w), BF16) for w in widths]
        + [pltpu.SemaphoreType.DMA((copies,))]
    )


def project(idx, slots, pieces, wx, wb, wd, bias, last):
    rows, depth = max(p.shape[0] for p in pieces), pieces[0].shape[1]
    plan, n = plan_of(pieces)
    nx, nb, nd = wx.shape[1], wb.shape[1], wd.shape[0]
    kind = BF16 if last else F32
    return pl.pallas_call(
        functools.partial(project_kernel, slots, plan, last),
        in_specs=[SMEM] + [ANY] * (len(pieces) + 2) + [VMEM, VMEM],
        out_specs=[VMEM] * 3,
        scratch_shapes=scratch_of(n, rows, depth, (nx, nb), 2 * n + len(pieces)),
        out_shape=[
            jax.ShapeDtypeStruct((rows, nx), kind),
            jax.ShapeDtypeStruct((rows, nb), kind),
            jax.ShapeDtypeStruct((SUB if last else nd, rows), F32),
        ],
        compiler_params=params(24),
        cost_estimate=pl.CostEstimate(
            flops=2 * rows * depth * n * (nx + nb + LANES),
            bytes_accessed=2 * depth * n * (rows + nx + nb),
            transcendentals=0,
        ),
        name="project",
    )(idx, *far(*pieces, wx, wb), wd, bias)


def gate_kernel(plan_a, plan_b, idx, *refs):
    na, nb = len(plan_a), len(plan_b)
    pieces_a, pieces_b, (wz, out, buf, vz, sems) = refs[:na], refs[na : na + nb], refs[na + nb :]
    half = out.shape[0] // 2
    n, depth = buf.shape[0], buf.shape[2]
    plan = [(s, at, r) for s, at, r in plan_a] + [(s, at + half, r) for s, at, r in plan_b]
    (total,) = multiply(
        tuple(range(n)), plan, idx, pieces_a + pieces_b, (wz,), None, buf, (vz,), sems, [None]
    )
    out[...] = silu(total.astype(BF16).astype(F32))


def gate_project(idx, pieces_a, pieces_b, wz):
    half, depth = pieces_a[0].shape
    nz = wz.shape[1]
    plan_a, n = plan_of(pieces_a)
    plan_b, _ = plan_of(pieces_b, half)
    count = len(plan_a) + len(plan_b)
    return pl.pallas_call(
        functools.partial(gate_kernel, plan_a, plan_b),
        in_specs=[SMEM] + [ANY] * (count + 1),
        out_specs=VMEM,
        scratch_shapes=scratch_of(n, 2 * half, depth, (nz,), n + count),
        out_shape=pltpu.HBM((2 * half, nz), F32),
        compiler_params=params(28),
        cost_estimate=pl.CostEstimate(
            flops=4 * half * depth * n * nz, bytes_accessed=2 * depth * n * (2 * half + nz), transcendentals=0
        ),
        name="gate",
    )(idx, *far(*pieces_a, *pieces_b, wz))


def order(strict=False):
    at = lax.broadcasted_iota(jnp.int32, (BLOCK, BLOCK), 0)
    to = lax.broadcasted_iota(jnp.int32, (BLOCK, BLOCK), 1)
    return at, to


def running(dt, rates):
    at, to = order()
    a = -dt * rates
    cf = jnp.dot(a, (at <= to).astype(F32), precision=lax.Precision.HIGHEST, preferred_element_type=F32)
    return cf, cf - a


def columns(*groups):
    zero = jnp.zeros((LANES - SUB * len(groups), BLOCK), F32)
    return jnp.concatenate([*groups, zero], axis=0).T


def equal(a, b):
    return (a == b).astype(F32)


def marks(segs):
    seg, prev, nxt = segs[0:1], segs[1:2], segs[2:3]
    return seg, prev, nxt, seg[:, :1], seg[:, BLOCK - 1 :], prev[:, :1], nxt[:, BLOCK - 1 :]


def spread(col, heads):
    return jnp.concatenate([jnp.broadcast_to(col[h : h + 1], (1, LANES)) for h in range(heads)], axis=1)


def weigh(values, weights, at, heads):
    return jnp.concatenate(
        [values[:, h * LANES : (h + 1) * LANES] * weights[:, at + h : at + h + 1] for h in range(heads)], axis=1
    )


def state_kernel(heads, slots, plan, idx, *refs):
    n = len(plan)
    pieces, refs = refs[:n], refs[n:]
    wx, wb, wd, bias, hx, hb, hd, xa, ba, da, kx, kb, segs, rates = refs[:14]
    xs, bcs, dts, pay, loc, dec = refs[14:20]
    buf, vx, vb, sems, xf, bf = refs[20:]
    half = xa.shape[0]
    blocks = 2 * half // BLOCK
    xf[8 : 8 + half] = xa[...].astype(F32)
    bf[8 : 8 + half] = ba[...].astype(F32)
    sums = multiply(slots, plan, idx, pieces, (wx, wb), wd, buf, (vx, vb), sems, [hx[...], hb[...], hd[...]])
    for dst, full in ((xf, sums[0]), (bf, sums[1])):
        full = full.astype(BF16).astype(F32)
        dst[8 + half : 8 + 2 * half] = full[:half]
        edge = full[half:]
        dst[7:8] = edge[SUB - 1 : SUB]
        dst[8 + 2 * half : 9 + 2 * half] = edge[SUB : SUB + 1]
    dts[:, :half] = da[...]
    dts[:, half:] = step_sizes(sums[2], bias[...][:, 0:1])[:, :half]
    rate = rates[...][:, 0:1]
    steps = []
    for b in range(blocks):
        at = b * BLOCK
        seg, prev, nxt, start, end, prev_end, next_start = marks(segs[:, at : at + BLOCK])
        dt = dts[:, at : at + BLOCK]
        cf, ce = running(dt, rate)
        last = cf[:, BLOCK - 1 :]
        wide = lambda row: jnp.broadcast_to(row, (SUB, BLOCK))
        col = columns(
            jnp.exp(last - cf) * dt * equal(seg, end),
            jnp.exp(ce) * dt * equal(seg, start),
            wide(equal(seg, prev)),
            wide(equal(seg, nxt)),
        )
        steps.append((jnp.exp(last) * equal(end, prev_end), jnp.exp(last) * equal(start, next_start)))
        same_prev, same_next = col[:, 2 * SUB : 2 * SUB + 1], col[:, 3 * SUB : 3 * SUB + 1]

        def conv(src, taps):
            base = 8 + at
            before = src[base - 1 : base - 1 + BLOCK] * same_prev
            after = src[base + 1 : base + 1 + BLOCK] * same_next
            return silu(taps[0:1] * before + taps[1:2] * src[base : base + BLOCK] + taps[2:3] * after)

        x_blk = conv(xf, kx).astype(BF16)
        bc_blk = conv(bf, kb).astype(BF16)
        xs[at : at + BLOCK] = x_blk
        bcs[at : at + BLOCK] = bc_blk
        x_f = x_blk.astype(F32)
        b_t = bc_blk[:, :LANES].astype(F32).T.astype(BF16)
        loc[0, b] = dot(b_t, weigh(x_f, col, 0, heads).astype(BF16))
        loc[1, b] = dot(b_t, weigh(x_f, col, SUB, heads).astype(BF16))
    for way in range(2):
        total = jnp.ones((SUB, 1), F32)
        state = jnp.zeros((loc.shape[2], loc.shape[3]), F32)
        for i in range(blocks):
            b = i if way == 0 else blocks - 1 - i
            fresh = loc[way, b]
            loc[way, b] = state
            dec[way, b : b + 1] = spread(total, heads)
            step = steps[b][way]
            state = spread(step, heads) * state + fresh
            total = total * step
        rows, width = state.shape
        pay[way * rows : (way + 1) * rows, :width] = state.astype(BF16)
        high = total[:heads].astype(BF16).astype(F32)
        both = jnp.concatenate([high, total[:heads] - high], axis=0)
        eight = jnp.broadcast_to(both, (2 * heads, LANES)).astype(BF16)
        pair = jnp.concatenate([eight, eight], axis=0)
        for j in range(rows // 16):
            pay[way * rows + 16 * j : way * rows + 16 * j + 16, width:] = pair


def states(heads, idx, slots, pieces, wx, wb, wd, bias, held, xa, ba, da, kx, kb, segs, rates):
    rows, part, depth = 2 * xa.shape[0], max(p.shape[0] for p in pieces), pieces[0].shape[1]
    nx, nb = wx.shape[1], wb.shape[1]
    blocks = rows // BLOCK
    plan, n = plan_of(pieces)
    return pl.pallas_call(
        functools.partial(state_kernel, heads, slots, plan),
        in_specs=[SMEM] + [ANY] * (len(pieces) + 2) + [VMEM] * 12,
        out_shape=[
            pltpu.HBM((rows, nx), BF16),
            pltpu.HBM((rows, nb), BF16),
            pltpu.HBM((SUB, rows), F32),
            pltpu.HBM((2 * LANES, nx + LANES), BF16),
            pltpu.HBM((2, blocks, LANES, nx), F32),
            pltpu.HBM((2, blocks, nx), F32),
        ],
        out_specs=[VMEM] * 6,
        scratch_shapes=scratch_of(n, part, depth, (nx, nb), 2 * n + len(pieces))
        + [pltpu.VMEM((rows + 16, nx), F32), pltpu.VMEM((rows + 16, nb), F32)],
        compiler_params=params(30),
        name="states",
    )(idx, *far(*pieces, wx, wb), wd, bias, *held, xa, ba, da, kx, kb, segs, rates)


def scan_kernel(heads, flag, src, out):
    count = src.shape[0]
    width = out.shape[2]
    ahead = flag[0] == 1

    def one(i, state):
        q = jnp.where(ahead, i, count - 1 - i)
        out[q] = state.astype(BF16)
        got = src[q].astype(F32)
        d = jnp.concatenate(
            [got[h : h + 1, width:] + got[heads + h : heads + h + 1, width:] for h in range(heads)], axis=1
        )
        return d * state + got[:, :width]

    lax.fori_loop(0, count, one, jnp.zeros((out.shape[1], width), F32), unroll=4)


def scan(heads, flag, src, width):
    return pl.pallas_call(
        functools.partial(scan_kernel, heads),
        in_specs=[pl.BlockSpec(memory_space=pltpu.SMEM), pl.BlockSpec(memory_space=pltpu.VMEM)],
        out_shape=jax.ShapeDtypeStruct((src.shape[0], src.shape[1], width), BF16),
        compiler_params=params(4),
        name="scan",
    )(flag, src)


def inside_kernel(heads, xs, bcs, dts, segs, rates, out):
    dt = dts[...]
    cf, ce = running(dt, rates[...][:, 0:1])
    row = segs[...]
    col = columns(cf, ce, row)
    bc = bcs[...]
    scores = nt_dot(bc[:, LANES:], bc[:, :LANES])
    scores = jnp.where(col[:, 2 * SUB : 2 * SUB + 1] == row[0:1], scores, 0.0)
    at, to = order()
    lower = to <= at
    x = xs[...]
    for h in range(heads):
        gap = jnp.where(lower, col[:, h : h + 1] - cf[h : h + 1], ce[h : h + 1] - col[:, SUB + h : SUB + h + 1])
        w = (scores * jnp.exp(gap) * dt[h : h + 1]).astype(BF16)
        out[:, h * LANES : (h + 1) * LANES] = dot(w, x[:, h * LANES : (h + 1) * LANES])


def row_block(width):
    return pl.BlockSpec((BLOCK, width), lambda b: (b, 0))


LANE_BLOCK = pl.BlockSpec((SUB, BLOCK), lambda b: (0, b))
RATE_BLOCK = pl.BlockSpec((SUB, LANES), lambda b: (0, 0))


def inside(heads, xs, bcs, dts, segs, rates):
    rows, nx = xs.shape
    nb = bcs.shape[1]
    return pl.pallas_call(
        functools.partial(inside_kernel, heads),
        grid=(rows // BLOCK,),
        in_specs=[row_block(nx), row_block(nb), LANE_BLOCK, LANE_BLOCK, RATE_BLOCK],
        out_specs=row_block(nx),
        out_shape=pltpu.HBM((rows, nx), F32),
        compiler_params=params(8),
        cost_estimate=pl.CostEstimate(
            flops=2 * rows * BLOCK * (nx + LANES), bytes_accessed=rows * nx * 6, transcendentals=rows * BLOCK * heads
        ),
        name="inside",
    )(*far(xs, bcs, dts), segs, rates)


def finish_kernel(heads, enter, loc, dec, y_in, sg, bcs, dts, segs, rates, out, ss):
    b = pl.program_id(0)
    cf, ce = running(dts[...], rates[...][:, 0:1])
    seg, prev, nxt, start, end, prev_end, next_start = marks(segs[...])
    col = columns(
        jnp.exp(cf) * equal(seg, prev_end), jnp.exp(cf[:, BLOCK - 1 :] - ce) * equal(seg, next_start)
    )
    c = bcs[...][:, LANES:]
    y = y_in[...]
    for way in range(2):
        held = dec[way, b][None] * enter[way * LANES : (way + 1) * LANES].astype(F32) + loc[way, 0]
        y = y + weigh(dot(c, held.astype(BF16)), col, way * SUB, heads)
    gated = y * sg[...]
    out[...] = gated
    sq = gated * gated
    part = sq[:, :LANES]
    for h in range(1, heads):
        part = part + sq[:, h * LANES : (h + 1) * LANES]
    ss[0] = jnp.sum(part.T, axis=0, keepdims=True)


def finish(heads, enter, loc, dec, y_in, sg, bcs, dts, segs, rates):
    rows, nx = y_in.shape
    nb = bcs.shape[1]
    blocks = rows // BLOCK
    return pl.pallas_call(
        functools.partial(finish_kernel, heads),
        grid=(blocks,),
        in_specs=[
            pl.BlockSpec(enter.shape, lambda b: (0, 0)),
            pl.BlockSpec((2, 1, LANES, nx), lambda b: (0, b, 0, 0)),
            pl.BlockSpec(dec.shape, lambda b: (0, 0, 0)),
            row_block(nx),
            row_block(nx),
            row_block(nb),
            LANE_BLOCK,
            LANE_BLOCK,
            RATE_BLOCK,
        ],
        out_specs=[row_block(nx), pl.BlockSpec((1, 1, BLOCK), lambda b: (b, 0, 0))],
        out_shape=[jax.ShapeDtypeStruct((rows, nx), F32), jax.ShapeDtypeStruct((blocks, 1, BLOCK), F32)],
        compiler_params=params(12),
        name="finish",
    )(enter, *far(loc, dec, y_in, sg, bcs, dts), segs, rates)


def scale_kernel(columns, gated, gain, *refs):
    parts, out = refs[:-1], refs[-1]
    total = parts[0][0]
    for p in parts[1:]:
        total = total + p[0]
    scale = lax.rsqrt(total / columns + 1e-05)
    col = jnp.broadcast_to(scale, (LANES, BLOCK)).T[:, 0:1]
    out[...] = (gated[...] * col * gain[...]).astype(BF16)


def scale(columns, gated, gain, parts):
    rows, nx = gated.shape
    row = pl.BlockSpec((BLOCK, nx), lambda b: (b, 0))
    part = pl.BlockSpec((1, 1, BLOCK), lambda b: (b, 0, 0))
    return pl.pallas_call(
        functools.partial(scale_kernel, columns),
        grid=(rows // BLOCK,),
        in_specs=[row, pl.BlockSpec((1, nx), lambda b: (0, 0))] + [part] * len(parts),
        out_specs=row,
        out_shape=jax.ShapeDtypeStruct((rows, nx), BF16),
        compiler_params=params(8),
        name="scale",
    )(gated, gain, *parts)


def tie(value, *after):
    return lax.optimization_barrier((value, *after))[0]


def shards(tokens, segment_ids, w_x, w_z, w_bc, w_dt, dt_bias, rates, conv_x, conv_bc, norm_gain):
    rows, depth = tokens.shape
    heads = w_dt.shape[1]
    nx = w_x.shape[1]
    mp, seq = lax.axis_size("mp"), lax.axis_size("seq")
    ring = mp // 2
    me = lax.axis_index("mp")
    row_at, col_at = me // ring, me % ring
    turn = lambda s: [(r * ring + c, r * ring + (c + s) % ring) for r in range(2) for c in range(ring)]
    send = lambda v, pairs: lax.ppermute(v, "mp", pairs)
    right, left = turn(1), turn(-1)
    across = [(i, (i + ring) % mp) for i in range(mp)]
    half = rows // 2

    def spread_out(own):
        cut = half // 2
        r1, l1, p = send(own, right), send(own, left), send(own, across)
        o1, o2 = send(r1[:cut], right), send(l1[cut:], left)
        pr, pm = send(p, right), send(p, left)
        return [own, r1, l1, p, o1, o2, pr, pm, send(o1, across), send(o2, across)]

    pieces_a = spread_out(tokens[:half])

    seg = segment_ids.astype(F32) + 1.0
    label = lambda v: jnp.broadcast_to(v[:, None], (SUB, LANES)).astype(BF16)
    tail = jnp.concatenate([tokens[rows - SUB :], label(seg[rows - SUB :])], axis=1)
    head = jnp.concatenate([tokens[:SUB], label(seg[:SUB])], axis=1)
    before = lax.ppermute(tail, "seq", [(i, i + 1) for i in range(seq - 1)])
    after = lax.ppermute(head, "seq", [(i + 1, i) for i in range(seq - 1)])
    left_seg = before[SUB - 1, depth].astype(F32)
    right_seg = after[0, depth].astype(F32)

    pieces_b = spread_out(jnp.concatenate([tokens[half:], before[:, :depth], after[:, :depth]], axis=0))
    idx = jnp.stack(
        [r * ring + (col_at + s) % ring for r, s in (
            (row_at, 0), (row_at, -1), (row_at, 1), (1 - row_at, 0),
            (row_at, 2), (1 - row_at, -1), (1 - row_at, 1), (1 - row_at, 2))]
    ).astype(jnp.int32)

    joined = jnp.concatenate([left_seg[None], seg, right_seg[None]])
    segs = jnp.stack([joined[1:-1], joined[:-2], joined[2:]] + [seg] * (SUB - 3))
    tall = lambda v, n: jnp.broadcast_to(jnp.pad(v, (0, n - heads))[:, None], (n, LANES))
    rate, bias = tall(rates, SUB), tall(dt_bias, 16)
    w_d = jnp.pad(w_dt.T, ((0, 16 - heads), (0, 0)))

    xa, ba, da = project(idx, tuple(range(8)), pieces_a, w_x, w_bc, w_d, bias, True)
    held = project(idx, (0, 1, 2, 3), pieces_b[:4], w_x, w_bc, w_d, bias, False)
    xs, bcs, dts, pay, loc, dec = states(
        heads, idx, (4, 5, 6, 7), pieces_b[4:], w_x, w_bc, w_d, bias, held, xa, ba, da, conv_x, conv_bc, segs, rate
    )

    width = nx
    got = lax.all_to_all(pay.reshape(seq, 2 * LANES // seq, width + LANES), "seq", 0, 0)
    flag = (lax.axis_index("seq") < seq // 2).astype(jnp.int32)[None]
    y_in = inside(heads, xs, bcs, dts, segs, rate)
    got, y_in = lax.optimization_barrier((got, y_in))
    entered = scan(heads, flag, got, width)
    enter = lax.all_to_all(entered, "seq", 0, 0).reshape(2 * LANES, width)
    sg = gate_project(idx, pieces_a, pieces_b, w_z)

    gated, ss = finish(heads, enter, loc, dec, y_in, sg, bcs, dts, segs, rate)
    ss = ss + send(ss, across)
    parts = [ss] + [send(ss, turn(s)) for s in range(1, ring)]
    return scale(nx * mp, gated, norm_gain[None], parts)


def solution(mesh):
    placed = (
        P("seq", "mp"),
        P("seq"),
        P(None, "mp"),
        P(None, "mp"),
        P(),
        P(None, "mp"),
        P("mp"),
        P("mp"),
        P(None, "mp"),
        P(),
        P("mp"),
    )
    return jax.shard_map(
        shards, mesh=mesh, in_specs=placed, out_specs=P("seq", "mp"), check_vma=False
    )
```

time: 191 us -> 150 us (0.79)
  local copies, waits for them, and re-layouts: 36.3 us -> 4.37 us
  Pallas kernels: 57.4 us -> 48.9 us
  other arithmetic: 5.66 us -> 0.14 us
  waiting for transfers between devices: 31.6 us -> 34.2 us
    unnamed x92 -> x38, local copies, waits for them, and re-layouts: 20.7 us -> 0.73 us
    pallas_call x5 -> x4, Pallas kernels: 44.6 us -> 33.9 us  [the longest x2 12.7 us: project(): pl.pallas_call(functools.partial(project_kernel, slots, plan, last), in_s...]
    ppermute x22, starting transfers between devices: 34.2 us -> 38.8 us  [shards(): send = lambda v, pairs: lax.ppermute(v, 'mp', pairs)]
    slice x11 -> x8, local copies, waits for them, and re-layouts: 7.16 us -> 2.66 us  [the longest x1 1.28 us: shards(): pieces_a = spread_out(tokens[:half])]
    all_to_all x1 -> x0, starting transfers between devices: 3.79 us -> none  [shards(): lax.all_to_all(jnp.broadcast_to(edge[None], (mp, HALO, depth)), 'mp', 0, 0)]
    all_to_all x1, waiting for transfers between devices: 0.01 us -> 3.26 us  [shards(): enter = lax.all_to_all(entered, 'seq', 0, 0).reshape(2 * LANES, width)]
    another operation x2 -> x0, other arithmetic: 2.67 us -> none  [the longest x1 1.39 us: shards(): jnp.stack([(seg == prev).astype(F32), (seg == nxt).astype(F32), (seg == w...]
    pad x1 -> x3, local copies, waits for them, and re-layouts: 2.43 us -> 0.02 us  [the longest x1 0.02 us: shards(): w_d = jnp.pad(w_dt.T, ((0, 16 - heads), (0, 0)))]
  transfers between devices with their start and end apart: 27 -> 26, of which waited for: 8 -> 12; matrix products, arithmetic and copies ran while one was open for 13% -> 2% of each run, Pallas kernels for 16% -> 19%
where the time goes in v2:
time: 150 us; the launch traced here: 148 us
  starting transfers between devices  58.7 us (39%)
  Pallas kernels  48.9 us (33%)
  waiting for transfers between devices  34.2 us (23%)
  local copies, waits for them, and re-layouts  4.37 us (3%)
  between operations  1.66 us (1%)
    ppermute x22, starting transfers between devices, shards(): send = lambda v, pairs: lax.ppermute(v, 'mp', pairs)  38.8 us
    ppermute x22, waiting for transfers between devices, shards(): send = lambda v, pairs: lax.ppermute(v, 'mp', pairs)  23.7 us
    pallas_call x2, Pallas kernels, project(): pl.pallas_call(functools.partial(project_kernel, slots, plan, last), in_s...  12.7 us
    pallas_call x1, Pallas kernels, states(): pl.pallas_call(functools.partial(state_kernel, heads, slots, plan), in_sp...  12.3 us
    all_to_all x1, starting transfers between devices, shards(): lax.all_to_all(pay.reshape(seq, 2 * LANES // seq, width + LANES), 'seq',...  10.2 us
    pallas_call x1, Pallas kernels, gate_project(): pl.pallas_call(functools.partial(gate_kernel, plan_a, plan_b), in_specs=[...  8.89 us
    all_to_all x1, waiting for transfers between devices, shards(): lax.all_to_all(pay.reshape(seq, 2 * LANES // seq, width + LANES), 'seq',...  7.21 us
    pallas_call x1, Pallas kernels, inside(): pl.pallas_call(functools.partial(inside_kernel, heads), grid=(rows // BLO...  6.28 us
  transfers between devices with their start and end apart: 26, of which 12 were waited for; matrix products, arithmetic and copies ran while one was open for 2% of the time, Pallas kernels for 19%

profile of v2, /device:TPU:8, one launch (start us, length us, event | category | flops | bytes accessed | tf_op | source)
XLA Modules:
  0.0 148.0 jit_solution(7016419412781044778)
XLA Ops:
  1.3 1.6 %collective-permute-start.11 = (bf16[512,512]{1,0:T(8,128)(2,1)S(1)}, bf16[512,512]{1,0:T(8,128)(2,1)S(1)}, u32[]{:S(2)}, u32[]{:S(2)}) collective-permute-start(bf16[512,512]{1,0:T(8,128)(2,1)S(1)} %get-tuple-element.37.refs_0_), channel_id=1, source_target_pairs={{0,1},{1,2},{2,3},{3,0},{4,5},{5,6},{6,7},{7,4},{8,9},{9,10},{10,1... | collective-permute-start | bytes 1572872 | tf_op jit(solution)/shard_map/ppermute | solution.py:464
  3.8 1.9 %collective-permute-start = (bf16[8,640]{1,0:T(8,128)(2,1)S(1)}, bf16[8,640]{1,0:T(8,128)(2,1)S(1)}, u32[]{:S(2)}, u32[]{:S(2)}) collective-permute-start(bf16[8,640]{1,0:T(8,128)(2,1)S(1)} %pad_maximum_fusion.1), channel_id=1, source_target_pairs={{0,8},{8,16},{16,24},{24,32},{32,40},{40,48},{48,56},{56,64},{64,7... | collective-permute-start | bytes 30728 | tf_op jit(solution)/shard_map/ppermute | solution.py:482
  5.8 3.6 %collective-permute-start.1 = (bf16[8,640]{1,0:T(8,128)(2,1)S(1)}, bf16[8,640]{1,0:T(8,128)(2,1)S(1)}, u32[]{:S(2)}, u32[]{:S(2)}) collective-permute-start(bf16[8,640]{1,0:T(8,128)(2,1)S(1)} %pad_maximum_fusion.2), channel_id=1, source_target_pairs={{8,0},{16,8},{24,16},{32,24},{40,32},{48,40},{56,48},{64,56},{72,6... | collective-permute-start | bytes 30728 | tf_op jit(solution)/shard_map/ppermute | solution.py:483
  9.4 1.8 %collective-permute-start.12 = (bf16[512,512]{1,0:T(8,128)(2,1)S(1)}, bf16[512,512]{1,0:T(8,128)(2,1)S(1)}, u32[]{:S(2)}, u32[]{:S(2)}) collective-permute-start(bf16[512,512]{1,0:T(8,128)(2,1)S(1)} %get-tuple-element.37.refs_0_), channel_id=1, source_target_pairs={{0,3},{1,0},{2,1},{3,2},{4,7},{5,4},{6,5},{7,6},{8,11},{9,8},{10,9... | collective-permute-start | bytes 1572872 | tf_op jit(solution)/shard_map/ppermute | solution.py:464
  11.3 1.6 %collective-permute-start.4 = (bf16[528,512]{1,0:T(8,128)(2,1)S(1)}, bf16[528,512]{1,0:T(8,128)(2,1)S(1)}, u32[]{:S(2)}, u32[]{:S(2)}) collective-permute-start(bf16[528,512]{1,0:T(8,128)(2,1)S(1)} %pad_maximum_fusion.refs_0_.refs_10_), channel_id=1, source_target_pairs={{0,3},{1,0},{2,1},{3,2},{4,7},{5,4},{6,5},{7,6},{8,11},{9,8},{10,9... | collective-permute-start | bytes 1622024 | tf_op jit(solution)/shard_map/ppermute | solution.py:464
  13.4 2.3 %collective-permute-start.13 = (bf16[512,512]{1,0:T(8,128)(2,1)S(1)}, bf16[512,512]{1,0:T(8,128)(2,1)}, u32[]{:S(2)}, u32[]{:S(2)}) collective-permute-start(bf16[512,512]{1,0:T(8,128)(2,1)S(1)} %get-tuple-element.37.refs_0_), channel_id=1, source_target_pairs={{0,4},{1,5},{2,6},{3,7},{4,0},{5,1},{6,2},{7,3},{8,12},{9,13},{10,... | collective-permute-start | bytes 1572872 | tf_op jit(solution)/shard_map/ppermute | solution.py:464
  16.3 2.3 %collective-permute-start.6 = (bf16[528,512]{1,0:T(8,128)(2,1)S(1)}, bf16[528,512]{1,0:T(8,128)(2,1)S(1)}, u32[]{:S(2)}, u32[]{:S(2)}) collective-permute-start(bf16[528,512]{1,0:T(8,128)(2,1)S(1)} %pad_maximum_fusion.refs_0_.refs_10_), channel_id=1, source_target_pairs={{0,4},{1,5},{2,6},{3,7},{4,0},{5,1},{6,2},{7,3},{8,12},{9,13},{10,... | collective-permute-start | bytes 1622024 | tf_op jit(solution)/shard_map/ppermute | solution.py:464
  18.6 5.7 %collective-permute-done.12.refs_2_ = bf16[512,512]{1,0:T(8,128)(2,1)S(1)} collective-permute-done((bf16[512,512]{1,0:T(8,128)(2,1)S(1)}, bf16[512,512]{1,0:T(8,128)(2,1)S(1)}, u32[]{:S(2)}, u32[]{:S(2)}) %collective-permute-start.12) | collective-permute-done | bytes 524320 | tf_op jit(solution)/shard_map/ppermute | solution.py:464
  25.8 9.3 %collective-permute-done.4.refs_2_.refs_12_ = bf16[528,512]{1,0:T(8,128)(2,1)S(1)} collective-permute-done((bf16[528,512]{1,0:T(8,128)(2,1)S(1)}, bf16[528,512]{1,0:T(8,128)(2,1)S(1)}, u32[]{:S(2)}, u32[]{:S(2)}) %collective-permute-start.4) | collective-permute-done | bytes 540704 | tf_op jit(solution)/shard_map/ppermute | solution.py:464
  35.1 3.0 %collective-permute-start.15 = (bf16[256,512]{1,0:T(8,128)(2,1)S(1)}, bf16[256,512]{1,0:T(8,128)(2,1)}, u32[]{:S(2)}, u32[]{:S(2)}) collective-permute-start(bf16[256,512]{1,0:T(8,128)(2,1)S(1)} %slice.73), channel_id=1, source_target_pairs={{0,3},{1,0},{2,1},{3,2},{4,7},{5,4},{6,5},{7,6},{8,11},{9,8},{10,9... | collective-permute-start | bytes 786440 | tf_op jit(solution)/shard_map/ppermute | solution.py:464
  38.5 1.8 %collective-permute-start.3 = (bf16[256,512]{1,0:T(8,128)(2,1)S(1)}, bf16[256,512]{1,0:T(8,128)(2,1)}, u32[]{:S(2)}, u32[]{:S(2)}) collective-permute-start(bf16[256,512]{1,0:T(8,128)(2,1)S(1)} %slice.70), channel_id=1, source_target_pairs={{0,1},{1,2},{2,3},{3,0},{4,5},{5,6},{6,7},{7,4},{8,9},{9,10},{10,1... | collective-permute-start | bytes 786440 | tf_op jit(solution)/shard_map/ppermute | solution.py:464
  40.3 2.6 %collective-permute-start.18 = (bf16[256,512]{1,0:T(8,128)(2,1)}, bf16[256,512]{1,0:T(8,128)(2,1)}, u32[]{:S(2)}, u32[]{:S(2)}) collective-permute-start(bf16[256,512]{1,0:T(8,128)(2,1)} %collective-permute-done.14.refs_4_), channel_id=1, source_target_pairs={{0,4},{1,5},{2,6},{3,7},{4,0},{5,1},{6,2},{7,3},{8,12},{9,13},{10,... | collective-permute-start | bytes 786440 | tf_op jit(solution)/shard_map/ppermute | solution.py:464
  43.1 1.7 %collective-permute-done.15.refs_5_ = bf16[256,512]{1,0:T(8,128)(2,1)} collective-permute-done((bf16[256,512]{1,0:T(8,128)(2,1)S(1)}, bf16[256,512]{1,0:T(8,128)(2,1)}, u32[]{:S(2)}, u32[]{:S(2)}) %collective-permute-start.15) | collective-permute-done | bytes 262176 | tf_op jit(solution)/shard_map/ppermute | solution.py:464
  44.8 3.8 %collective-permute-start.17 = (bf16[512,512]{1,0:T(8,128)(2,1)}, bf16[512,512]{1,0:T(8,128)(2,1)}, u32[]{:S(2)}, u32[]{:S(2)}) collective-permute-start(bf16[512,512]{1,0:T(8,128)(2,1)} %collective-permute-done.13.refs_3_), channel_id=1, source_target_pairs={{0,3},{1,0},{2,1},{3,2},{4,7},{5,4},{6,5},{7,6},{8,11},{9,8},{10,9... | collective-permute-start | bytes 1572872 | tf_op jit(solution)/shard_map/ppermute | solution.py:464
  51.2 3.2 %collective-permute-start.8 = (bf16[528,512]{1,0:T(8,128)(2,1)S(1)}, bf16[528,512]{1,0:T(8,128)(2,1)}, u32[]{:S(2)}, u32[]{:S(2)}) collective-permute-start(bf16[528,512]{1,0:T(8,128)(2,1)S(1)} %collective-permute-done.6.refs_3_.refs_13_), channel_id=1, source_target_pairs={{0,3},{1,0},{2,1},{3,2},{4,7},{5,4},{6,5},{7,6},{8,11},{9,8},{10,9... | collective-permute-start | bytes 1622024 | tf_op jit(solution)/shard_map/ppermute | solution.py:464
  54.5 2.6 %collective-permute-start.19 = (bf16[256,512]{1,0:T(8,128)(2,1)}, bf16[256,512]{1,0:T(8,128)(2,1)S(1)}, u32[]{:S(2)}, u32[]{:S(2)}) collective-permute-start(bf16[256,512]{1,0:T(8,128)(2,1)} %collective-permute-done.15.refs_5_), channel_id=1, source_target_pairs={{0,4},{1,5},{2,6},{3,7},{4,0},{5,1},{6,2},{7,3},{8,12},{9,13},{10,... | collective-permute-start | bytes 786440 | tf_op jit(solution)/shard_map/ppermute | solution.py:464
  57.3 5.0 %project.2 = (f32[528,512]{1,0:T(8,128)S(1)}, f32[528,256]{1,0:T(8,128)S(1)}, f32[16,528]{1,0:T(8,128)S(1)}) custom-call(s32[8]{0:T(128)S(1)} %stack.52.idx, bf16[528,512]{1,0:T(8,128)(2,1)} %copy-done.3, bf16[528,512]{1,0:T(8,128)(2,1)} %copy-done.5, bf16[528,512]{1,0:T(8,128)(2,1)} %copy-done.4, bf16[528,512]{1,0:T(8,128)(2,1)} %copy-done.6, ...), custom_call_target="tpu_custom_call" | custom-call | flops 1937768448 | bytes 5308416 | tf_op jit(solution)/shard_map/project/pallas_call | solution.py:126
  62.6 2.6 %collective-permute-start.9 = (bf16[256,512]{1,0:T(8,128)(2,1)}, bf16[256,512]{1,0:T(8,128)(2,1)S(1)}, u32[]{:S(2)}, u32[]{:S(2)}) collective-permute-start(bf16[256,512]{1,0:T(8,128)(2,1)} %collective-permute-done.3.refs_0_.refs_14_), channel_id=1, source_target_pairs={{0,4},{1,5},{2,6},{3,7},{4,0},{5,1},{6,2},{7,3},{8,12},{9,13},{10,... | collective-permute-start | bytes 786440 | tf_op jit(solution)/shard_map/ppermute | solution.py:464
  66.1 7.7 %project.3 = (bf16[512,512]{1,0:T(8,128)(2,1)S(1)}, bf16[512,256]{1,0:T(8,128)(2,1)S(1)}, f32[8,512]{1,0:T(8,128)S(1)}) custom-call(s32[8]{0:T(128)S(1)} %stack.52.idx, bf16[512,512]{1,0:T(8,128)(2,1)} %copy-done.8, bf16[512,512]{1,0:T(8,128)(2,1)} %copy-done.12, bf16[512,512]{1,0:T(8,128)(2,1)} %copy-done.13, ...), custom_call_target="tpu_custom_call" | custom-call | flops 3758096384 | bytes 10485760 | tf_op jit(solution)/shard_map/project/pallas_call | solution.py:126
  76.0 12.3 %states.1 = (bf16[1024,512]{1,0:T(8,128)(2,1)}, bf16[1024,256]{1,0:T(8,128)(2,1)}, f32[8,1024]{1,0:T(8,128)}, bf16[256,640]{1,0:T(8,128)(2,1)}, f32[2,4,128,512]{3,2,1,0:T(8,128)}, /*index=5*/f32[2,4,512]{2,1,0:T(4,128)}) custom-call(s32[8]{0:T(128)S(1)} %stack.52.idx, bf16[256,512]{1,0:T(8,128)(2,1)} %collective-permute-done.3.refs_0_.refs_14_, ...), custom_call_target="tpu_custom_call" | custom-call | tf_op jit(solution)/shard_map/states/pallas_call | solution.py:292
  88.3 10.2 %all-to-all-start = ((bf16[32,8,640]{2,1,0:T(8,128)(2,1)}), bf16[32,8,640]{2,1,0:T(8,128)(2,1)S(1)}, u32[]{:S(2)}, u32[]{:S(2)}) async-start(bf16[32,8,640]{2,1,0:T(8,128)(2,1)} %bitcast.22), calls=%async_computation | async-start | bytes 655360 | tf_op jit(solution)/shard_map/all_to_all | solution.py:507
  98.5 6.3 %inside.1.y_in = f32[1024,512]{1,0:T(8,128)} custom-call(bf16[1024,512]{1,0:T(8,128)(2,1)} %get-tuple-element.28.xs, bf16[1024,256]{1,0:T(8,128)(2,1)} %get-tuple-element.29.bcs, f32[8,1024]{1,0:T(8,128)} %get-tuple-element.30.dts, f32[8,1024]{1,0:T(8,128)S(1)} %stack.56.refs_18_.segs, f32[8,128]{1,0:T(8,128)S(1)} %broadcast_in_dim.53.refs_19_.rates), custom_call_target="tpu_custom_call" | custom-call | flops 335544320 | bytes 3145728 | tf_op jit(solution)/shard_map/inside/pallas_call | solution.py:366
  104.8 7.2 %all-to-all-done.src = bf16[32,8,640]{2,1,0:T(8,128)(2,1)S(1)} async-done(((bf16[32,8,640]{2,1,0:T(8,128)(2,1)}), bf16[32,8,640]{2,1,0:T(8,128)(2,1)S(1)}, u32[]{:S(2)}, u32[]{:S(2)}) %all-to-all-start) | async-done | bytes 327712 | tf_op jit(solution)/shard_map/all_to_all | solution.py:507
  112.8 4.1 %all-to-all-start.1 = ((bf16[32,8,512]{2,1,0:T(8,128)(2,1)}), bf16[32,8,512]{2,1,0:T(8,128)(2,1)S(1)}, u32[]{:S(2)}, u32[]{:S(2)}) async-start(bf16[32,8,512]{2,1,0:T(8,128)(2,1)} %scan.1), calls=%async_computation.1 | async-start | bytes 524288 | tf_op jit(solution)/shard_map/all_to_all | solution.py:512
  116.9 8.9 %gate.1.sg = f32[1024,512]{1,0:T(8,128)} custom-call(s32[8]{0:T(128)S(1)} %stack.52.idx, bf16[512,512]{1,0:T(8,128)(2,1)} %copy-done.8, bf16[512,512]{1,0:T(8,128)(2,1)} %copy-done.12, bf16[512,512]{1,0:T(8,128)(2,1)} %copy-done.13, bf16[512,512]{1,0:T(8,128)(2,1)} %collective-permute-done.13.refs_3_, bf16[256,512]{1,0:T(8,128)(2,1)} %collective-permute-done.14.refs_4_, ...), custom_call_target="tpu_custom_call" | custom-call | flops 4294967296 | bytes 12582912 | tf_op jit(solution)/shard_map/gate/pallas_call | solution.py:164
  125.9 3.3 %all-to-all-done.1 = bf16[32,8,512]{2,1,0:T(8,128)(2,1)S(1)} async-done(((bf16[32,8,512]{2,1,0:T(8,128)(2,1)}), bf16[32,8,512]{2,1,0:T(8,128)(2,1)S(1)}, u32[]{:S(2)}, u32[]{:S(2)}) %all-to-all-start.1) | async-done | bytes 262176 | tf_op jit(solution)/shard_map/all_to_all | solution.py:512
  129.1 5.9 %finish.1 = (f32[1024,512]{1,0:T(8,128)S(1)}, f32[4,1,256]{2,1,0:T(1,128)S(1)}) custom-call(bf16[256,512]{1,0:T(8,128)(2,1)S(1)} %bitcast.20, f32[2,4,128,512]{3,2,1,0:T(8,128)} %get-tuple-element.32.loc, f32[2,4,512]{2,1,0:T(4,128)} %get-tuple-element.33.dec, f32[1024,512]{1,0:T(8,128)} %inside.1.y_in, f32[1024,512]{1,0:T(8,128)} %gate.1.sg, ...), custom_call_target="tpu_custom_call" | custom-call | tf_op jit(solution)/shard_map/finish/pallas_call | solution.py:405
  135.0 2.9 %collective-permute-start.20 = (f32[4,1,256]{2,1,0:T(1,128)S(1)}, f32[4,1,256]{2,1,0:T(1,128)S(1)}, u32[]{:S(2)}, u32[]{:S(2)}) collective-permute-start(f32[4,1,256]{2,1,0:T(1,128)S(1)} %get-tuple-element.36), channel_id=1, source_target_pairs={{0,4},{1,5},{2,6},{3,7},{4,0},{5,1},{6,2},{7,3},{8,12},{9,13},{10,... | collective-permute-start | bytes 12296 | tf_op jit(solution)/shard_map/ppermute | solution.py:464
  137.9 2.3 %collective-permute-done.20 = f32[4,1,256]{2,1,0:T(1,128)S(1)} collective-permute-done((f32[4,1,256]{2,1,0:T(1,128)S(1)}, f32[4,1,256]{2,1,0:T(1,128)S(1)}, u32[]{:S(2)}, u32[]{:S(2)}) %collective-permute-start.20) | collective-permute-done | bytes 4128 | tf_op jit(solution)/shard_map/ppermute | solution.py:464
  140.3 1.9 %collective-permute-start.22 = (f32[4,1,256]{2,1,0:T(1,128)S(1)}, f32[4,1,256]{2,1,0:T(1,128)S(1)}, u32[]{:S(2)}, u32[]{:S(2)}) collective-permute-start(f32[4,1,256]{2,1,0:T(1,128)S(1)} %add.90.refs_0_), channel_id=1, source_target_pairs={{0,2},{1,3},{2,0},{3,1},{4,6},{5,7},{6,4},{7,5},{8,10},{9,11},{10,... | collective-permute-start | bytes 12296 | tf_op jit(solution)/shard_map/ppermute | solution.py:464
  143.5 1.6 %collective-permute-done.21.refs_1_ = f32[4,1,256]{2,1,0:T(1,128)S(1)} collective-permute-done((f32[4,1,256]{2,1,0:T(1,128)S(1)}, f32[4,1,256]{2,1,0:T(1,128)S(1)}, u32[]{:S(2)}, u32[]{:S(2)}) %collective-permute-start.21) | collective-permute-done | bytes 4128 | tf_op jit(solution)/shard_map/ppermute | solution.py:464
  146.0 2.0 %scale.1 = bf16[1024,512]{1,0:T(8,128)(2,1)} custom-call(f32[1024,512]{1,0:T(8,128)S(1)} %get-tuple-element.35.gated, f32[1,512]{1,0:T(1,128)S(1)} %bitcast.21, f32[4,1,256]{2,1,0:T(1,128)S(1)} %add.90.refs_0_, f32[4,1,256]{2,1,0:T(1,128)S(1)} %collective-permute-done.21.refs_1_, f32[4,1,256]{2,1,0:T(1,128)S(1)} %collective-permute-done.22.refs_2_, ...), custom_call_target="tpu_custom_call" | custom-call | tf_op jit(solution)/shard_map/scale/pallas_call | solution.py:440
  (92 shorter events, 13.5 us)
Async XLA Ops:
  1.3 41.6 %copy-start.8 = (bf16[512,512]{1,0:T(8,128)(2,1)}, bf16[512,512]{1,0:T(8,128)(2,1)S(1)}, u32[]{:S(2)}) copy-start(bf16[512,512]{1,0:T(8,128)(2,1)S(1)} %get-tuple-element.37.refs_0_) | copy-start | bytes 1572868
  1.3 47.3 %copy-start.17 = (f32[4]{0:T(128)S(1)}, f32[4]{0:T(128)}, u32[]{:S(2)}) copy-start(f32[4]{0:T(128)} %param.17) | copy-start | bytes 52
  1.3 47.3 %copy-start.18 = (f32[4]{0:T(128)S(1)}, f32[4]{0:T(128)}, u32[]{:S(2)}) copy-start(f32[4]{0:T(128)} %param.18) | copy-start | bytes 52
  1.3 47.3 %copy-start.14 = (bf16[4096,4]{0,1:T(4,128)(2,1)S(1)}, bf16[4096,4]{0,1:T(4,128)(2,1)}, u32[]{:S(2)}) copy-start(bf16[4096,4]{0,1:T(4,128)(2,1)} %param.16) | copy-start | bytes 98308
  1.3 15.0 %collective-permute-start.11 = (bf16[512,512]{1,0:T(8,128)(2,1)S(1)}, bf16[512,512]{1,0:T(8,128)(2,1)S(1)}, u32[]{:S(2)}, u32[]{:S(2)}) collective-permute-start(bf16[512,512]{1,0:T(8,128)(2,1)S(1)} %get-tuple-element.37.refs_0_), channel_id=1, source_target_pairs={{0,1},{1,2},{2,3},{3,0},{4,5},{5,6},{6,7},{7,4},{8,9},{9,10},{10,1... | collective-permute-start | bytes 1572872 | tf_op jit(solution)/shard_map/ppermute | solution.py:464
  3.8 7.5 %collective-permute-start = (bf16[8,640]{1,0:T(8,128)(2,1)S(1)}, bf16[8,640]{1,0:T(8,128)(2,1)S(1)}, u32[]{:S(2)}, u32[]{:S(2)}) collective-permute-start(bf16[8,640]{1,0:T(8,128)(2,1)S(1)} %pad_maximum_fusion.1), channel_id=1, source_target_pairs={{0,8},{8,16},{16,24},{24,32},{32,40},{40,48},{48,56},{56,64},{64,7... | collective-permute-start | bytes 30728 | tf_op jit(solution)/shard_map/ppermute | solution.py:482
  5.8 5.5 %collective-permute-start.1 = (bf16[8,640]{1,0:T(8,128)(2,1)S(1)}, bf16[8,640]{1,0:T(8,128)(2,1)S(1)}, u32[]{:S(2)}, u32[]{:S(2)}) collective-permute-start(bf16[8,640]{1,0:T(8,128)(2,1)S(1)} %pad_maximum_fusion.2), channel_id=1, source_target_pairs={{8,0},{16,8},{24,16},{32,24},{40,32},{48,40},{56,48},{64,56},{72,6... | collective-permute-start | bytes 30728 | tf_op jit(solution)/shard_map/ppermute | solution.py:483
  9.4 14.8 %collective-permute-start.12 = (bf16[512,512]{1,0:T(8,128)(2,1)S(1)}, bf16[512,512]{1,0:T(8,128)(2,1)S(1)}, u32[]{:S(2)}, u32[]{:S(2)}) collective-permute-start(bf16[512,512]{1,0:T(8,128)(2,1)S(1)} %get-tuple-element.37.refs_0_), channel_id=1, source_target_pairs={{0,3},{1,0},{2,1},{3,2},{4,7},{5,4},{6,5},{7,6},{8,11},{9,8},{10,9... | collective-permute-start | bytes 1572872 | tf_op jit(solution)/shard_map/ppermute | solution.py:464
  11.3 45.9 %copy-start.3 = (bf16[528,512]{1,0:T(8,128)(2,1)}, bf16[528,512]{1,0:T(8,128)(2,1)S(1)}, u32[]{:S(2)}) copy-start(bf16[528,512]{1,0:T(8,128)(2,1)S(1)} %pad_maximum_fusion.refs_0_.refs_10_) | copy-start | bytes 1622020
  11.3 23.8 %collective-permute-start.4 = (bf16[528,512]{1,0:T(8,128)(2,1)S(1)}, bf16[528,512]{1,0:T(8,128)(2,1)S(1)}, u32[]{:S(2)}, u32[]{:S(2)}) collective-permute-start(bf16[528,512]{1,0:T(8,128)(2,1)S(1)} %pad_maximum_fusion.refs_0_.refs_10_), channel_id=1, source_target_pairs={{0,3},{1,0},{2,1},{3,2},{4,7},{5,4},{6,5},{7,6},{8,11},{9,8},{10,9... | collective-permute-start | bytes 1622024 | tf_op jit(solution)/shard_map/ppermute | solution.py:464
  12.9 25.1 %collective-permute-start.2 = (bf16[528,512]{1,0:T(8,128)(2,1)S(1)}, bf16[528,512]{1,0:T(8,128)(2,1)S(1)}, u32[]{:S(2)}, u32[]{:S(2)}) collective-permute-start(bf16[528,512]{1,0:T(8,128)(2,1)S(1)} %pad_maximum_fusion.refs_0_.refs_10_), channel_id=1, source_target_pairs={{0,1},{1,2},{2,3},{3,0},{4,5},{5,6},{6,7},{7,4},{8,9},{9,10},{10,1... | collective-permute-start | bytes 1622024 | tf_op jit(solution)/shard_map/ppermute | solution.py:464
  13.4 25.1 %collective-permute-start.13 = (bf16[512,512]{1,0:T(8,128)(2,1)S(1)}, bf16[512,512]{1,0:T(8,128)(2,1)}, u32[]{:S(2)}, u32[]{:S(2)}) collective-permute-start(bf16[512,512]{1,0:T(8,128)(2,1)S(1)} %get-tuple-element.37.refs_0_), channel_id=1, source_target_pairs={{0,4},{1,5},{2,6},{3,7},{4,0},{5,1},{6,2},{7,3},{8,12},{9,13},{10,... | collective-permute-start | bytes 1572872 | tf_op jit(solution)/shard_map/ppermute | solution.py:464
  16.3 28.5 %copy-start.12 = (bf16[512,512]{1,0:T(8,128)(2,1)}, bf16[512,512]{1,0:T(8,128)(2,1)S(1)}, u32[]{:S(2)}) copy-start(bf16[512,512]{1,0:T(8,128)(2,1)S(1)} %collective-permute-done.11.refs_1_) | copy-start | bytes 1572868
  16.3 26.6 %collective-permute-start.6 = (bf16[528,512]{1,0:T(8,128)(2,1)S(1)}, bf16[528,512]{1,0:T(8,128)(2,1)S(1)}, u32[]{:S(2)}, u32[]{:S(2)}) collective-permute-start(bf16[528,512]{1,0:T(8,128)(2,1)S(1)} %pad_maximum_fusion.refs_0_.refs_10_), channel_id=1, source_target_pairs={{0,4},{1,5},{2,6},{3,7},{4,0},{5,1},{6,2},{7,3},{8,12},{9,13},{10,... | collective-permute-start | bytes 1622024 | tf_op jit(solution)/shard_map/ppermute | solution.py:464
  24.3 16.1 %collective-permute-start.14 = (bf16[256,512]{1,0:T(8,128)(2,1)S(1)}, bf16[256,512]{1,0:T(8,128)(2,1)}, u32[]{:S(2)}, u32[]{:S(2)}) collective-permute-start(bf16[256,512]{1,0:T(8,128)(2,1)S(1)} %slice.72), channel_id=1, source_target_pairs={{0,1},{1,2},{2,3},{3,0},{4,5},{5,6},{6,7},{7,4},{8,9},{9,10},{10,1... | collective-permute-start | bytes 786440 | tf_op jit(solution)/shard_map/ppermute | solution.py:464
  35.1 9.7 %collective-permute-start.15 = (bf16[256,512]{1,0:T(8,128)(2,1)S(1)}, bf16[256,512]{1,0:T(8,128)(2,1)}, u32[]{:S(2)}, u32[]{:S(2)}) collective-permute-start(bf16[256,512]{1,0:T(8,128)(2,1)S(1)} %slice.73), channel_id=1, source_target_pairs={{0,3},{1,0},{2,1},{3,2},{4,7},{5,4},{6,5},{7,6},{8,11},{9,8},{10,9... | collective-permute-start | bytes 786440 | tf_op jit(solution)/shard_map/ppermute | solution.py:464
  38.1 13.1 %collective-permute-start.5 = (bf16[272,512]{1,0:T(8,128)(2,1)S(1)}, bf16[272,512]{1,0:T(8,128)(2,1)S(1)}, u32[]{:S(2)}, u32[]{:S(2)}) collective-permute-start(bf16[272,512]{1,0:T(8,128)(2,1)S(1)} %slice.71), channel_id=1, source_target_pairs={{0,3},{1,0},{2,1},{3,2},{4,7},{5,4},{6,5},{7,6},{8,11},{9,8},{10,9... | collective-permute-start | bytes 835592 | tf_op jit(solution)/shard_map/ppermute | solution.py:464
  38.5 12.6 %collective-permute-start.3 = (bf16[256,512]{1,0:T(8,128)(2,1)S(1)}, bf16[256,512]{1,0:T(8,128)(2,1)}, u32[]{:S(2)}, u32[]{:S(2)}) collective-permute-start(bf16[256,512]{1,0:T(8,128)(2,1)S(1)} %slice.70), channel_id=1, source_target_pairs={{0,1},{1,2},{2,3},{3,0},{4,5},{5,6},{6,7},{7,4},{8,9},{9,10},{10,1... | collective-permute-start | bytes 786440 | tf_op jit(solution)/shard_map/ppermute | solution.py:464
  40.3 14.2 %collective-permute-start.18 = (bf16[256,512]{1,0:T(8,128)(2,1)}, bf16[256,512]{1,0:T(8,128)(2,1)}, u32[]{:S(2)}, u32[]{:S(2)}) collective-permute-start(bf16[256,512]{1,0:T(8,128)(2,1)} %collective-permute-done.14.refs_4_), channel_id=1, source_target_pairs={{0,4},{1,5},{2,6},{3,7},{4,0},{5,1},{6,2},{7,3},{8,12},{9,13},{10,... | collective-permute-start | bytes 786440 | tf_op jit(solution)/shard_map/ppermute | solution.py:464
  42.9 22.2 %collective-permute-start.16 = (bf16[512,512]{1,0:T(8,128)(2,1)}, bf16[512,512]{1,0:T(8,128)(2,1)}, u32[]{:S(2)}, u32[]{:S(2)}) collective-permute-start(bf16[512,512]{1,0:T(8,128)(2,1)} %collective-permute-done.13.refs_3_), channel_id=1, source_target_pairs={{0,1},{1,2},{2,3},{3,0},{4,5},{5,6},{6,7},{7,4},{8,9},{9,10},{10,1... | collective-permute-start | bytes 1572872 | tf_op jit(solution)/shard_map/ppermute | solution.py:464
  44.8 21.3 %collective-permute-start.17 = (bf16[512,512]{1,0:T(8,128)(2,1)}, bf16[512,512]{1,0:T(8,128)(2,1)}, u32[]{:S(2)}, u32[]{:S(2)}) collective-permute-start(bf16[512,512]{1,0:T(8,128)(2,1)} %collective-permute-done.13.refs_3_), channel_id=1, source_target_pairs={{0,3},{1,0},{2,1},{3,2},{4,7},{5,4},{6,5},{7,6},{8,11},{9,8},{10,9... | collective-permute-start | bytes 1572872 | tf_op jit(solution)/shard_map/ppermute | solution.py:464
  51.1 22.7 %collective-permute-start.7 = (bf16[528,512]{1,0:T(8,128)(2,1)S(1)}, bf16[528,512]{1,0:T(8,128)(2,1)S(1)}, u32[]{:S(2)}, u32[]{:S(2)}) collective-permute-start(bf16[528,512]{1,0:T(8,128)(2,1)S(1)} %collective-permute-done.6.refs_3_.refs_13_), channel_id=1, source_target_pairs={{0,1},{1,2},{2,3},{3,0},{4,5},{5,6},{6,7},{7,4},{8,9},{9,10},{10,1... | collective-permute-start | bytes 1622024 | tf_op jit(solution)/shard_map/ppermute | solution.py:464
  51.2 22.6 %collective-permute-start.8 = (bf16[528,512]{1,0:T(8,128)(2,1)S(1)}, bf16[528,512]{1,0:T(8,128)(2,1)}, u32[]{:S(2)}, u32[]{:S(2)}) collective-permute-start(bf16[528,512]{1,0:T(8,128)(2,1)S(1)} %collective-permute-done.6.refs_3_.refs_13_), channel_id=1, source_target_pairs={{0,3},{1,0},{2,1},{3,2},{4,7},{5,4},{6,5},{7,6},{8,11},{9,8},{10,9... | collective-permute-start | bytes 1622024 | tf_op jit(solution)/shard_map/ppermute | solution.py:464
  54.5 8.1 %collective-permute-start.19 = (bf16[256,512]{1,0:T(8,128)(2,1)}, bf16[256,512]{1,0:T(8,128)(2,1)S(1)}, u32[]{:S(2)}, u32[]{:S(2)}) collective-permute-start(bf16[256,512]{1,0:T(8,128)(2,1)} %collective-permute-done.15.refs_5_), channel_id=1, source_target_pairs={{0,4},{1,5},{2,6},{3,7},{4,0},{5,1},{6,2},{7,3},{8,12},{9,13},{10,... | collective-permute-start | bytes 786440 | tf_op jit(solution)/shard_map/ppermute | solution.py:464
  62.6 11.2 %collective-permute-start.9 = (bf16[256,512]{1,0:T(8,128)(2,1)}, bf16[256,512]{1,0:T(8,128)(2,1)S(1)}, u32[]{:S(2)}, u32[]{:S(2)}) collective-permute-start(bf16[256,512]{1,0:T(8,128)(2,1)} %collective-permute-done.3.refs_0_.refs_14_), channel_id=1, source_target_pairs={{0,4},{1,5},{2,6},{3,7},{4,0},{5,1},{6,2},{7,3},{8,12},{9,13},{10,... | collective-permute-start | bytes 786440 | tf_op jit(solution)/shard_map/ppermute | solution.py:464
  65.1 10.1 %collective-permute-start.10 = (bf16[272,512]{1,0:T(8,128)(2,1)S(1)}, bf16[272,512]{1,0:T(8,128)(2,1)S(1)}, u32[]{:S(2)}, u32[]{:S(2)}) collective-permute-start(bf16[272,512]{1,0:T(8,128)(2,1)S(1)} %collective-permute-done.5.refs_1_.refs_15_), channel_id=1, source_target_pairs={{0,4},{1,5},{2,6},{3,7},{4,0},{5,1},{6,2},{7,3},{8,12},{9,13},{10,... | collective-permute-start | bytes 835592 | tf_op jit(solution)/shard_map/ppermute | solution.py:464
  88.3 23.7 %all-to-all-start = ((bf16[32,8,640]{2,1,0:T(8,128)(2,1)}), bf16[32,8,640]{2,1,0:T(8,128)(2,1)S(1)}, u32[]{:S(2)}, u32[]{:S(2)}) async-start(bf16[32,8,640]{2,1,0:T(8,128)(2,1)} %bitcast.22), calls=%async_computation | async-start | bytes 655360 | tf_op jit(solution)/shard_map/all_to_all | solution.py:507
  112.8 16.3 %all-to-all-start.1 = ((bf16[32,8,512]{2,1,0:T(8,128)(2,1)}), bf16[32,8,512]{2,1,0:T(8,128)(2,1)S(1)}, u32[]{:S(2)}, u32[]{:S(2)}) async-start(bf16[32,8,512]{2,1,0:T(8,128)(2,1)} %scan.1), calls=%async_computation.1 | async-start | bytes 524288 | tf_op jit(solution)/shard_map/all_to_all | solution.py:512
  135.0 5.2 %collective-permute-start.20 = (f32[4,1,256]{2,1,0:T(1,128)S(1)}, f32[4,1,256]{2,1,0:T(1,128)S(1)}, u32[]{:S(2)}, u32[]{:S(2)}) collective-permute-start(f32[4,1,256]{2,1,0:T(1,128)S(1)} %get-tuple-element.36), channel_id=1, source_target_pairs={{0,4},{1,5},{2,6},{3,7},{4,0},{5,1},{6,2},{7,3},{8,12},{9,13},{10,... | collective-permute-start | bytes 12296 | tf_op jit(solution)/shard_map/ppermute | solution.py:464
  140.2 4.8 %collective-permute-start.21 = (f32[4,1,256]{2,1,0:T(1,128)S(1)}, f32[4,1,256]{2,1,0:T(1,128)S(1)}, u32[]{:S(2)}, u32[]{:S(2)}) collective-permute-start(f32[4,1,256]{2,1,0:T(1,128)S(1)} %add.90.refs_0_), channel_id=1, source_target_pairs={{0,1},{1,2},{2,3},{3,0},{4,5},{5,6},{6,7},{7,4},{8,9},{9,10},{10,1... | collective-permute-start | bytes 12296 | tf_op jit(solution)/shard_map/ppermute | solution.py:464
  140.3 5.2 %collective-permute-start.22 = (f32[4,1,256]{2,1,0:T(1,128)S(1)}, f32[4,1,256]{2,1,0:T(1,128)S(1)}, u32[]{:S(2)}, u32[]{:S(2)}) collective-permute-start(f32[4,1,256]{2,1,0:T(1,128)S(1)} %add.90.refs_0_), channel_id=1, source_target_pairs={{0,2},{1,3},{2,0},{3,1},{4,6},{5,7},{6,4},{7,5},{8,10},{9,11},{10,... | collective-permute-start | bytes 12296 | tf_op jit(solution)/shard_map/ppermute | solution.py:464
  142.1 3.8 %collective-permute-start.23 = (f32[4,1,256]{2,1,0:T(1,128)S(1)}, f32[4,1,256]{2,1,0:T(1,128)S(1)}, u32[]{:S(2)}, u32[]{:S(2)}) collective-permute-start(f32[4,1,256]{2,1,0:T(1,128)S(1)} %add.90.refs_0_), channel_id=1, source_target_pairs={{0,3},{1,0},{2,1},{3,2},{4,7},{5,4},{6,5},{7,6},{8,11},{9,8},{10,9... | collective-permute-start | bytes 12296 | tf_op jit(solution)/shard_map/ppermute | solution.py:464
  (13 other events, 135.5 us)

commit v3 on v2

--- a/solution.py
+++ b/solution.py
@@ -99,8 +99,10 @@
     n = len(plan)
     pieces, refs = refs[:n], refs[n:]
     wx, wb, wd, bias = refs[:4]
-    outs, (buf, vx, vb, sems) = refs[4:7], refs[7:]
-    sums = multiply(slots, plan, idx, pieces, (wx, wb), wd, buf, (vx, vb), sems, [None] * 3)
+    held, refs = (refs[4:7], refs[7:]) if last else (None, refs[4:])
+    outs, (buf, vx, vb, sems) = refs[:3], refs[3:]
+    sums = [h[...] for h in held] if last else [None] * 3
+    sums = multiply(slots, plan, idx, pieces, (wx, wb), wd, buf, (vx, vb), sems, sums)
     if last:
         outs[0][...] = sums[0].astype(BF16)
         outs[1][...] = sums[1].astype(BF16)
@@ -118,14 +120,15 @@
     )
 
 
-def project(idx, slots, pieces, wx, wb, wd, bias, last):
+def project(idx, slots, pieces, wx, wb, wd, bias, held=()):
+    last = len(held) > 0
     rows, depth = max(p.shape[0] for p in pieces), pieces[0].shape[1]
     plan, n = plan_of(pieces)
     nx, nb, nd = wx.shape[1], wb.shape[1], wd.shape[0]
     kind = BF16 if last else F32
     return pl.pallas_call(
         functools.partial(project_kernel, slots, plan, last),
-        in_specs=[SMEM] + [ANY] * (len(pieces) + 2) + [VMEM, VMEM],
+        in_specs=[SMEM] + [ANY] * (len(pieces) + 2) + [VMEM] * (2 + len(held)),
         out_specs=[VMEM] * 3,
         scratch_shapes=scratch_of(n, rows, depth, (nx, nb), 2 * n + len(pieces)),
         out_shape=[
@@ -140,7 +143,7 @@
             transcendentals=0,
         ),
         name="project",
-    )(idx, *far(*pieces, wx, wb), wd, bias)
+    )(idx, *far(*pieces, wx, wb), wd, bias, *held)
 
 
 def gate_kernel(plan_a, plan_b, idx, *refs):
@@ -184,7 +187,13 @@
 def running(dt, rates):
     at, to = order()
     a = -dt * rates
-    cf = jnp.dot(a, (at <= to).astype(F32), precision=lax.Precision.HIGHEST, preferred_element_type=F32)
+    rows = a.shape[0]
+    high = a.astype(BF16)
+    rest = a - high.astype(F32)
+    mid = rest.astype(BF16)
+    low = (rest - mid.astype(F32)).astype(BF16)
+    three = dot(jnp.concatenate([high, mid, low], axis=0), (at <= to).astype(F32).astype(BF16))
+    cf = three[:rows] + three[rows : 2 * rows] + three[2 * rows :]
     return cf, cf - a
 
 
@@ -216,8 +225,8 @@
     n = len(plan)
     pieces, refs = refs[:n], refs[n:]
     wx, wb, wd, bias, hx, hb, hd, xa, ba, da, kx, kb, segs, rates = refs[:14]
-    xs, bcs, dts, pay, loc, dec = refs[14:20]
-    buf, vx, vb, sems, xf, bf = refs[20:]
+    xs, bcs, dts, sums_out, opens, pay, loc_out, dec = refs[14:22]
+    buf, vx, vb, sems, xf, bf, loc = refs[22:]
     half = xa.shape[0]
     blocks = 2 * half // BLOCK
     xf[8 : 8 + half] = xa[...].astype(F32)
@@ -232,13 +241,21 @@
     dts[:, :half] = da[...]
     dts[:, half:] = step_sizes(sums[2], bias[...][:, 0:1])[:, :half]
     rate = rates[...][:, 0:1]
+    cut = lambda ref, b: ref[:, b * BLOCK : (b + 1) * BLOCK]
+    cfs, ces = running(
+        jnp.concatenate([cut(dts, b) for b in range(blocks)], axis=0), jnp.concatenate([rate] * blocks, axis=0)
+    )
     steps = []
     for b in range(blocks):
         at = b * BLOCK
         seg, prev, nxt, start, end, prev_end, next_start = marks(segs[:, at : at + BLOCK])
         dt = dts[:, at : at + BLOCK]
-        cf, ce = running(dt, rate)
+        cf, ce = cfs[SUB * b : SUB * (b + 1)], ces[SUB * b : SUB * (b + 1)]
         last = cf[:, BLOCK - 1 :]
+        sums_out[:, at : at + BLOCK] = jnp.concatenate([cf, ce], axis=0)
+        opens[:, at : at + BLOCK] = jnp.concatenate(
+            [jnp.exp(cf) * equal(seg, prev_end), jnp.exp(last - ce) * equal(seg, next_start)], axis=0
+        )
         wide = lambda row: jnp.broadcast_to(row, (SUB, BLOCK))
         col = columns(
             jnp.exp(last - cf) * dt * equal(seg, end),
@@ -269,7 +286,7 @@
         for i in range(blocks):
             b = i if way == 0 else blocks - 1 - i
             fresh = loc[way, b]
-            loc[way, b] = state
+            loc_out[way, b] = state.astype(BF16)
             dec[way, b : b + 1] = spread(total, heads)
             step = steps[b][way]
             state = spread(step, heads) * state + fresh
@@ -296,13 +313,19 @@
             pltpu.HBM((rows, nx), BF16),
             pltpu.HBM((rows, nb), BF16),
             pltpu.HBM((SUB, rows), F32),
+            pltpu.HBM((2 * SUB, rows), F32),
+            pltpu.HBM((2 * SUB, rows), F32),
             pltpu.HBM((2 * LANES, nx + LANES), BF16),
-            pltpu.HBM((2, blocks, LANES, nx), F32),
+            pltpu.HBM((2, blocks, LANES, nx), BF16),
             pltpu.HBM((2, blocks, nx), F32),
         ],
-        out_specs=[VMEM] * 6,
+        out_specs=[VMEM] * 8,
         scratch_shapes=scratch_of(n, part, depth, (nx, nb), 2 * n + len(pieces))
-        + [pltpu.VMEM((rows + 16, nx), F32), pltpu.VMEM((rows + 16, nb), F32)],
+        + [
+            pltpu.VMEM((rows + 16, nx), F32),
+            pltpu.VMEM((rows + 16, nb), F32),
+            pltpu.VMEM((2, blocks, LANES, nx), F32),
+        ],
         compiler_params=params(30),
         name="states",
     )(idx, *far(*pieces, wx, wb), wd, bias, *held, xa, ba, da, kx, kb, segs, rates)
@@ -335,9 +358,9 @@
     )(flag, src)
 
 
-def inside_kernel(heads, xs, bcs, dts, segs, rates, out):
+def inside_kernel(heads, xs, bcs, dts, sums, segs, out):
     dt = dts[...]
-    cf, ce = running(dt, rates[...][:, 0:1])
+    cf, ce = sums[:SUB], sums[SUB:]
     row = segs[...]
     col = columns(cf, ce, row)
     bc = bcs[...]
@@ -357,16 +380,16 @@
 
 
 LANE_BLOCK = pl.BlockSpec((SUB, BLOCK), lambda b: (0, b))
-RATE_BLOCK = pl.BlockSpec((SUB, LANES), lambda b: (0, 0))
-
-
-def inside(heads, xs, bcs, dts, segs, rates):
+PAIR_BLOCK = pl.BlockSpec((2 * SUB, BLOCK), lambda b: (0, b))
+
+
+def inside(heads, xs, bcs, dts, sums, segs):
     rows, nx = xs.shape
     nb = bcs.shape[1]
     return pl.pallas_call(
         functools.partial(inside_kernel, heads),
         grid=(rows // BLOCK,),
-        in_specs=[row_block(nx), row_block(nb), LANE_BLOCK, LANE_BLOCK, RATE_BLOCK],
+        in_specs=[row_block(nx), row_block(nb), LANE_BLOCK, PAIR_BLOCK, LANE_BLOCK],
         out_specs=row_block(nx),
         out_shape=pltpu.HBM((rows, nx), F32),
         compiler_params=params(8),
@@ -374,20 +397,16 @@
             flops=2 * rows * BLOCK * (nx + LANES), bytes_accessed=rows * nx * 6, transcendentals=rows * BLOCK * heads
         ),
         name="inside",
-    )(*far(xs, bcs, dts), segs, rates)
-
-
-def finish_kernel(heads, enter, loc, dec, y_in, sg, bcs, dts, segs, rates, out, ss):
+    )(*far(xs, bcs, dts, sums), segs)
+
+
+def finish_kernel(heads, enter, loc, dec, y_in, sg, bcs, opens, out, ss):
     b = pl.program_id(0)
-    cf, ce = running(dts[...], rates[...][:, 0:1])
-    seg, prev, nxt, start, end, prev_end, next_start = marks(segs[...])
-    col = columns(
-        jnp.exp(cf) * equal(seg, prev_end), jnp.exp(cf[:, BLOCK - 1 :] - ce) * equal(seg, next_start)
-    )
+    col = columns(opens[:SUB], opens[SUB:])
     c = bcs[...][:, LANES:]
     y = y_in[...]
     for way in range(2):
-        held = dec[way, b][None] * enter[way * LANES : (way + 1) * LANES].astype(F32) + loc[way, 0]
+        held = dec[way, b][None] * enter[way * LANES : (way + 1) * LANES].astype(F32) + loc[way, 0].astype(F32)
         y = y + weigh(dot(c, held.astype(BF16)), col, way * SUB, heads)
     gated = y * sg[...]
     out[...] = gated
@@ -398,7 +417,7 @@
     ss[0] = jnp.sum(part.T, axis=0, keepdims=True)
 
 
-def finish(heads, enter, loc, dec, y_in, sg, bcs, dts, segs, rates):
+def finish(heads, enter, loc, dec, y_in, sg, bcs, opens):
     rows, nx = y_in.shape
     nb = bcs.shape[1]
     blocks = rows // BLOCK
@@ -412,34 +431,35 @@
             row_block(nx),
             row_block(nx),
             row_block(nb),
-            LANE_BLOCK,
-            LANE_BLOCK,
-            RATE_BLOCK,
+            PAIR_BLOCK,
         ],
         out_specs=[row_block(nx), pl.BlockSpec((1, 1, BLOCK), lambda b: (b, 0, 0))],
         out_shape=[jax.ShapeDtypeStruct((rows, nx), F32), jax.ShapeDtypeStruct((blocks, 1, BLOCK), F32)],
         compiler_params=params(12),
         name="finish",
-    )(enter, *far(loc, dec, y_in, sg, bcs, dts), segs, rates)
+    )(enter, *far(loc, dec, y_in, sg, bcs, opens))
 
 
 def scale_kernel(columns, gated, gain, *refs):
     parts, out = refs[:-1], refs[-1]
-    total = parts[0][0]
-    for p in parts[1:]:
-        total = total + p[0]
-    scale = lax.rsqrt(total / columns + 1e-05)
-    col = jnp.broadcast_to(scale, (LANES, BLOCK)).T[:, 0:1]
-    out[...] = (gated[...] * col * gain[...]).astype(BF16)
+    for i in range(out.shape[0] // BLOCK):
+        total = parts[0][i]
+        for p in parts[1:]:
+            total = total + p[i]
+        factor = lax.rsqrt(total / columns + 1e-05)
+        col = jnp.broadcast_to(factor, (LANES, BLOCK)).T[:, 0:1]
+        at = pl.ds(i * BLOCK, BLOCK)
+        out[at] = (gated[at] * col * gain[...]).astype(BF16)
 
 
 def scale(columns, gated, gain, parts):
     rows, nx = gated.shape
-    row = pl.BlockSpec((BLOCK, nx), lambda b: (b, 0))
-    part = pl.BlockSpec((1, 1, BLOCK), lambda b: (b, 0, 0))
+    per = 2
+    row = pl.BlockSpec((per * BLOCK, nx), lambda b: (b, 0))
+    part = pl.BlockSpec((per, 1, BLOCK), lambda b: (b, 0, 0))
     return pl.pallas_call(
         functools.partial(scale_kernel, columns),
-        grid=(rows // BLOCK,),
+        grid=(rows // (per * BLOCK),),
         in_specs=[row, pl.BlockSpec((1, nx), lambda b: (0, 0))] + [part] * len(parts),
         out_specs=row,
         out_shape=jax.ShapeDtypeStruct((rows, nx), BF16),
@@ -466,14 +486,16 @@
     across = [(i, (i + ring) % mp) for i in range(mp)]
     half = rows // 2
 
-    def spread_out(own):
+    def hop(own):
+        return own, send(own, right), send(own, left), send(own, across)
+
+    def spread_out(own, r1, l1, p):
         cut = half // 2
-        r1, l1, p = send(own, right), send(own, left), send(own, across)
         o1, o2 = send(r1[:cut], right), send(l1[cut:], left)
-        pr, pm = send(p, right), send(p, left)
-        return [own, r1, l1, p, o1, o2, pr, pm, send(o1, across), send(o2, across)]
-
-    pieces_a = spread_out(tokens[:half])
+        o1, o2, q = lax.optimization_barrier((o1, o2, p))
+        return [own, r1, l1, p, o1, o2, send(q, right), send(q, left), send(o1, across), send(o2, across)]
+
+    hop_a = hop(tokens[:half])
 
     seg = segment_ids.astype(F32) + 1.0
     label = lambda v: jnp.broadcast_to(v[:, None], (SUB, LANES)).astype(BF16)
@@ -484,7 +506,10 @@
     left_seg = before[SUB - 1, depth].astype(F32)
     right_seg = after[0, depth].astype(F32)
 
-    pieces_b = spread_out(jnp.concatenate([tokens[half:], before[:, :depth], after[:, :depth]], axis=0))
+    own_b = jnp.concatenate([tokens[half:], before[:, :depth], after[:, :depth]], axis=0)
+    own_b, *hop_a = lax.optimization_barrier((own_b, *hop_a))
+    pieces_a = spread_out(*hop_a)
+    pieces_b = spread_out(*hop(own_b))
     idx = jnp.stack(
         [r * ring + (col_at + s) % ring for r, s in (
             (row_at, 0), (row_at, -1), (row_at, 1), (1 - row_at, 0),
@@ -497,22 +522,25 @@
     rate, bias = tall(rates, SUB), tall(dt_bias, 16)
     w_d = jnp.pad(w_dt.T, ((0, 16 - heads), (0, 0)))
 
-    xa, ba, da = project(idx, tuple(range(8)), pieces_a, w_x, w_bc, w_d, bias, True)
-    held = project(idx, (0, 1, 2, 3), pieces_b[:4], w_x, w_bc, w_d, bias, False)
-    xs, bcs, dts, pay, loc, dec = states(
+    w_d = tie(w_d, pieces_a[4], pieces_a[5])
+    held_a = project(idx, (0, 1, 2, 3), pieces_a[:4], w_x, w_bc, w_d, bias)
+    w_d, *held_a = lax.optimization_barrier((w_d, *held_a, pieces_b[4], pieces_b[5]))[:4]
+    xa, ba, da = project(idx, (4, 5, 6, 7), pieces_a[4:], w_x, w_bc, w_d, bias, held_a)
+    held = project(idx, (0, 1, 2, 3), pieces_b[:4], w_x, w_bc, w_d, bias)
+    xs, bcs, dts, sums, opens, pay, loc, dec = states(
         heads, idx, (4, 5, 6, 7), pieces_b[4:], w_x, w_bc, w_d, bias, held, xa, ba, da, conv_x, conv_bc, segs, rate
     )
 
     width = nx
     got = lax.all_to_all(pay.reshape(seq, 2 * LANES // seq, width + LANES), "seq", 0, 0)
     flag = (lax.axis_index("seq") < seq // 2).astype(jnp.int32)[None]
-    y_in = inside(heads, xs, bcs, dts, segs, rate)
+    y_in = inside(heads, xs, bcs, dts, sums, segs)
     got, y_in = lax.optimization_barrier((got, y_in))
     entered = scan(heads, flag, got, width)
     enter = lax.all_to_all(entered, "seq", 0, 0).reshape(2 * LANES, width)
     sg = gate_project(idx, pieces_a, pieces_b, w_z)
 
-    gated, ss = finish(heads, enter, loc, dec, y_in, sg, bcs, dts, segs, rate)
+    gated, ss = finish(heads, enter, loc, dec, y_in, sg, bcs, opens)
     ss = ss + send(ss, across)
     parts = [ss] + [send(ss, turn(s)) for s in range(1, ring)]
     return scale(nx * mp, gated, norm_gain[None], parts)

time: 150 us -> 144 us (0.960)
  starting transfers between devices: 58.7 us -> 55.3 us
  Pallas kernels: 48.9 us -> 46.1 us
  local copies, waits for them, and re-layouts: 4.37 us -> 5.97 us
    ppermute x22, waiting for transfers between devices: 23.7 us -> 17.9 us  [shards(): send = lambda v, pairs: lax.ppermute(v, 'mp', pairs)]
    ppermute x1, waiting for transfers between devices: 0.01 us -> 4.36 us  [shards(): before = lax.ppermute(tail, 'seq', [(i, i + 1) for i in range(seq - 1)])]
    ppermute x22, starting transfers between devices: 38.8 us -> 35.5 us  [shards(): send = lambda v, pairs: lax.ppermute(v, 'mp', pairs)]
    pallas_call x2 -> x3, Pallas kernels: 12.7 us -> 14.4 us  [project(): pl.pallas_call(functools.partial(project_kernel, slots, plan, last), in_s...]
    slice x4, local copies, waits for them, and re-layouts: 0.07 us -> 1.6 us  [spread_out(): o1, o2 = (send(r1[:cut], right), send(l1[cut:], left))]
  transfers between devices with their start and end apart: 26 -> 26, of which waited for: 12 -> 10; matrix products, arithmetic and copies ran while one was open for 2% -> 3% of each run, Pallas kernels for 19% -> 20%
where the time goes in v3:
time: 144 us; the launch traced here: 143 us
  starting transfers between devices  55.3 us (38%)
  Pallas kernels  46.1 us (32%)
  waiting for transfers between devices  33.8 us (23%)
  local copies, waits for them, and re-layouts  5.97 us (4%)
  between operations  1.64 us (1%)
    ppermute x22, starting transfers between devices, shards(): send = lambda v, pairs: lax.ppermute(v, 'mp', pairs)  35.5 us
    ppermute x22, waiting for transfers between devices, shards(): send = lambda v, pairs: lax.ppermute(v, 'mp', pairs)  17.9 us
    pallas_call x3, Pallas kernels, project(): pl.pallas_call(functools.partial(project_kernel, slots, plan, last), in_s...  14.4 us
    pallas_call x1, Pallas kernels, states(): pl.pallas_call(functools.partial(state_kernel, heads, slots, plan), in_sp...  10.8 us
    all_to_all x1, starting transfers between devices, shards(): lax.all_to_all(pay.reshape(seq, 2 * LANES // seq, width + LANES), 'seq',...  10.2 us
    pallas_call x1, Pallas kernels, gate_project(): pl.pallas_call(functools.partial(gate_kernel, plan_a, plan_b), in_specs=[...  8.89 us
    all_to_all x1, waiting for transfers between devices, shards(): lax.all_to_all(pay.reshape(seq, 2 * LANES // seq, width + LANES), 'seq',...  8.27 us
    pallas_call x1, Pallas kernels, inside(): pl.pallas_call(functools.partial(inside_kernel, heads), grid=(rows // BLO...  5.22 us
  transfers between devices with their start and end apart: 26, of which 10 were waited for; matrix products, arithmetic and copies ran while one was open for 3% of the time, Pallas kernels for 20%

profile of v3, /device:TPU:8, one launch (start us, length us, event | category | flops | bytes accessed | tf_op | source)
XLA Modules:
  0.0 143.0 jit_solution(10481944433268558849)
XLA Ops:
  1.3 1.6 %collective-permute-start.2 = (bf16[512,512]{1,0:T(8,128)(2,1)S(1)}, bf16[512,512]{1,0:T(8,128)(2,1)S(1)}, u32[]{:S(2)}, u32[]{:S(2)}) collective-permute-start(bf16[512,512]{1,0:T(8,128)(2,1)S(1)} %get-tuple-element.52.refs_0_), channel_id=1, source_target_pairs={{0,1},{1,2},{2,3},{3,0},{4,5},{5,6},{6,7},{7,4},{8,9},{9,10},{10,1... | collective-permute-start | bytes 1572872 | tf_op jit(solution)/shard_map/ppermute | solution.py:484
  2.9 1.7 %collective-permute-start.3 = (bf16[512,512]{1,0:T(8,128)(2,1)S(1)}, bf16[512,512]{1,0:T(8,128)(2,1)S(1)}, u32[]{:S(2)}, u32[]{:S(2)}) collective-permute-start(bf16[512,512]{1,0:T(8,128)(2,1)S(1)} %get-tuple-element.52.refs_0_), channel_id=1, source_target_pairs={{0,3},{1,0},{2,1},{3,2},{4,7},{5,4},{6,5},{7,6},{8,11},{9,8},{10,9... | collective-permute-start | bytes 1572872 | tf_op jit(solution)/shard_map/ppermute | solution.py:484
  4.6 2.3 %collective-permute-start.4 = (bf16[512,512]{1,0:T(8,128)(2,1)S(1)}, bf16[512,512]{1,0:T(8,128)(2,1)}, u32[]{:S(2)}, u32[]{:S(2)}) collective-permute-start(bf16[512,512]{1,0:T(8,128)(2,1)S(1)} %get-tuple-element.52.refs_0_), channel_id=1, source_target_pairs={{0,4},{1,5},{2,6},{3,7},{4,0},{5,1},{6,2},{7,3},{8,12},{9,13},{10,... | collective-permute-start | bytes 1572872 | tf_op jit(solution)/shard_map/ppermute | solution.py:484
  7.8 1.9 %collective-permute-start = (bf16[8,640]{1,0:T(8,128)(2,1)S(1)}, bf16[8,640]{1,0:T(8,128)(2,1)S(1)}, u32[]{:S(2)}, u32[]{:S(2)}) collective-permute-start(bf16[8,640]{1,0:T(8,128)(2,1)S(1)} %pad_maximum_fusion.1), channel_id=1, source_target_pairs={{0,8},{8,16},{16,24},{24,32},{32,40},{40,48},{48,56},{56,64},{64,7... | collective-permute-start | bytes 30728 | tf_op jit(solution)/shard_map/ppermute | solution.py:504
  9.8 3.6 %collective-permute-start.1 = (bf16[8,640]{1,0:T(8,128)(2,1)S(1)}, bf16[8,640]{1,0:T(8,128)(2,1)S(1)}, u32[]{:S(2)}, u32[]{:S(2)}) collective-permute-start(bf16[8,640]{1,0:T(8,128)(2,1)S(1)} %pad_maximum_fusion.2), channel_id=1, source_target_pairs={{8,0},{16,8},{24,16},{32,24},{40,32},{48,40},{56,48},{64,56},{72,6... | collective-permute-start | bytes 30728 | tf_op jit(solution)/shard_map/ppermute | solution.py:505
  13.5 4.4 %collective-permute-done = bf16[8,640]{1,0:T(8,128)(2,1)S(1)} collective-permute-done((bf16[8,640]{1,0:T(8,128)(2,1)S(1)}, bf16[8,640]{1,0:T(8,128)(2,1)S(1)}, u32[]{:S(2)}, u32[]{:S(2)}) %collective-permute-start) | collective-permute-done | bytes 10272 | tf_op jit(solution)/shard_map/ppermute | solution.py:504
  17.9 1.4 %collective-permute-done.4.refs_3_ = bf16[512,512]{1,0:T(8,128)(2,1)} collective-permute-done((bf16[512,512]{1,0:T(8,128)(2,1)S(1)}, bf16[512,512]{1,0:T(8,128)(2,1)}, u32[]{:S(2)}, u32[]{:S(2)}) %collective-permute-start.4) | collective-permute-done | bytes 524320 | tf_op jit(solution)/shard_map/ppermute | solution.py:484
  19.4 1.5 %collective-permute-start.7 = (bf16[528,512]{1,0:T(8,128)(2,1)S(1)}, bf16[528,512]{1,0:T(8,128)(2,1)S(1)}, u32[]{:S(2)}, u32[]{:S(2)}) collective-permute-start(bf16[528,512]{1,0:T(8,128)(2,1)S(1)} %pad_maximum_fusion.refs_0_.refs_10_), channel_id=1, source_target_pairs={{0,3},{1,0},{2,1},{3,2},{4,7},{5,4},{6,5},{7,6},{8,11},{9,8},{10,9... | collective-permute-start | bytes 1622024 | tf_op jit(solution)/shard_map/ppermute | solution.py:484
  21.4 2.3 %collective-permute-start.9 = (bf16[528,512]{1,0:T(8,128)(2,1)S(1)}, bf16[528,512]{1,0:T(8,128)(2,1)S(1)}, u32[]{:S(2)}, u32[]{:S(2)}) collective-permute-start(bf16[528,512]{1,0:T(8,128)(2,1)S(1)} %pad_maximum_fusion.refs_0_.refs_10_), channel_id=1, source_target_pairs={{0,4},{1,5},{2,6},{3,7},{4,0},{5,1},{6,2},{7,3},{8,12},{9,13},{10,... | collective-permute-start | bytes 1622024 | tf_op jit(solution)/shard_map/ppermute | solution.py:484
  24.1 3.0 %collective-permute-start.15 = (bf16[256,512]{1,0:T(8,128)(2,1)S(1)}, bf16[256,512]{1,0:T(8,128)(2,1)S(1)}, u32[]{:S(2)}, u32[]{:S(2)}) collective-permute-start(bf16[256,512]{1,0:T(8,128)(2,1)S(1)} %slice.63), channel_id=1, source_target_pairs={{0,3},{1,0},{2,1},{3,2},{4,7},{5,4},{6,5},{7,6},{8,11},{9,8},{10,9... | collective-permute-start | bytes 786440 | tf_op jit(solution)/shard_map/ppermute | solution.py:484
  27.1 7.4 %collective-permute-done.7.refs_2_.refs_12_ = bf16[528,512]{1,0:T(8,128)(2,1)S(1)} collective-permute-done((bf16[528,512]{1,0:T(8,128)(2,1)S(1)}, bf16[528,512]{1,0:T(8,128)(2,1)S(1)}, u32[]{:S(2)}, u32[]{:S(2)}) %collective-permute-start.7) | collective-permute-done | bytes 540704 | tf_op jit(solution)/shard_map/ppermute | solution.py:484
  35.3 2.8 %collective-permute-start.8 = (bf16[272,512]{1,0:T(8,128)(2,1)}, bf16[272,512]{1,0:T(8,128)(2,1)}, u32[]{:S(2)}, u32[]{:S(2)}) collective-permute-start(bf16[272,512]{1,0:T(8,128)(2,1)} %slice.71), channel_id=1, source_target_pairs={{0,3},{1,0},{2,1},{3,2},{4,7},{5,4},{6,5},{7,6},{8,11},{9,8},{10,9... | collective-permute-start | bytes 835592 | tf_op jit(solution)/shard_map/ppermute | solution.py:484
  38.9 3.7 %collective-permute-done.14.refs_0_.refs_4_ = bf16[256,512]{1,0:T(8,128)(2,1)} collective-permute-done((bf16[256,512]{1,0:T(8,128)(2,1)S(1)}, bf16[256,512]{1,0:T(8,128)(2,1)}, u32[]{:S(2)}, u32[]{:S(2)}) %collective-permute-start.14) | collective-permute-done | bytes 262176 | tf_op jit(solution)/shard_map/ppermute | solution.py:484
  42.6 2.3 %collective-permute-start.18 = (bf16[256,512]{1,0:T(8,128)(2,1)}, bf16[256,512]{1,0:T(8,128)(2,1)}, u32[]{:S(2)}, u32[]{:S(2)}) collective-permute-start(bf16[256,512]{1,0:T(8,128)(2,1)} %collective-permute-done.14.refs_0_.refs_4_), channel_id=1, source_target_pairs={{0,4},{1,5},{2,6},{3,7},{4,0},{5,1},{6,2},{7,3},{8,12},{9,13},{10,... | collective-permute-start | bytes 786440 | tf_op jit(solution)/shard_map/ppermute | solution.py:484
  45.0 3.3 %collective-permute-start.17 = (bf16[512,512]{1,0:T(8,128)(2,1)}, bf16[512,512]{1,0:T(8,128)(2,1)}, u32[]{:S(2)}, u32[]{:S(2)}) collective-permute-start(bf16[512,512]{1,0:T(8,128)(2,1)} %collective-permute-done.4.refs_3_), channel_id=1, source_target_pairs={{0,3},{1,0},{2,1},{3,2},{4,7},{5,4},{6,5},{7,6},{8,11},{9,8},{10,9... | collective-permute-start | bytes 1572872 | tf_op jit(solution)/shard_map/ppermute | solution.py:484
  52.0 3.2 %collective-permute-start.11 = (bf16[528,512]{1,0:T(8,128)(2,1)S(1)}, bf16[528,512]{1,0:T(8,128)(2,1)}, u32[]{:S(2)}, u32[]{:S(2)}) collective-permute-start(bf16[528,512]{1,0:T(8,128)(2,1)S(1)} %collective-permute-done.9.refs_3_.refs_13_), channel_id=1, source_target_pairs={{0,3},{1,0},{2,1},{3,2},{4,7},{5,4},{6,5},{7,6},{8,11},{9,8},{10,9... | collective-permute-start | bytes 1622024 | tf_op jit(solution)/shard_map/ppermute | solution.py:484
  55.5 4.8 %project.3 = (f32[512,512]{1,0:T(8,128)S(1)}, f32[512,256]{1,0:T(8,128)S(1)}, f32[16,512]{1,0:T(8,128)S(1)}) custom-call(s32[8]{0:T(128)S(1)} %stack.52.idx, bf16[512,512]{1,0:T(8,128)(2,1)} %copy-done.4, bf16[512,512]{1,0:T(8,128)(2,1)} %copy-done.7, bf16[512,512]{1,0:T(8,128)(2,1)} %copy-done.8, bf16[512,512]{1,0:T(8,128)(2,1)} %collective-permute-done.4.refs_3_, ...), custom_call_target="tpu_custom_call" | custom-call | flops 1879048192 | bytes 5242880 | tf_op jit(solution)/shard_map/project/pallas_call | solution.py:129
  60.3 2.4 %collective-permute-start.13 = (bf16[272,512]{1,0:T(8,128)(2,1)}, bf16[272,512]{1,0:T(8,128)(2,1)S(1)}, u32[]{:S(2)}, u32[]{:S(2)}) collective-permute-start(bf16[272,512]{1,0:T(8,128)(2,1)} %collective-permute-done.8.refs_1_.refs_15_), channel_id=1, source_target_pairs={{0,4},{1,5},{2,6},{3,7},{4,0},{5,1},{6,2},{7,3},{8,12},{9,13},{10,... | collective-permute-start | bytes 835592 | tf_op jit(solution)/shard_map/ppermute | solution.py:484
  63.9 4.7 %project.5 = (bf16[512,512]{1,0:T(8,128)(2,1)S(1)}, bf16[512,256]{1,0:T(8,128)(2,1)S(1)}, f32[8,512]{1,0:T(8,128)S(1)}) custom-call(s32[8]{0:T(128)S(1)} %stack.52.idx, bf16[256,512]{1,0:T(8,128)(2,1)} %collective-permute-done.14.refs_0_.refs_4_, bf16[256,512]{1,0:T(8,128)(2,1)} %copy-done.11, bf16[512,512]{1,0:T(8,128)(2,1)} %collective-permute-done.16.refs_2_.refs_6_, ...), custom_call_target="tpu_custom_call" | custom-call | flops 1879048192 | bytes 5242880 | tf_op jit(solution)/shard_map/project/pallas_call | solution.py:129
  68.6 5.0 %project.4 = (f32[528,512]{1,0:T(8,128)S(1)}, f32[528,256]{1,0:T(8,128)S(1)}, f32[16,528]{1,0:T(8,128)S(1)}) custom-call(s32[8]{0:T(128)S(1)} %stack.52.idx, bf16[528,512]{1,0:T(8,128)(2,1)} %copy-done.3, bf16[528,512]{1,0:T(8,128)(2,1)} %copy-done.6, bf16[528,512]{1,0:T(8,128)(2,1)} %copy-done.5, bf16[528,512]{1,0:T(8,128)(2,1)} %copy-done.9, ...), custom_call_target="tpu_custom_call" | custom-call | flops 1937768448 | bytes 5308416 | tf_op jit(solution)/shard_map/project/pallas_call | solution.py:129
  74.5 10.8 %states.1 = (bf16[1024,512]{1,0:T(8,128)(2,1)}, bf16[1024,256]{1,0:T(8,128)(2,1)}, f32[8,1024]{1,0:T(8,128)}, f32[16,1024]{1,0:T(8,128)}, f32[16,1024]{1,0:T(8,1...) custom-call(s32[8]{0:T(128)S(1)} %stack.52.idx, ...), custom_call_target="tpu_custom_call" | custom-call | tf_op jit(solution)/shard_map/states/pallas_call | solution.py:309
  85.3 10.2 %all-to-all-start = ((bf16[32,8,640]{2,1,0:T(8,128)(2,1)}), bf16[32,8,640]{2,1,0:T(8,128)(2,1)S(1)}, u32[]{:S(2)}, u32[]{:S(2)}) async-start(bf16[32,8,640]{2,1,0:T(8,128)(2,1)} %bitcast.22), calls=%async_computation | async-start | bytes 655360 | tf_op jit(solution)/shard_map/all_to_all | solution.py:535
  95.6 5.2 %inside.1.y_in = f32[1024,512]{1,0:T(8,128)} custom-call(bf16[1024,512]{1,0:T(8,128)(2,1)} %get-tuple-element.68.xs, bf16[1024,256]{1,0:T(8,128)(2,1)} %get-tuple-element.69.bcs, f32[8,1024]{1,0:T(8,128)} %get-tuple-element.70.dts, f32[16,1024]{1,0:T(8,128)} %get-tuple-element.71.sums, f32[8,1024]{1,0:T(8,128)S(1)} %stack.56.refs_18_.segs), custom_call_target="tpu_custom_call" | custom-call | flops 335544320 | bytes 3145728 | tf_op jit(solution)/shard_map/inside/pallas_call | solution.py:389
  100.8 8.3 %all-to-all-done.src = bf16[32,8,640]{2,1,0:T(8,128)(2,1)S(1)} async-done(((bf16[32,8,640]{2,1,0:T(8,128)(2,1)}), bf16[32,8,640]{2,1,0:T(8,128)(2,1)S(1)}, u32[]{:S(2)}, u32[]{:S(2)}) %all-to-all-start) | async-done | bytes 327712 | tf_op jit(solution)/shard_map/all_to_all | solution.py:535
  109.9 4.1 %all-to-all-start.1 = ((bf16[32,8,512]{2,1,0:T(8,128)(2,1)}), bf16[32,8,512]{2,1,0:T(8,128)(2,1)S(1)}, u32[]{:S(2)}, u32[]{:S(2)}) async-start(bf16[32,8,512]{2,1,0:T(8,128)(2,1)} %scan.1), calls=%async_computation.1 | async-start | bytes 524288 | tf_op jit(solution)/shard_map/all_to_all | solution.py:540
  114.0 8.9 %gate.1.sg = f32[1024,512]{1,0:T(8,128)} custom-call(s32[8]{0:T(128)S(1)} %stack.52.idx, bf16[512,512]{1,0:T(8,128)(2,1)} %copy-done.4, bf16[512,512]{1,0:T(8,128)(2,1)} %copy-done.7, bf16[512,512]{1,0:T(8,128)(2,1)} %copy-done.8, bf16[512,512]{1,0:T(8,128)(2,1)} %collective-permute-done.4.refs_3_, bf16[256,512]{1,0:T(8,128)(2,1)} %collective-permute-done.14.refs_0_.refs_4_, ...), custom_call_target="tpu_custom_call" | custom-call | flops 4294967296 | bytes 12582912 | tf_op jit(solution)/shard_map/gate/pallas_call | solution.py:167
  122.9 3.3 %all-to-all-done.1 = bf16[32,8,512]{2,1,0:T(8,128)(2,1)S(1)} async-done(((bf16[32,8,512]{2,1,0:T(8,128)(2,1)}), bf16[32,8,512]{2,1,0:T(8,128)(2,1)S(1)}, u32[]{:S(2)}, u32[]{:S(2)}) %all-to-all-start.1) | async-done | bytes 262176 | tf_op jit(solution)/shard_map/all_to_all | solution.py:540
  126.2 4.6 %finish.1 = (f32[1024,512]{1,0:T(8,128)S(1)}, f32[4,1,256]{2,1,0:T(1,128)S(1)}) custom-call(bf16[256,512]{1,0:T(8,128)(2,1)S(1)} %bitcast.20, bf16[2,4,128,512]{3,2,1,0:T(8,128)(2,1)} %get-tuple-element.73.loc, f32[2,4,512]{2,1,0:T(4,128)} %get-tuple-element.74.dec, f32[1024,512]{1,0:T(8,128)} %inside.1.y_in, f32[1024,512]{1,0:T(8,128)} %gate.1.sg, ...), custom_call_target="tpu_custom_call" | custom-call | tf_op jit(solution)/shard_map/finish/pallas_call | solution.py:424
  130.8 2.4 %collective-permute-start.20 = (f32[4,1,256]{2,1,0:T(1,128)S(1)}, f32[4,1,256]{2,1,0:T(1,128)S(1)}, u32[]{:S(2)}, u32[]{:S(2)}) collective-permute-start(f32[4,1,256]{2,1,0:T(1,128)S(1)} %get-tuple-element.78), channel_id=1, source_target_pairs={{0,4},{1,5},{2,6},{3,7},{4,0},{5,1},{6,2},{7,3},{8,12},{9,13},{10,... | collective-permute-start | bytes 12296 | tf_op jit(solution)/shard_map/ppermute | solution.py:484
  133.2 2.8 %collective-permute-done.20 = f32[4,1,256]{2,1,0:T(1,128)S(1)} collective-permute-done((f32[4,1,256]{2,1,0:T(1,128)S(1)}, f32[4,1,256]{2,1,0:T(1,128)S(1)}, u32[]{:S(2)}, u32[]{:S(2)}) %collective-permute-start.20) | collective-permute-done | bytes 4128 | tf_op jit(solution)/shard_map/ppermute | solution.py:484
  136.0 2.1 %collective-permute-start.22 = (f32[4,1,256]{2,1,0:T(1,128)S(1)}, f32[4,1,256]{2,1,0:T(1,128)S(1)}, u32[]{:S(2)}, u32[]{:S(2)}) collective-permute-start(f32[4,1,256]{2,1,0:T(1,128)S(1)} %add.90.refs_0_), channel_id=1, source_target_pairs={{0,2},{1,3},{2,0},{3,1},{4,6},{5,7},{6,4},{7,5},{8,10},{9,11},{10,... | collective-permute-start | bytes 12296 | tf_op jit(solution)/shard_map/ppermute | solution.py:484
  139.2 1.6 %collective-permute-done.21.refs_1_ = f32[4,1,256]{2,1,0:T(1,128)S(1)} collective-permute-done((f32[4,1,256]{2,1,0:T(1,128)S(1)}, f32[4,1,256]{2,1,0:T(1,128)S(1)}, u32[]{:S(2)}, u32[]{:S(2)}) %collective-permute-start.21) | collective-permute-done | bytes 4128 | tf_op jit(solution)/shard_map/ppermute | solution.py:484
  (89 shorter events, 13.7 us)
Async XLA Ops:
  1.3 54.2 %copy-start.4 = (bf16[512,512]{1,0:T(8,128)(2,1)}, bf16[512,512]{1,0:T(8,128)(2,1)S(1)}, u32[]{:S(2)}) copy-start(bf16[512,512]{1,0:T(8,128)(2,1)S(1)} %get-tuple-element.52.refs_0_) | copy-start | bytes 1572868
  1.3 47.0 %copy-start.15 = (f32[4]{0:T(128)S(1)}, f32[4]{0:T(128)}, u32[]{:S(2)}) copy-start(f32[4]{0:T(128)} %param.17) | copy-start | bytes 52
  1.3 47.0 %copy-start.16 = (f32[4]{0:T(128)S(1)}, f32[4]{0:T(128)}, u32[]{:S(2)}) copy-start(f32[4]{0:T(128)} %param.18) | copy-start | bytes 52
  1.3 47.0 %copy-start.13 = (bf16[4096,4]{0,1:T(4,128)(2,1)S(1)}, bf16[4096,4]{0,1:T(4,128)(2,1)}, u32[]{:S(2)}) copy-start(bf16[4096,4]{0,1:T(4,128)(2,1)} %param.16) | copy-start | bytes 98308
  1.3 16.6 %collective-permute-start.2 = (bf16[512,512]{1,0:T(8,128)(2,1)S(1)}, bf16[512,512]{1,0:T(8,128)(2,1)S(1)}, u32[]{:S(2)}, u32[]{:S(2)}) collective-permute-start(bf16[512,512]{1,0:T(8,128)(2,1)S(1)} %get-tuple-element.52.refs_0_), channel_id=1, source_target_pairs={{0,1},{1,2},{2,3},{3,0},{4,5},{5,6},{6,7},{7,4},{8,9},{9,10},{10,1... | collective-permute-start | bytes 1572872 | tf_op jit(solution)/shard_map/ppermute | solution.py:484
  2.9 15.0 %collective-permute-start.3 = (bf16[512,512]{1,0:T(8,128)(2,1)S(1)}, bf16[512,512]{1,0:T(8,128)(2,1)S(1)}, u32[]{:S(2)}, u32[]{:S(2)}) collective-permute-start(bf16[512,512]{1,0:T(8,128)(2,1)S(1)} %get-tuple-element.52.refs_0_), channel_id=1, source_target_pairs={{0,3},{1,0},{2,1},{3,2},{4,7},{5,4},{6,5},{7,6},{8,11},{9,8},{10,9... | collective-permute-start | bytes 1572872 | tf_op jit(solution)/shard_map/ppermute | solution.py:484
  4.6 14.7 %collective-permute-start.4 = (bf16[512,512]{1,0:T(8,128)(2,1)S(1)}, bf16[512,512]{1,0:T(8,128)(2,1)}, u32[]{:S(2)}, u32[]{:S(2)}) collective-permute-start(bf16[512,512]{1,0:T(8,128)(2,1)S(1)} %get-tuple-element.52.refs_0_), channel_id=1, source_target_pairs={{0,4},{1,5},{2,6},{3,7},{4,0},{5,1},{6,2},{7,3},{8,12},{9,13},{10,... | collective-permute-start | bytes 1572872 | tf_op jit(solution)/shard_map/ppermute | solution.py:484
  7.8 10.0 %collective-permute-start = (bf16[8,640]{1,0:T(8,128)(2,1)S(1)}, bf16[8,640]{1,0:T(8,128)(2,1)S(1)}, u32[]{:S(2)}, u32[]{:S(2)}) collective-permute-start(bf16[8,640]{1,0:T(8,128)(2,1)S(1)} %pad_maximum_fusion.1), channel_id=1, source_target_pairs={{0,8},{8,16},{16,24},{24,32},{32,40},{40,48},{48,56},{56,64},{64,7... | collective-permute-start | bytes 30728 | tf_op jit(solution)/shard_map/ppermute | solution.py:504
  9.8 8.0 %collective-permute-start.1 = (bf16[8,640]{1,0:T(8,128)(2,1)S(1)}, bf16[8,640]{1,0:T(8,128)(2,1)S(1)}, u32[]{:S(2)}, u32[]{:S(2)}) collective-permute-start(bf16[8,640]{1,0:T(8,128)(2,1)S(1)} %pad_maximum_fusion.2), channel_id=1, source_target_pairs={{8,0},{16,8},{24,16},{32,24},{40,32},{48,40},{56,48},{64,56},{72,6... | collective-permute-start | bytes 30728 | tf_op jit(solution)/shard_map/ppermute | solution.py:505
  17.9 42.4 %copy-start.3 = (bf16[528,512]{1,0:T(8,128)(2,1)}, bf16[528,512]{1,0:T(8,128)(2,1)S(1)}, u32[]{:S(2)}) copy-start(bf16[528,512]{1,0:T(8,128)(2,1)S(1)} %pad_maximum_fusion.refs_0_.refs_10_) | copy-start | bytes 1622020
  17.9 37.6 %copy-start.7 = (bf16[512,512]{1,0:T(8,128)(2,1)}, bf16[512,512]{1,0:T(8,128)(2,1)S(1)}, u32[]{:S(2)}) copy-start(bf16[512,512]{1,0:T(8,128)(2,1)S(1)} %collective-permute-done.2.refs_1_) | copy-start | bytes 1572868
  19.4 15.2 %collective-permute-start.7 = (bf16[528,512]{1,0:T(8,128)(2,1)S(1)}, bf16[528,512]{1,0:T(8,128)(2,1)S(1)}, u32[]{:S(2)}, u32[]{:S(2)}) collective-permute-start(bf16[528,512]{1,0:T(8,128)(2,1)S(1)} %pad_maximum_fusion.refs_0_.refs_10_), channel_id=1, source_target_pairs={{0,3},{1,0},{2,1},{3,2},{4,7},{5,4},{6,5},{7,6},{8,11},{9,8},{10,9... | collective-permute-start | bytes 1622024 | tf_op jit(solution)/shard_map/ppermute | solution.py:484
  20.9 17.2 %collective-permute-start.5 = (bf16[528,512]{1,0:T(8,128)(2,1)S(1)}, bf16[528,512]{1,0:T(8,128)(2,1)S(1)}, u32[]{:S(2)}, u32[]{:S(2)}) collective-permute-start(bf16[528,512]{1,0:T(8,128)(2,1)S(1)} %pad_maximum_fusion.refs_0_.refs_10_), channel_id=1, source_target_pairs={{0,1},{1,2},{2,3},{3,0},{4,5},{5,6},{6,7},{7,4},{8,9},{9,10},{10,1... | collective-permute-start | bytes 1622024 | tf_op jit(solution)/shard_map/ppermute | solution.py:484
  21.4 23.6 %collective-permute-start.9 = (bf16[528,512]{1,0:T(8,128)(2,1)S(1)}, bf16[528,512]{1,0:T(8,128)(2,1)S(1)}, u32[]{:S(2)}, u32[]{:S(2)}) collective-permute-start(bf16[528,512]{1,0:T(8,128)(2,1)S(1)} %pad_maximum_fusion.refs_0_.refs_10_), channel_id=1, source_target_pairs={{0,4},{1,5},{2,6},{3,7},{4,0},{5,1},{6,2},{7,3},{8,12},{9,13},{10,... | collective-permute-start | bytes 1622024 | tf_op jit(solution)/shard_map/ppermute | solution.py:484
  23.7 18.9 %collective-permute-start.14 = (bf16[256,512]{1,0:T(8,128)(2,1)S(1)}, bf16[256,512]{1,0:T(8,128)(2,1)}, u32[]{:S(2)}, u32[]{:S(2)}) collective-permute-start(bf16[256,512]{1,0:T(8,128)(2,1)S(1)} %slice.62), channel_id=1, source_target_pairs={{0,1},{1,2},{2,3},{3,0},{4,5},{5,6},{6,7},{7,4},{8,9},{9,10},{10,1... | collective-permute-start | bytes 786440 | tf_op jit(solution)/shard_map/ppermute | solution.py:484
  24.1 18.5 %collective-permute-start.15 = (bf16[256,512]{1,0:T(8,128)(2,1)S(1)}, bf16[256,512]{1,0:T(8,128)(2,1)S(1)}, u32[]{:S(2)}, u32[]{:S(2)}) collective-permute-start(bf16[256,512]{1,0:T(8,128)(2,1)S(1)} %slice.63), channel_id=1, source_target_pairs={{0,3},{1,0},{2,1},{3,2},{4,7},{5,4},{6,5},{7,6},{8,11},{9,8},{10,9... | collective-permute-start | bytes 786440 | tf_op jit(solution)/shard_map/ppermute | solution.py:484
  35.3 16.7 %collective-permute-start.8 = (bf16[272,512]{1,0:T(8,128)(2,1)}, bf16[272,512]{1,0:T(8,128)(2,1)}, u32[]{:S(2)}, u32[]{:S(2)}) collective-permute-start(bf16[272,512]{1,0:T(8,128)(2,1)} %slice.71), channel_id=1, source_target_pairs={{0,3},{1,0},{2,1},{3,2},{4,7},{5,4},{6,5},{7,6},{8,11},{9,8},{10,9... | collective-permute-start | bytes 835592 | tf_op jit(solution)/shard_map/ppermute | solution.py:484
  38.9 11.9 %collective-permute-start.6 = (bf16[256,512]{1,0:T(8,128)(2,1)}, bf16[256,512]{1,0:T(8,128)(2,1)}, u32[]{:S(2)}, u32[]{:S(2)}) collective-permute-start(bf16[256,512]{1,0:T(8,128)(2,1)} %slice.70), channel_id=1, source_target_pairs={{0,1},{1,2},{2,3},{3,0},{4,5},{5,6},{6,7},{7,4},{8,9},{9,10},{10,1... | collective-permute-start | bytes 786440 | tf_op jit(solution)/shard_map/ppermute | solution.py:484
  42.6 9.4 %collective-permute-start.18 = (bf16[256,512]{1,0:T(8,128)(2,1)}, bf16[256,512]{1,0:T(8,128)(2,1)}, u32[]{:S(2)}, u32[]{:S(2)}) collective-permute-start(bf16[256,512]{1,0:T(8,128)(2,1)} %collective-permute-done.14.refs_0_.refs_4_), channel_id=1, source_target_pairs={{0,4},{1,5},{2,6},{3,7},{4,0},{5,1},{6,2},{7,3},{8,12},{9,13},{10,... | collective-permute-start | bytes 786440 | tf_op jit(solution)/shard_map/ppermute | solution.py:484
  44.9 17.8 %collective-permute-start.16 = (bf16[512,512]{1,0:T(8,128)(2,1)}, bf16[512,512]{1,0:T(8,128)(2,1)}, u32[]{:S(2)}, u32[]{:S(2)}) collective-permute-start(bf16[512,512]{1,0:T(8,128)(2,1)} %collective-permute-done.4.refs_3_), channel_id=1, source_target_pairs={{0,1},{1,2},{2,3},{3,0},{4,5},{5,6},{6,7},{7,4},{8,9},{9,10},{10,1... | collective-permute-start | bytes 1572872 | tf_op jit(solution)/shard_map/ppermute | solution.py:484
  45.0 19.0 %collective-permute-start.17 = (bf16[512,512]{1,0:T(8,128)(2,1)}, bf16[512,512]{1,0:T(8,128)(2,1)}, u32[]{:S(2)}, u32[]{:S(2)}) collective-permute-start(bf16[512,512]{1,0:T(8,128)(2,1)} %collective-permute-done.4.refs_3_), channel_id=1, source_target_pairs={{0,3},{1,0},{2,1},{3,2},{4,7},{5,4},{6,5},{7,6},{8,11},{9,8},{10,9... | collective-permute-start | bytes 1572872 | tf_op jit(solution)/shard_map/ppermute | solution.py:484
  50.7 9.5 %collective-permute-start.19 = (bf16[256,512]{1,0:T(8,128)(2,1)}, bf16[256,512]{1,0:T(8,128)(2,1)}, u32[]{:S(2)}, u32[]{:S(2)}) collective-permute-start(bf16[256,512]{1,0:T(8,128)(2,1)} %copy-done.11), channel_id=1, source_target_pairs={{0,4},{1,5},{2,6},{3,7},{4,0},{5,1},{6,2},{7,3},{8,12},{9,13},{10,... | collective-permute-start | bytes 786440 | tf_op jit(solution)/shard_map/ppermute | solution.py:484
  52.0 21.6 %collective-permute-start.10 = (bf16[528,512]{1,0:T(8,128)(2,1)S(1)}, bf16[528,512]{1,0:T(8,128)(2,1)}, u32[]{:S(2)}, u32[]{:S(2)}) collective-permute-start(bf16[528,512]{1,0:T(8,128)(2,1)S(1)} %collective-permute-done.9.refs_3_.refs_13_), channel_id=1, source_target_pairs={{0,1},{1,2},{2,3},{3,0},{4,5},{5,6},{6,7},{7,4},{8,9},{9,10},{10,1... | collective-permute-start | bytes 1622024 | tf_op jit(solution)/shard_map/ppermute | solution.py:484
  52.0 21.6 %collective-permute-start.11 = (bf16[528,512]{1,0:T(8,128)(2,1)S(1)}, bf16[528,512]{1,0:T(8,128)(2,1)}, u32[]{:S(2)}, u32[]{:S(2)}) collective-permute-start(bf16[528,512]{1,0:T(8,128)(2,1)S(1)} %collective-permute-done.9.refs_3_.refs_13_), channel_id=1, source_target_pairs={{0,3},{1,0},{2,1},{3,2},{4,7},{5,4},{6,5},{7,6},{8,11},{9,8},{10,9... | collective-permute-start | bytes 1622024 | tf_op jit(solution)/shard_map/ppermute | solution.py:484
  60.3 13.4 %collective-permute-start.13 = (bf16[272,512]{1,0:T(8,128)(2,1)}, bf16[272,512]{1,0:T(8,128)(2,1)S(1)}, u32[]{:S(2)}, u32[]{:S(2)}) collective-permute-start(bf16[272,512]{1,0:T(8,128)(2,1)} %collective-permute-done.8.refs_1_.refs_15_), channel_id=1, source_target_pairs={{0,4},{1,5},{2,6},{3,7},{4,0},{5,1},{6,2},{7,3},{8,12},{9,13},{10,... | collective-permute-start | bytes 835592 | tf_op jit(solution)/shard_map/ppermute | solution.py:484
  62.7 10.9 %collective-permute-start.12 = (bf16[256,512]{1,0:T(8,128)(2,1)}, bf16[256,512]{1,0:T(8,128)(2,1)S(1)}, u32[]{:S(2)}, u32[]{:S(2)}) collective-permute-start(bf16[256,512]{1,0:T(8,128)(2,1)} %collective-permute-done.6.refs_0_.refs_14_), channel_id=1, source_target_pairs={{0,4},{1,5},{2,6},{3,7},{4,0},{5,1},{6,2},{7,3},{8,12},{9,13},{10,... | collective-permute-start | bytes 786440 | tf_op jit(solution)/shard_map/ppermute | solution.py:484
  85.3 23.7 %all-to-all-start = ((bf16[32,8,640]{2,1,0:T(8,128)(2,1)}), bf16[32,8,640]{2,1,0:T(8,128)(2,1)S(1)}, u32[]{:S(2)}, u32[]{:S(2)}) async-start(bf16[32,8,640]{2,1,0:T(8,128)(2,1)} %bitcast.22), calls=%async_computation | async-start | bytes 655360 | tf_op jit(solution)/shard_map/all_to_all | solution.py:535
  109.9 16.3 %all-to-all-start.1 = ((bf16[32,8,512]{2,1,0:T(8,128)(2,1)}), bf16[32,8,512]{2,1,0:T(8,128)(2,1)S(1)}, u32[]{:S(2)}, u32[]{:S(2)}) async-start(bf16[32,8,512]{2,1,0:T(8,128)(2,1)} %scan.1), calls=%async_computation.1 | async-start | bytes 524288 | tf_op jit(solution)/shard_map/all_to_all | solution.py:540
  130.8 5.2 %collective-permute-start.20 = (f32[4,1,256]{2,1,0:T(1,128)S(1)}, f32[4,1,256]{2,1,0:T(1,128)S(1)}, u32[]{:S(2)}, u32[]{:S(2)}) collective-permute-start(f32[4,1,256]{2,1,0:T(1,128)S(1)} %get-tuple-element.78), channel_id=1, source_target_pairs={{0,4},{1,5},{2,6},{3,7},{4,0},{5,1},{6,2},{7,3},{8,12},{9,13},{10,... | collective-permute-start | bytes 12296 | tf_op jit(solution)/shard_map/ppermute | solution.py:484
  136.0 4.8 %collective-permute-start.21 = (f32[4,1,256]{2,1,0:T(1,128)S(1)}, f32[4,1,256]{2,1,0:T(1,128)S(1)}, u32[]{:S(2)}, u32[]{:S(2)}) collective-permute-start(f32[4,1,256]{2,1,0:T(1,128)S(1)} %add.90.refs_0_), channel_id=1, source_target_pairs={{0,1},{1,2},{2,3},{3,0},{4,5},{5,6},{6,7},{7,4},{8,9},{9,10},{10,1... | collective-permute-start | bytes 12296 | tf_op jit(solution)/shard_map/ppermute | solution.py:484
  136.0 5.2 %collective-permute-start.22 = (f32[4,1,256]{2,1,0:T(1,128)S(1)}, f32[4,1,256]{2,1,0:T(1,128)S(1)}, u32[]{:S(2)}, u32[]{:S(2)}) collective-permute-start(f32[4,1,256]{2,1,0:T(1,128)S(1)} %add.90.refs_0_), channel_id=1, source_target_pairs={{0,2},{1,3},{2,0},{3,1},{4,6},{5,7},{6,4},{7,5},{8,10},{9,11},{10,... | collective-permute-start | bytes 12296 | tf_op jit(solution)/shard_map/ppermute | solution.py:484
  138.1 3.7 %collective-permute-start.23 = (f32[4,1,256]{2,1,0:T(1,128)S(1)}, f32[4,1,256]{2,1,0:T(1,128)S(1)}, u32[]{:S(2)}, u32[]{:S(2)}) collective-permute-start(f32[4,1,256]{2,1,0:T(1,128)S(1)} %add.90.refs_0_), channel_id=1, source_target_pairs={{0,3},{1,0},{2,1},{3,2},{4,7},{5,4},{6,5},{7,6},{8,11},{9,8},{10,9... | collective-permute-start | bytes 12296 | tf_op jit(solution)/shard_map/ppermute | solution.py:484
  (11 other events, 140.7 us)
